TPU v7x, 256 devices: a whole 4x4x8 slice. The times are simulated.
256 devices in a mesh: det: 2 (over core), grp: 4 (over x), filt: 32 (over y, z).
Axes of the slice: x: 4, y: 4, z: 8, core: 2. Of those that a mesh axis runs over, the one named last changes fastest.
Arguments:
- strain: float32 [2, 131072], P('det'), may hold values from -6 to 6
- inv_asd: float32 [2, 65536], P('det'), may hold values from 0.25 to 4
- templates: bfloat16 [1536, 4096], P(('grp', 'filt')), may hold values from -6 to 6
- chirp_blocks: int32 [1536], P(('grp', 'filt')), may hold values from 1 to 32, as said below
- owner: int32 [1536], P(('grp', 'filt')), may hold values from 0 to 31, as said below
- slide: int32 [4], P('grp'), may hold values from 0 to 1023
Outputs:
- peaks: float32 [1536, 1024], P(('grp', 'filt'), 'det')
- loudest: float32 [1024], P('det')
Inputs may be any that keep to these rules, and one draw needn't show every extreme that they name: `chirp_blocks`: every device holds a template of 32 blocks. Each device sends either 1 or none of its templates to each owner of its group, and each owner receives exactly 12 templates.
All inputs are finite; a program needn't handle non-finite values.
Results may differ from a plain program's by a relative error of at most 0.0052.
Values may be sent and summed in bfloat16 or wider, within the bound.
A program may use at most 64 MiB of HBM per device.

v0:
```python
import jax
import jax.numpy as jnp
from jax import lax
from jax.sharding import PartitionSpec as P

N1 = 256
N2 = 512
NFFT = 131072
BLK = 128
TL = 4096


TWO_PI = 6.283185307179586


def partner_2(value, axis, stride):
    mask = 2**stride
    pairs = [(source, source ^ mask) for source in range(lax.axis_size(axis))]
    return lax.ppermute(value, axis, pairs)


def angle_table(rows, cols, period):
    left = jnp.arange(rows, dtype=jnp.int32)[:, None]
    right = jnp.arange(cols, dtype=jnp.int32)[None, :]
    return TWO_PI / period * (left * right % period).astype(jnp.float32)


def make_tables():
    first = angle_table(N1, N1, N1)
    twist = angle_table(N1, N2, NFFT)
    second = angle_table(N2, N2 // 2, N2)
    back = angle_table(N2 // 2, N2, N2)
    return (
        jnp.cos(first).astype(jnp.bfloat16),
        jnp.sin(first).astype(jnp.bfloat16),
        jnp.cos(twist),
        jnp.sin(twist),
        jnp.cos(second).astype(jnp.bfloat16),
        jnp.sin(second).astype(jnp.bfloat16),
        jnp.cos(back).astype(jnp.bfloat16),
        jnp.sin(back).astype(jnp.bfloat16),
    )


def forward(signal, cos_rows, sin_rows, tables):
    cos_first, sin_first, cos_twist, sin_twist, cos_second, sin_second, cos_back, sin_back = tables
    real_a = jnp.dot(cos_rows, signal, preferred_element_type=jnp.float32)
    imag_a = -jnp.dot(sin_rows, signal, preferred_element_type=jnp.float32)
    real_b = (real_a * cos_twist + imag_a * sin_twist).astype(jnp.bfloat16)
    imag_b = (imag_a * cos_twist - real_a * sin_twist).astype(jnp.bfloat16)
    real_x = jnp.dot(real_b, cos_second, preferred_element_type=jnp.float32) + jnp.dot(
        imag_b, sin_second, preferred_element_type=jnp.float32
    )
    imag_x = jnp.dot(imag_b, cos_second, preferred_element_type=jnp.float32) - jnp.dot(
        real_b, sin_second, preferred_element_type=jnp.float32
    )
    return (real_x, imag_x)


def correlate(windowed, spectrum, weight2d, tables):
    cos_first, sin_first, cos_twist, sin_twist, cos_second, sin_second, cos_back, sin_back = tables
    rows_used = windowed.shape[0]
    temp_real, temp_imag = forward(
        windowed, cos_first[:, :rows_used], sin_first[:, :rows_used], tables
    )
    sigma = jnp.sum(weight2d * weight2d * (temp_real * temp_real + temp_imag * temp_imag))
    data_real, data_imag = spectrum
    q_real = (temp_real * data_real + temp_imag * data_imag).astype(jnp.bfloat16)
    q_imag = (temp_real * data_imag - temp_imag * data_real).astype(jnp.bfloat16)
    d_real = jnp.dot(q_real, cos_back, preferred_element_type=jnp.float32) - jnp.dot(
        q_imag, sin_back, preferred_element_type=jnp.float32
    )
    d_imag = jnp.dot(q_real, sin_back, preferred_element_type=jnp.float32) + jnp.dot(
        q_imag, cos_back, preferred_element_type=jnp.float32
    )
    e_real = (d_real * cos_twist - d_imag * sin_twist).astype(jnp.bfloat16)
    e_imag = (d_real * sin_twist + d_imag * cos_twist).astype(jnp.bfloat16)
    z_real = jnp.dot(cos_first, e_real, preferred_element_type=jnp.float32) - jnp.dot(
        sin_first, e_imag, preferred_element_type=jnp.float32
    )
    z_imag = jnp.dot(sin_first, e_real, preferred_element_type=jnp.float32) + jnp.dot(
        cos_first, e_imag, preferred_element_type=jnp.float32
    )
    return ((z_real * z_real + z_imag * z_imag) / (NFFT * sigma)).reshape(NFFT)


def data_spectrum(strain_row, weight_row, tables):
    weight2d = weight_row.reshape(N2 // 2, N1).T
    signal = strain_row.astype(jnp.bfloat16).reshape(N1, N2)
    real_s, imag_s = forward(signal, tables[0], tables[1], tables)
    return ((weight2d * real_s, weight2d * imag_s), weight2d)


def compact(rows, blocks, valid, count):
    slot_rank = jnp.cumsum(valid.astype(jnp.int32)) - 1
    wanted = jnp.arange(count, dtype=jnp.int32)[:, None]
    picker = jnp.logical_and(valid[None, :], slot_rank[None, :] == wanted)
    picked = jnp.dot(picker.astype(jnp.bfloat16), rows, preferred_element_type=jnp.float32).astype(
        jnp.bfloat16
    )
    picked_blocks = jnp.sum(jnp.where(picker, blocks[None, :], 0), axis=1).astype(jnp.int32)
    return (picked, picked_blocks)


def shards(strain, inv_asd, templates, chirp_blocks, owner, slide):
    tables = make_tables()
    detector = lax.axis_index("det")
    per_dev = templates.shape[0]
    half_len = NFFT // 2
    filt_count = lax.axis_size("filt")
    capacity = (per_dev + filt_count - 1) // filt_count
    positions = jnp.arange(per_dev, dtype=jnp.int32)
    same_owner = owner[:, None] == owner[None, :]
    earlier = positions[None, :] < positions[:, None]
    owner_rank = jnp.sum(jnp.logical_and(same_owner, earlier).astype(jnp.int32), axis=1)
    dest_slot = owner * capacity + owner_rank
    slot_ids = jnp.arange(filt_count * capacity, dtype=jnp.int32)[:, None]
    placing = slot_ids == dest_slot[None, :]
    send_rows = jnp.dot(
        placing.astype(jnp.bfloat16), templates, preferred_element_type=jnp.float32
    ).astype(jnp.bfloat16)
    send_blocks = jnp.sum(jnp.where(placing, chirp_blocks[None, :], 0), axis=1)
    recv_rows, recv_blocks = (
        lax.all_to_all(send_rows, "filt", split_axis=0, concat_axis=0, tiled=True),
        lax.all_to_all(send_blocks, "filt", split_axis=0, concat_axis=0, tiled=True),
    )
    local_rows, local_blocks = compact(recv_rows, recv_blocks, recv_blocks > 0, per_dev)
    samples = jnp.arange(TL, dtype=jnp.int32)
    windowed = jnp.where(
        samples[None, :] < BLK * local_blocks[:, None], local_rows, jnp.zeros_like(local_rows)
    )
    windowed = windowed.reshape(per_dev, TL // N2, N2)
    own_spec, own_weight = data_spectrum(strain[0], inv_asd[0], tables)
    slide_shift = jnp.where(detector == 1, BLK * slide[0], 0)

    def filter_template(kept_row):
        snr_sq = jnp.roll(correlate(kept_row, own_spec, own_weight, tables), -slide_shift)
        partner = partner_2(snr_sq, "det", 0)
        network = lax.dynamic_slice_in_dim(snr_sq + partner, detector * half_len, half_len)
        return jnp.max(network.reshape(half_len // BLK, BLK), axis=1)

    peaks = lax.map(filter_template, windowed)
    loudest = lax.pmax(jnp.max(peaks, axis=0), ("grp", "filt"))
    return (peaks, loudest)


def solution(mesh):
    return jax.shard_map(
        shards,
        mesh=mesh,
        in_specs=(
            P("det", None),
            P("det", None),
            P(("grp", "filt"), None),
            P(("grp", "filt")),
            P(("grp", "filt")),
            P("grp"),
        ),
        out_specs=(P(("grp", "filt"), "det"), P("det")),
        check_vma=False,
    )
```

profile of v0, /device:TPU:32, one launch (start us, length us, event | category | flops | bytes accessed | tf_op | source)
XLA Modules:
  0.0 761.0 jit_solution(15973358883322284147)
XLA Ops:
  3.1 11.4 %all-to-all-start = ((s32[32,1,1]{2,1,0:T(1,128)}), s32[32,1,1]{2,1,0:T(1,128)S(1)}, u32[]{:S(2)}, u32[]{:S(2)}) async-start(s32[32,1,1]{2,1,0:T(1,128)} %copy.43), calls=%async_computation | async-start | bytes 32768 | tf_op jit(solution)/shard_map/all_to_all | solution.py:125
  19.2 3.4 subtract_convert_fusion.3
  36.5 9.8 %all-to-all-start.1 = ((bf16[32,2,2048]{2,1,0:T(2,128)(2,1)}), bf16[32,2,2048]{2,1,0:T(2,128)(2,1)S(1)}, u32[]{:S(2)}, u32[]{:S(2)}) async-start(bf16[32,2,2048]{2,1,0:T(2,128)(2,1)} %reshape.99), calls=%async_computation.1 | async-start | bytes 524288 | tf_op jit(solution)/shard_map/all_to_all | solution.py:124
  47.3 10.7 %all-to-all-done.1 = bf16[32,2,2048]{2,1,0:T(2,128)(2,1)S(1)} async-done(((bf16[32,2,2048]{2,1,0:T(2,128)(2,1)}), bf16[32,2,2048]{2,1,0:T(2,128)(2,1)S(1)}, u32[]{:S(2)}, u32[]{:S(2)}) %all-to-all-start.1) | async-done | bytes 262176 | tf_op jit(solution)/shard_map/all_to_all | solution.py:124
  58.7 359.2 %while.14 = (s32[]{:T(128)}, f32[12,512]{1,0:T(8,128)S(1)}, bf16[12,8,512]{2,1,0:T(8,128)(2,1)S(1)}, bf16[256,256]{1,0:T(8,128)(2,1)S(1)}, bf16[256,256]{1,0:T(8...) while((s32[]{:T(128)}, f32[12,512]{1,0:T(8,128)S(1)}, ...), condition=%wide.region_7.8_spmd.clone.clone, body=%wide.region_4.7_spmd.clone.clone.sunk | while | flops 833420800 | bytes 20601044 | solution.py:142
  79.7 4.5 add_convert_fusion.7
  98.2 3.0 subtract_convert_fusion.5
  109.6 4.5 add_convert_fusion.7
  128.1 3.0 subtract_convert_fusion.5
  139.5 4.5 add_convert_fusion.7
  158.0 3.0 subtract_convert_fusion.5
  169.4 4.5 add_convert_fusion.7
  187.9 3.0 subtract_convert_fusion.5
  199.3 4.5 add_convert_fusion.7
  217.9 3.0 subtract_convert_fusion.5
  229.2 4.5 add_convert_fusion.7
  247.8 3.0 subtract_convert_fusion.5
  259.2 4.5 add_convert_fusion.7
  289.1 4.5 add_convert_fusion.7
  319.0 4.5 add_convert_fusion.7
  348.9 4.5 add_convert_fusion.7
  378.8 4.5 add_convert_fusion.7
  408.7 4.5 add_convert_fusion.7
  418.0 343.0 %pmax.7 = f32[512]{0:T(512)} all-reduce(f32[512]{0:T(512)S(1)} %reduce_max.20), channel_id=1, replica_groups=mesh['det'=2,'grp'=4,'filt'=32] {'grp','filt'}, use_global_device_ids=true, to_apply=%region_9.10 | all-reduce | flops 512 | bytes 4096 | tf_op jit(solution)/shard_map/pmax | solution.py:143
  (279 shorter events, 299.7 us)
Async XLA Ops:
  0.6 15.5 %copy-start = (bf16[12,4096]{1,0:T(8,128)(2,1)S(1)}, bf16[12,4096]{1,0:T(8,128)(2,1)}, u32[]{:S(2)}) copy-start(bf16[12,4096]{1,0:T(8,128)(2,1)} %param.10) | copy-start | bytes 294916
  0.6 1.0 copy-start.4
  0.7 15.8 %copy-start.1 = (f32[1,131072]{1,0:T(1,128)S(1)}, f32[1,131072]{1,0:T(1,128)}, u32[]{:S(2)}) copy-start(f32[1,131072]{1,0:T(1,128)} %param.8) | copy-start | bytes 1572868
  3.1 33.4 %all-to-all-start = ((s32[32,1,1]{2,1,0:T(1,128)}), s32[32,1,1]{2,1,0:T(1,128)S(1)}, u32[]{:S(2)}, u32[]{:S(2)}) async-start(s32[32,1,1]{2,1,0:T(1,128)} %copy.43), calls=%async_computation | async-start | bytes 32768 | tf_op jit(solution)/shard_map/all_to_all | solution.py:125
  22.6 2.7 copy-start.2
  36.5 21.5 %all-to-all-start.1 = ((bf16[32,2,2048]{2,1,0:T(2,128)(2,1)}), bf16[32,2,2048]{2,1,0:T(2,128)(2,1)S(1)}, u32[]{:S(2)}, u32[]{:S(2)}) async-start(bf16[32,2,2048]{2,1,0:T(2,128)(2,1)} %reshape.99), calls=%async_computation.1 | async-start | bytes 524288 | tf_op jit(solution)/shard_map/all_to_all | solution.py:124
  86.7 2.0 collective-permute-start
  116.6 2.0 collective-permute-start
  146.5 2.0 collective-permute-start
  176.4 2.0 collective-permute-start
  206.3 2.0 collective-permute-start
  236.2 2.0 collective-permute-start
  266.2 2.0 collective-permute-start
  296.1 2.0 collective-permute-start
  326.0 2.0 collective-permute-start
  355.9 2.0 collective-permute-start
  385.8 2.0 collective-permute-start
  415.7 2.0 collective-permute-start
  418.0 343.0 %copy-start.3 = (f32[12,512]{1,0:T(8,128)}, f32[12,512]{1,0:T(8,128)S(1)}, u32[]{:S(2)}) copy-start(f32[12,512]{1,0:T(8,128)S(1)} %get-tuple-element.244) | copy-start | bytes 73732
where the time goes:
time: 763 us; the launch traced here: 761 us
  blocking collectives  343 us (45%)
  matrix products  327 us (43%)
  waiting for transfers between devices  32.1 us (4%)
  starting transfers between devices  23.7 us (3%)
  other arithmetic  15.4 us (2%)
  loops' own time  9.65 us (1%)
  local copies, waits for them, and re-layouts  8.2 us (1%)
    pmax x1, blocking collectives, shards(): loudest = lax.pmax(jnp.max(peaks, axis=0), ('grp', 'filt'))  343 us
    dot_general x12, matrix products, correlate(): jnp.dot(q_imag, cos_back, preferred_element_type=jnp.float32)  53.5 us
    dot_general x13, matrix products, forward(): jnp.dot(real_b, sin_second, preferred_element_type=jnp.float32)  38.6 us
    dot_general x12, matrix products, correlate(): jnp.dot(q_imag, sin_back, preferred_element_type=jnp.float32)  33.6 us
    dot_general x12, matrix products, correlate(): jnp.dot(q_real, sin_back, preferred_element_type=jnp.float32)  33.3 us
    dot_general x12, matrix products, correlate(): jnp.dot(q_real, cos_back, preferred_element_type=jnp.float32)  32.9 us
    dot_general x13, matrix products, forward(): imag_a = -jnp.dot(sin_rows, signal, preferred_element_type=jnp.float32)  32.9 us
    dot_general x13, matrix products, forward(): jnp.dot(imag_b, sin_second, preferred_element_type=jnp.float32)  27.7 us
  transfers between devices with their start and end apart: 14, of which 13 were waited for; matrix products, arithmetic and copies ran while one was open for 3% of the time, Pallas kernels for 0%

commit v1 on v0

--- a/solution.py
+++ b/solution.py
@@ -102,11 +102,41 @@
     return (picked, picked_blocks)
 
 
+def template_transform(windowed, tables):
+    rows_used = windowed.shape[0]
+    return forward(windowed, tables[0][:, :rows_used], tables[1][:, :rows_used], tables)
+
+
+def correlate_with(temp_real, temp_imag, spectrum, weight2d, tables):
+    cos_first, sin_first, cos_twist, sin_twist, cos_second, sin_second, cos_back, sin_back = tables
+    sigma = jnp.sum(weight2d * weight2d * (temp_real * temp_real + temp_imag * temp_imag))
+    data_real, data_imag = spectrum
+    q_real = (temp_real * data_real + temp_imag * data_imag).astype(jnp.bfloat16)
+    q_imag = (temp_real * data_imag - temp_imag * data_real).astype(jnp.bfloat16)
+    d_real = jnp.dot(q_real, cos_back, preferred_element_type=jnp.float32) - jnp.dot(
+        q_imag, sin_back, preferred_element_type=jnp.float32
+    )
+    d_imag = jnp.dot(q_real, sin_back, preferred_element_type=jnp.float32) + jnp.dot(
+        q_imag, cos_back, preferred_element_type=jnp.float32
+    )
+    e_real = (d_real * cos_twist - d_imag * sin_twist).astype(jnp.bfloat16)
+    e_imag = (d_real * sin_twist + d_imag * cos_twist).astype(jnp.bfloat16)
+    z_real = jnp.dot(cos_first, e_real, preferred_element_type=jnp.float32) - jnp.dot(
+        sin_first, e_imag, preferred_element_type=jnp.float32
+    )
+    z_imag = jnp.dot(sin_first, e_real, preferred_element_type=jnp.float32) + jnp.dot(
+        cos_first, e_imag, preferred_element_type=jnp.float32
+    )
+    return (z_real * z_real + z_imag * z_imag) / (NFFT * sigma)
+
+
 def shards(strain, inv_asd, templates, chirp_blocks, owner, slide):
-    tables = make_tables()
+    tables = lax.optimization_barrier(make_tables())
     detector = lax.axis_index("det")
     per_dev = templates.shape[0]
-    half_len = NFFT // 2
+    mine = per_dev // 2
+    n_blk = NFFT // BLK
+    half_blk = n_blk // 2
     filt_count = lax.axis_size("filt")
     capacity = (per_dev + filt_count - 1) // filt_count
     positions = jnp.arange(per_dev, dtype=jnp.int32)
@@ -125,22 +155,37 @@
         lax.all_to_all(send_blocks, "filt", split_axis=0, concat_axis=0, tiled=True),
     )
     local_rows, local_blocks = compact(recv_rows, recv_blocks, recv_blocks > 0, per_dev)
+    my_rows = lax.dynamic_slice_in_dim(local_rows, detector * mine, mine)
+    my_blocks = lax.dynamic_slice_in_dim(local_blocks, detector * mine, mine)
     samples = jnp.arange(TL, dtype=jnp.int32)
     windowed = jnp.where(
-        samples[None, :] < BLK * local_blocks[:, None], local_rows, jnp.zeros_like(local_rows)
-    )
-    windowed = windowed.reshape(per_dev, TL // N2, N2)
-    own_spec, own_weight = data_spectrum(strain[0], inv_asd[0], tables)
-    slide_shift = jnp.where(detector == 1, BLK * slide[0], 0)
+        samples[None, :] < BLK * my_blocks[:, None], my_rows, jnp.zeros_like(my_rows)
+    )
+    windowed = windowed.reshape(mine, TL // N2, N2)
+    strain_both = lax.all_gather(strain[0].astype(jnp.bfloat16), "det")
+    asd_both = lax.all_gather(inv_asd[0], "det")
+    spec_0, weight_0 = data_spectrum(strain_both[0], asd_both[0], tables)
+    spec_1, weight_1 = data_spectrum(strain_both[1], asd_both[1], tables)
+    shift = slide[0]
 
     def filter_template(kept_row):
-        snr_sq = jnp.roll(correlate(kept_row, own_spec, own_weight, tables), -slide_shift)
-        partner = partner_2(snr_sq, "det", 0)
-        network = lax.dynamic_slice_in_dim(snr_sq + partner, detector * half_len, half_len)
-        return jnp.max(network.reshape(half_len // BLK, BLK), axis=1)
-
-    peaks = lax.map(filter_template, windowed)
-    loudest = lax.pmax(jnp.max(peaks, axis=0), ("grp", "filt"))
+        temp_real, temp_imag = template_transform(kept_row, tables)
+        first = correlate_with(temp_real, temp_imag, spec_0, weight_0, tables)
+        second = correlate_with(temp_real, temp_imag, spec_1, weight_1, tables)
+        second = jnp.roll(second.reshape(n_blk, BLK), -shift, axis=0)
+        network = first.reshape(n_blk, BLK) + second
+        return jnp.max(network, axis=1)
+
+    full = lax.map(filter_template, windowed)
+    keep = lax.dynamic_slice_in_dim(full, detector * half_blk, half_blk, axis=1)
+    give = lax.dynamic_slice_in_dim(full, (1 - detector) * half_blk, half_blk, axis=1)
+    got = lax.ppermute(give, "det", [(0, 1), (1, 0)])
+    peaks = jnp.where(
+        detector == 0, jnp.concatenate([keep, got], axis=0), jnp.concatenate([got, keep], axis=0)
+    )
+    local_max = jnp.max(peaks, axis=0)
+    gathered = lax.all_gather(local_max, ("grp", "filt"))
+    loudest = jnp.max(gathered, axis=0)
     return (peaks, loudest)
 
 

time: 763 us -> 618 us (0.81)
  matrix products: 327 us -> 127 us
  local copies, waits for them, and re-layouts: 8.2 us -> 74.1 us
  waiting for transfers between devices: 32.1 us -> 12.8 us
    all_gather x0 -> x3, blocking collectives: none -> 344 us  [the longest x1 339 us: shards(): gathered = lax.all_gather(local_max, ('grp', 'filt'))]
    pmax x1 -> x0, blocking collectives: 343 us -> none  [shards(): loudest = lax.pmax(jnp.max(peaks, axis=0), ('grp', 'filt'))]
    dot_general x96, matrix products: 166 us -> 84.9 us  [the longest x12 25.4 us: correlate_with(): jnp.dot(cos_first, e_imag, preferred_element_type=jnp.float32)]
    dot_general x13 -> x8, matrix products: 27.7 us -> 2.81 us  [forward(): jnp.dot(imag_b, sin_second, preferred_element_type=jnp.float32)]
    dot_general x13 -> x8, matrix products: 27.4 us -> 2.76 us  [forward(): jnp.dot(imag_b, cos_second, preferred_element_type=jnp.float32)]
    dot_general x13 -> x8, matrix products: 32.9 us -> 8.31 us  [forward(): imag_a = -jnp.dot(sin_rows, signal, preferred_element_type=jnp.float32)]
    dot_general x13 -> x8, matrix products: 27.4 us -> 2.99 us  [forward(): jnp.dot(real_b, cos_second, preferred_element_type=jnp.float32)]
    dot_general x13 -> x8, matrix products: 38.6 us -> 14.7 us  [forward(): jnp.dot(real_b, sin_second, preferred_element_type=jnp.float32)]
  transfers between devices with their start and end apart: 14 -> 3, of which waited for: 13 -> 2; matrix products, arithmetic and copies ran while one was open for 3% -> 5% of each run, Pallas kernels for 0% -> 0%
where the time goes in v1:
time: 618 us; the launch traced here: 612 us
  blocking collectives  344 us (56%)
  matrix products  127 us (21%)
  local copies, waits for them, and re-layouts  74.1 us (12%)
  other arithmetic  22.4 us (4%)
  starting transfers between devices  21.2 us (3%)
  waiting for transfers between devices  12.8 us (2%)
  loops' own time  8.64 us (1%)
    all_gather x1, blocking collectives, shards(): gathered = lax.all_gather(local_max, ('grp', 'filt'))  339 us
    dot_general x12, matrix products, correlate_with(): jnp.dot(cos_first, e_imag, preferred_element_type=jnp.float32)  25.4 us
    dot_general x12, matrix products, correlate_with(): jnp.dot(q_imag, cos_back, preferred_element_type=jnp.float32)  22.7 us
    div x12, local copies, waits for them, and re-layouts, correlate_with(): return (z_real * z_real + z_imag * z_imag) / (NFFT * sigma)  14.8 us
    dot_general x8, matrix products, forward(): jnp.dot(real_b, sin_second, preferred_element_type=jnp.float32)  14.7 us
    dot_general x12, matrix products, correlate_with(): jnp.dot(sin_first, e_imag, preferred_element_type=jnp.float32)  12.9 us
    dot_general x12, matrix products, correlate_with(): jnp.dot(q_imag, sin_back, preferred_element_type=jnp.float32)  12.4 us
  transfers between devices with their start and end apart: 3, of which 2 were waited for; matrix products, arithmetic and copies ran while one was open for 5% of the time, Pallas kernels for 0%

profile of v1, /device:TPU:32, one launch (start us, length us, event | category | flops | bytes accessed | tf_op | source)
XLA Modules:
  0.0 611.8 jit_solution(7049468659921841333)
XLA Ops:
  3.5 11.4 %all-to-all-start = ((s32[32,1,1]{2,1,0:T(1,128)}), s32[32,1,1]{2,1,0:T(1,128)S(1)}, u32[]{:S(2)}, u32[]{:S(2)}) async-start(s32[32,1,1]{2,1,0:T(1,128)} %copy.78), calls=%async_computation | async-start | bytes 32768 | tf_op jit(solution)/shard_map/all_to_all | solution.py:155
  17.0 2.2 sine_convert_fusion
  19.1 2.2 sine_convert_fusion.1
  23.5 2.6 all-gather.2
  26.0 3.8 slice_reduce_fusion
  34.8 2.3 all-gather.1
  40.5 2.5 subtract_convert_fusion.5
  55.1 9.8 %all-to-all-start.1 = ((bf16[32,2,2048]{2,1,0:T(2,128)(2,1)}), bf16[32,2,2048]{2,1,0:T(2,128)(2,1)}, u32[]{:S(2)}, u32[]{:S(2)}) async-start(bf16[32,2,2048]{2,1,0:T(2,128)(2,1)} %reshape.108), calls=%async_computation.1 | async-start | bytes 524288 | tf_op jit(solution)/shard_map/all_to_all | solution.py:154
  66.0 11.6 %all-to-all-done.1 = bf16[32,2,2048]{2,1,0:T(2,128)(2,1)} async-done(((bf16[32,2,2048]{2,1,0:T(2,128)(2,1)}), bf16[32,2,2048]{2,1,0:T(2,128)(2,1)}, u32[]{:S(2)}, u32[]{:S(2)}) %all-to-all-start.1) | async-done | bytes 262176 | tf_op jit(solution)/shard_map/all_to_all | solution.py:154
  77.6 2.2 reshape.109
  80.9 188.1 %while.12 = (s32[]{:T(128)}, f32[6,1024]{1,0:T(8,128)}, bf16[6,8,512]{2,1,0:T(8,128)(2,1)}, bf16[256,256]{1,0:T(8,128)(2,1)S(1)}, f32[256,512]{0,1:T(8,128)S(1)}...) while((s32[]{:T(128)}, f32[6,1024]{1,0:T(8,128)}, ...), condition=%wide.region_8.9_spmd, body=%wide.region_4.8_spmd.sunk | while | flops 1353776128 | bytes 49444356 | solution.py:179
  83.8 2.3 subtract_convert_fusion.8
  92.1 2.7 add_convert_fusion.10
  115.1 2.3 subtract_convert_fusion.8
  123.4 2.7 add_convert_fusion.10
  146.5 2.3 subtract_convert_fusion.8
  154.8 2.7 add_convert_fusion.10
  177.8 2.3 subtract_convert_fusion.8
  186.2 2.7 add_convert_fusion.10
  209.2 2.3 subtract_convert_fusion.8
  217.5 2.7 add_convert_fusion.10
  240.6 2.3 subtract_convert_fusion.8
  248.9 2.7 add_convert_fusion.10
  271.6 339.4 %all-gather.3 = f32[128,1,512]{2,1,0:T(1,128)S(1)} all-gather(f32[1,1,512]{2,1,0:T(1,128)S(1)} %bitcast.203), channel_id=2, replica_groups=mesh['det'=2,'grp'=4,'filt'=32] {'grp','filt'}, dimensions={0}, use_global_device_ids=true | all-gather | bytes 264192 | tf_op jit(solution)/shard_map/all_gather | solution.py:187
  (367 shorter events, 181.7 us)
Async XLA Ops:
  0.6 51.2 %copy-start = (bf16[12,4096]{1,0:T(8,128)(2,1)S(1)}, bf16[12,4096]{1,0:T(8,128)(2,1)}, u32[]{:S(2)}) copy-start(bf16[12,4096]{1,0:T(8,128)(2,1)} %param.10) | copy-start | bytes 294916
  3.5 51.6 %all-to-all-start = ((s32[32,1,1]{2,1,0:T(1,128)}), s32[32,1,1]{2,1,0:T(1,128)S(1)}, u32[]{:S(2)}, u32[]{:S(2)}) async-start(s32[32,1,1]{2,1,0:T(1,128)} %copy.78), calls=%async_computation | async-start | bytes 32768 | tf_op jit(solution)/shard_map/all_to_all | solution.py:155
  19.1 4.0 copy-start.19
  55.1 22.5 %all-to-all-start.1 = ((bf16[32,2,2048]{2,1,0:T(2,128)(2,1)}), bf16[32,2,2048]{2,1,0:T(2,128)(2,1)}, u32[]{:S(2)}, u32[]{:S(2)}) async-start(bf16[32,2,2048]{2,1,0:T(2,128)(2,1)} %reshape.108), calls=%async_computation.1 | async-start | bytes 524288 | tf_op jit(solution)/shard_map/all_to_all | solution.py:154
  109.3 3.0 copy-start.8
  109.3 3.0 copy-start.10
  112.2 2.9 copy-start.7
  112.2 2.9 copy-start.9
  140.6 3.0 copy-start.8
  140.6 3.0 copy-start.10
  143.6 2.9 copy-start.7
  143.6 2.9 copy-start.9
  172.0 3.0 copy-start.8
  172.0 3.0 copy-start.10
  174.9 2.9 copy-start.9
  203.3 3.0 copy-start.8
  203.3 3.0 copy-start.10
  206.3 2.9 copy-start.9
  234.7 3.0 copy-start.8
  234.7 3.0 copy-start.10
  237.7 2.9 copy-start.9
  266.1 3.0 copy-start.8
  266.1 3.0 copy-start.10
  269.8 1.2 collective-permute-start
  (54 other events, 72.6 us)

commit v2 on v1

--- a/solution.py
+++ b/solution.py
@@ -1,6 +1,10 @@
+import functools
+
 import jax
 import jax.numpy as jnp
 from jax import lax
+from jax.experimental import pallas as pl
+from jax.experimental.pallas import tpu as pltpu
 from jax.sharding import PartitionSpec as P
 
 N1 = 256
@@ -91,15 +95,78 @@
     return ((weight2d * real_s, weight2d * imag_s), weight2d)
 
 
-def compact(rows, blocks, valid, count):
+def compact(rows, valid, wanted):
     slot_rank = jnp.cumsum(valid.astype(jnp.int32)) - 1
-    wanted = jnp.arange(count, dtype=jnp.int32)[:, None]
-    picker = jnp.logical_and(valid[None, :], slot_rank[None, :] == wanted)
-    picked = jnp.dot(picker.astype(jnp.bfloat16), rows, preferred_element_type=jnp.float32).astype(
+    picker = jnp.logical_and(valid[None, :], slot_rank[None, :] == wanted[:, None])
+    return jnp.dot(picker.astype(jnp.bfloat16), rows, preferred_element_type=jnp.float32).astype(
         jnp.bfloat16
     )
-    picked_blocks = jnp.sum(jnp.where(picker, blocks[None, :], 0), axis=1).astype(jnp.int32)
-    return (picked, picked_blocks)
+
+
+def loudest_kernel(n_grp, n_filt, local_ref, out_ref, held, send_sems, recv_sems):
+    det = lax.axis_index("det")
+    size = n_grp * n_filt
+    me = lax.axis_index("grp") * n_filt + lax.axis_index("filt")
+    mesh_ids = pl.DeviceIdType.MESH
+
+    def peer_of(i):
+        peer = lax.rem(me + 1 + i, size)
+        return (det, peer // n_filt, lax.rem(peer, n_filt))
+
+    def copy_to(i):
+        row = size - 2 - i
+        return pltpu.make_async_remote_copy(
+            src_ref=local_ref,
+            dst_ref=held.at[row],
+            send_sem=send_sems.at[i],
+            recv_sem=recv_sems.at[row],
+            device_id=peer_of(i),
+            device_id_type=mesh_ids,
+        )
+
+    barrier = pltpu.get_barrier_semaphore()
+
+    def greet(i, carry):
+        pl.semaphore_signal(barrier, inc=1, device_id=peer_of(i), device_id_type=mesh_ids)
+        return carry
+
+    lax.fori_loop(0, size - 1, greet, 0)
+    pl.semaphore_wait(barrier, size - 1)
+
+    def send(i, carry):
+        copy_to(i).start()
+        return carry
+
+    lax.fori_loop(0, size - 1, send, 0)
+
+    def finish(i, carry):
+        copy = copy_to(i)
+        copy.wait_send()
+        copy.wait_recv()
+        return carry
+
+    lax.fori_loop(0, size - 1, finish, 0)
+    out_ref[...] = jnp.maximum(local_ref[...], jnp.max(held[...], axis=0))
+
+
+def group_max(local_max):
+    n_grp = lax.axis_size("grp")
+    n_filt = lax.axis_size("filt")
+    size = n_grp * n_filt
+    width = local_max.shape[-1]
+    out = pl.pallas_call(
+        functools.partial(loudest_kernel, n_grp, n_filt),
+        out_shape=jax.ShapeDtypeStruct((1, width), jnp.float32),
+        in_specs=[pl.BlockSpec(memory_space=pltpu.VMEM)],
+        out_specs=pl.BlockSpec(memory_space=pltpu.VMEM),
+        scratch_shapes=[
+            pltpu.VMEM((size - 1, 1, width), jnp.float32),
+            pltpu.SemaphoreType.DMA((size - 1,)),
+            pltpu.SemaphoreType.DMA((size - 1,)),
+        ],
+        compiler_params=pltpu.CompilerParams(collective_id=0, has_side_effects=True),
+    )(local_max.reshape(1, width))
+    return out.reshape(width)
 
 
 def template_transform(windowed, tables):
@@ -146,22 +213,19 @@
     dest_slot = owner * capacity + owner_rank
     slot_ids = jnp.arange(filt_count * capacity, dtype=jnp.int32)[:, None]
     placing = slot_ids == dest_slot[None, :]
-    send_rows = jnp.dot(
-        placing.astype(jnp.bfloat16), templates, preferred_element_type=jnp.float32
-    ).astype(jnp.bfloat16)
-    send_blocks = jnp.sum(jnp.where(placing, chirp_blocks[None, :], 0), axis=1)
-    recv_rows, recv_blocks = (
-        lax.all_to_all(send_rows, "filt", split_axis=0, concat_axis=0, tiled=True),
-        lax.all_to_all(send_blocks, "filt", split_axis=0, concat_axis=0, tiled=True),
-    )
-    local_rows, local_blocks = compact(recv_rows, recv_blocks, recv_blocks > 0, per_dev)
-    my_rows = lax.dynamic_slice_in_dim(local_rows, detector * mine, mine)
-    my_blocks = lax.dynamic_slice_in_dim(local_blocks, detector * mine, mine)
     samples = jnp.arange(TL, dtype=jnp.int32)
     windowed = jnp.where(
-        samples[None, :] < BLK * my_blocks[:, None], my_rows, jnp.zeros_like(my_rows)
-    )
-    windowed = windowed.reshape(mine, TL // N2, N2)
+        samples[None, :] < BLK * chirp_blocks[:, None], templates, jnp.zeros_like(templates)
+    )
+    payload = jnp.concatenate([windowed, jnp.ones((per_dev, 128), jnp.bfloat16)], axis=1)
+    send_rows = jnp.dot(
+        placing.astype(jnp.bfloat16), payload, preferred_element_type=jnp.float32
+    ).astype(jnp.bfloat16)
+    recv_rows = lax.all_to_all(send_rows, "filt", split_axis=0, concat_axis=0, tiled=True)
+    valid = recv_rows[:, TL] > 0.5
+    wanted = detector * mine + jnp.arange(mine, dtype=jnp.int32)
+    my_rows = compact(recv_rows[:, :TL], valid, wanted)
+    windowed = my_rows.reshape(mine, TL // N2, N2)
     strain_both = lax.all_gather(strain[0].astype(jnp.bfloat16), "det")
     asd_both = lax.all_gather(inv_asd[0], "det")
     spec_0, weight_0 = data_spectrum(strain_both[0], asd_both[0], tables)
@@ -184,8 +248,7 @@
         detector == 0, jnp.concatenate([keep, got], axis=0), jnp.concatenate([got, keep], axis=0)
     )
     local_max = jnp.max(peaks, axis=0)
-    gathered = lax.all_gather(local_max, ("grp", "filt"))
-    loudest = jnp.max(gathered, axis=0)
+    loudest = group_max(local_max)
     return (peaks, loudest)
 
 

time: 618 us -> 275 us (0.44)
  blocking collectives: 344 us -> 4.91 us
  Pallas kernels: 0 us -> 22.7 us
  local copies, waits for them, and re-layouts: 74.1 us -> 52 us
  matrix products: 127 us -> 146 us
  waiting for transfers between devices: 12.8 us -> 1.05 us
  starting transfers between devices: 21.2 us -> 11.5 us
    all_gather x1 -> x0, blocking collectives: 339 us -> none  [shards(): gathered = lax.all_gather(local_max, ('grp', 'filt'))]
    pallas_call x0 -> x1, Pallas kernels: none -> 22.7 us  [group_max(): pl.pallas_call(functools.partial(loudest_kernel, n_grp, n_filt), out_shap...]
    dot_general x12, matrix products: 3.1 us -> 14.8 us  [correlate_with(): jnp.dot(cos_first, e_real, preferred_element_type=jnp.float32)]
    all_to_all x1, waiting for transfers between devices: 11.6 us -> 0.01 us  [shards(): lax.all_to_all(send_rows, 'filt', split_axis=0, concat_axis=0, tiled=True)]
    all_to_all x1 -> x0, starting transfers between devices: 11.4 us -> none  [shards(): lax.all_to_all(send_blocks, 'filt', split_axis=0, concat_axis=0, tiled=True)]
    while x120 -> x132, local copies, waits for them, and re-layouts: 9.36 us -> 0.56 us
  transfers between devices with their start and end apart: 3 -> 2, of which waited for: 2 -> 1; matrix products, arithmetic and copies ran while one was open for 5% -> 11% of each run, Pallas kernels for 0% -> 0%
where the time goes in v2:
time: 275 us; the launch traced here: 271 us
  matrix products  146 us (53%)
  local copies, waits for them, and re-layouts  52 us (19%)
  Pallas kernels  22.7 us (8%)
  other arithmetic  22.1 us (8%)
  starting transfers between devices  11.5 us (4%)
  loops' own time  8.76 us (3%)
  blocking collectives  4.91 us (2%)
    dot_general x12, matrix products, correlate_with(): jnp.dot(cos_first, e_imag, preferred_element_type=jnp.float32)  27.1 us
    pallas_call x1, Pallas kernels, group_max(): pl.pallas_call(functools.partial(loudest_kernel, n_grp, n_filt), out_shap...  22.7 us
    dot_general x12, matrix products, correlate_with(): jnp.dot(q_imag, cos_back, preferred_element_type=jnp.float32)  22.1 us
    dot_general x8, matrix products, forward(): jnp.dot(real_b, sin_second, preferred_element_type=jnp.float32)  15.6 us
    div x12, local copies, waits for them, and re-layouts, correlate_with(): return (z_real * z_real + z_imag * z_imag) / (NFFT * sigma)  14.8 us
    dot_general x12, matrix products, correlate_with(): jnp.dot(cos_first, e_real, preferred_element_type=jnp.float32)  14.8 us
    dot_general x12, matrix products, correlate_with(): jnp.dot(sin_first, e_imag, preferred_element_type=jnp.float32)  12.8 us
    dot_general x12, matrix products, correlate_with(): jnp.dot(q_imag, sin_back, preferred_element_type=jnp.float32)  12.4 us
  transfers between devices with their start and end apart: 2, of which 1 were waited for; matrix products, arithmetic and copies ran while one was open for 11% of the time, Pallas kernels for 0%

profile of v2, /device:TPU:32, one launch (start us, length us, event | category | flops | bytes accessed | tf_op | source)
XLA Modules:
  0.0 271.1 jit_solution(17570705754583156987)
XLA Ops:
  4.9 11.4 %all-to-all-start = ((bf16[32,2,2112]{2,1,0:T(2,128)(2,1)}), bf16[32,2,2112]{2,1,0:T(2,128)(2,1)}, u32[]{:S(2)}, u32[]{:S(2)}) async-start(bf16[32,2,2112]{2,1,0:T(2,128)(2,1)} %reshape.94), calls=%async_computation | async-start | bytes 557056 | tf_op jit(solution)/shard_map/all_to_all | solution.py:224
  24.2 2.6 all-gather.1
  26.8 3.0 %slice_reduce_fusion = (bf16[131072]{0:T(1024)(128)(2,1)S(1)}, bf16[131072]{0:T(1024)(128)(2,1)S(1)}) fusion(bf16[2,1,131072]{2,1,0:T(2,128)(2,1)S(1)} %all-gather.1), kind=kLoop, calls=%fused_computation.77 | loop fusion | bytes 1048576 | tf_op jit(solution)/shard_map/slice | solution.py:232
  33.2 2.3 all-gather
  37.8 2.4 subtract_convert_fusion.5
  52.0 2.3 reshape.95
  57.1 186.8 %while.12 = (s32[]{:T(128)}, f32[6,1024]{1,0:T(8,128)}, bf16[6,8,512]{2,1,0:T(8,128)(2,1)}, bf16[256,256]{1,0:T(8,128)(2,1)S(1)}, f32[256,512]{0,1:T(8,128)S(1)}...) while((s32[]{:T(128)}, f32[6,1024]{1,0:T(8,128)}, ...), condition=%wide.region_6.7_spmd, body=%wide.region_2.6_spmd.sunk | while | flops 1353776128 | bytes 48920096 | solution.py:243
  60.0 2.2 subtract_convert_fusion.8
  67.5 2.6 add_convert_fusion.10
  80.9 2.3 fusion.253
  91.2 2.2 subtract_convert_fusion.8
  98.6 2.6 add_convert_fusion.10
  112.0 2.3 fusion.253
  122.3 2.2 subtract_convert_fusion.8
  129.8 2.6 add_convert_fusion.10
  143.2 2.3 fusion.253
  153.5 2.2 subtract_convert_fusion.8
  160.9 2.6 add_convert_fusion.10
  174.3 2.3 fusion.253
  192.1 2.6 add_convert_fusion.10
  205.5 2.3 fusion.253
  223.2 2.6 add_convert_fusion.10
  236.6 2.3 fusion.253
  247.1 22.7 %shard_map.77 = f32[1,512]{1,0:T(1,128)} custom-call(f32[1,512]{1,0:T(1,128)} %bitcast.202), custom_call_target="tpu_custom_call" | custom-call | tf_op jit(solution)/shard_map/pallas_call | solution.py:157
  (364 shorter events, 175.3 us)
Async XLA Ops:
  4.9 47.1 %all-to-all-start = ((bf16[32,2,2112]{2,1,0:T(2,128)(2,1)}), bf16[32,2,2112]{2,1,0:T(2,128)(2,1)}, u32[]{:S(2)}, u32[]{:S(2)}) async-start(bf16[32,2,2112]{2,1,0:T(2,128)(2,1)} %reshape.94), calls=%async_computation | async-start | bytes 557056 | tf_op jit(solution)/shard_map/all_to_all | solution.py:224
  20.5 3.3 %copy-start.17 = (f32[1,131072]{1,0:T(1,128)S(1)}, f32[1,131072]{1,0:T(1,128)}, u32[]{:S(2)}) copy-start(f32[1,131072]{1,0:T(1,128)} %param.8) | copy-start | bytes 1572868
  85.2 3.0 %copy-start.1 = (bf16[256,256]{1,0:T(8,128)(2,1)S(1)}, bf16[256,256]{1,0:T(8,128)(2,1)}, u32[]{:S(2)}) copy-start(bf16[256,256]{1,0:T(8,128)(2,1)} %copy-done) | copy-start | bytes 393220 | tf_op jit(solution)/shard_map/while
  85.3 3.0 %copy-start.8 = (f32[256,256]{1,0:T(8,128)S(1)}, f32[256,256]{1,0:T(8,128)}, u32[]{:S(2)}) copy-start(f32[256,256]{1,0:T(8,128)} %copy-done.7) | copy-start | bytes 786436 | tf_op jit(solution)/shard_map/while
  85.3 3.0 %copy-start.10 = (f32[256,256]{1,0:T(8,128)S(1)}, f32[256,256]{1,0:T(8,128)}, u32[]{:S(2)}) copy-start(f32[256,256]{1,0:T(8,128)} %copy-done.9) | copy-start | bytes 786436 | tf_op jit(solution)/shard_map/while
  88.3 2.9 %copy-start.7 = (f32[256,256]{1,0:T(8,128)}, f32[256,256]{1,0:T(8,128)S(1)}, u32[]{:S(2)}) copy-start(f32[256,256]{1,0:T(8,128)S(1)} %get-tuple-element.600) | copy-start | bytes 786436 | tf_op jit(solution)/shard_map/while
  116.4 3.0 %copy-start.1 = (bf16[256,256]{1,0:T(8,128)(2,1)S(1)}, bf16[256,256]{1,0:T(8,128)(2,1)}, u32[]{:S(2)}) copy-start(bf16[256,256]{1,0:T(8,128)(2,1)} %copy-done) | copy-start | bytes 393220 | tf_op jit(solution)/shard_map/while
  116.4 3.0 %copy-start.8 = (f32[256,256]{1,0:T(8,128)S(1)}, f32[256,256]{1,0:T(8,128)}, u32[]{:S(2)}) copy-start(f32[256,256]{1,0:T(8,128)} %copy-done.7) | copy-start | bytes 786436 | tf_op jit(solution)/shard_map/while
  116.4 3.0 %copy-start.10 = (f32[256,256]{1,0:T(8,128)S(1)}, f32[256,256]{1,0:T(8,128)}, u32[]{:S(2)}) copy-start(f32[256,256]{1,0:T(8,128)} %copy-done.9) | copy-start | bytes 786436 | tf_op jit(solution)/shard_map/while
  147.5 3.0 %copy-start.1 = (bf16[256,256]{1,0:T(8,128)(2,1)S(1)}, bf16[256,256]{1,0:T(8,128)(2,1)}, u32[]{:S(2)}) copy-start(bf16[256,256]{1,0:T(8,128)(2,1)} %copy-done) | copy-start | bytes 393220 | tf_op jit(solution)/shard_map/while
  147.6 3.0 %copy-start.8 = (f32[256,256]{1,0:T(8,128)S(1)}, f32[256,256]{1,0:T(8,128)}, u32[]{:S(2)}) copy-start(f32[256,256]{1,0:T(8,128)} %copy-done.7) | copy-start | bytes 786436 | tf_op jit(solution)/shard_map/while
  147.6 3.0 %copy-start.10 = (f32[256,256]{1,0:T(8,128)S(1)}, f32[256,256]{1,0:T(8,128)}, u32[]{:S(2)}) copy-start(f32[256,256]{1,0:T(8,128)} %copy-done.9) | copy-start | bytes 786436 | tf_op jit(solution)/shard_map/while
  150.5 2.9 %copy-start.7 = (f32[256,256]{1,0:T(8,128)}, f32[256,256]{1,0:T(8,128)S(1)}, u32[]{:S(2)}) copy-start(f32[256,256]{1,0:T(8,128)S(1)} %get-tuple-element.600) | copy-start | bytes 786436 | tf_op jit(solution)/shard_map/while
  150.6 2.9 %copy-start.9 = (f32[256,256]{1,0:T(8,128)}, f32[256,256]{1,0:T(8,128)S(1)}, u32[]{:S(2)}) copy-start(f32[256,256]{1,0:T(8,128)S(1)} %get-tuple-element.599) | copy-start | bytes 786436 | tf_op jit(solution)/shard_map/while
  178.7 3.0 %copy-start.1 = (bf16[256,256]{1,0:T(8,128)(2,1)S(1)}, bf16[256,256]{1,0:T(8,128)(2,1)}, u32[]{:S(2)}) copy-start(bf16[256,256]{1,0:T(8,128)(2,1)} %copy-done) | copy-start | bytes 393220 | tf_op jit(solution)/shard_map/while
  178.7 3.0 %copy-start.8 = (f32[256,256]{1,0:T(8,128)S(1)}, f32[256,256]{1,0:T(8,128)}, u32[]{:S(2)}) copy-start(f32[256,256]{1,0:T(8,128)} %copy-done.7) | copy-start | bytes 786436 | tf_op jit(solution)/shard_map/while
  178.7 3.0 %copy-start.10 = (f32[256,256]{1,0:T(8,128)S(1)}, f32[256,256]{1,0:T(8,128)}, u32[]{:S(2)}) copy-start(f32[256,256]{1,0:T(8,128)} %copy-done.9) | copy-start | bytes 786436 | tf_op jit(solution)/shard_map/while
  209.8 3.0 %copy-start.1 = (bf16[256,256]{1,0:T(8,128)(2,1)S(1)}, bf16[256,256]{1,0:T(8,128)(2,1)}, u32[]{:S(2)}) copy-start(bf16[256,256]{1,0:T(8,128)(2,1)} %copy-done) | copy-start | bytes 393220 | tf_op jit(solution)/shard_map/while
  209.8 3.0 %copy-start.8 = (f32[256,256]{1,0:T(8,128)S(1)}, f32[256,256]{1,0:T(8,128)}, u32[]{:S(2)}) copy-start(f32[256,256]{1,0:T(8,128)} %copy-done.7) | copy-start | bytes 786436 | tf_op jit(solution)/shard_map/while
  209.9 3.0 %copy-start.10 = (f32[256,256]{1,0:T(8,128)S(1)}, f32[256,256]{1,0:T(8,128)}, u32[]{:S(2)}) copy-start(f32[256,256]{1,0:T(8,128)} %copy-done.9) | copy-start | bytes 786436 | tf_op jit(solution)/shard_map/while
  241.0 3.0 %copy-start.1 = (bf16[256,256]{1,0:T(8,128)(2,1)S(1)}, bf16[256,256]{1,0:T(8,128)(2,1)}, u32[]{:S(2)}) copy-start(bf16[256,256]{1,0:T(8,128)(2,1)} %copy-done) | copy-start | bytes 393220 | tf_op jit(solution)/shard_map/while
  241.0 3.0 %copy-start.8 = (f32[256,256]{1,0:T(8,128)S(1)}, f32[256,256]{1,0:T(8,128)}, u32[]{:S(2)}) copy-start(f32[256,256]{1,0:T(8,128)} %copy-done.7) | copy-start | bytes 786436 | tf_op jit(solution)/shard_map/while
  241.0 3.0 %copy-start.10 = (f32[256,256]{1,0:T(8,128)S(1)}, f32[256,256]{1,0:T(8,128)}, u32[]{:S(2)}) copy-start(f32[256,256]{1,0:T(8,128)} %copy-done.9) | copy-start | bytes 786436 | tf_op jit(solution)/shard_map/while
  244.7 1.2 collective-permute-start
  (54 other events, 92.0 us)

commit v3 on v2

--- a/solution.py
+++ b/solution.py
@@ -169,32 +169,129 @@
     return out.reshape(width)
 
 
-def template_transform(windowed, tables):
-    rows_used = windowed.shape[0]
-    return forward(windowed, tables[0][:, :rows_used], tables[1][:, :rows_used], tables)
-
-
-def correlate_with(temp_real, temp_imag, spectrum, weight2d, tables):
+def filter_kernel(
+    rem_ref, x_ref, cfn_ref, sfn_ref, ct_ref, st_ref, cs_ref, ss_ref, cb_ref, sb_ref,
+    cf_ref, sf_ref, cfr_ref, sfr_ref, pr_ref, pi_ref, w2_ref, out_ref, er_ref, ei_ref,
+):
+    f32 = jnp.float32
+    bf16 = jnp.bfloat16
+    x = x_ref[0]
+    cos_twist = ct_ref[...]
+    sin_twist = st_ref[...]
+    real_a = jnp.dot(cfn_ref[...], x, preferred_element_type=f32)
+    imag_a = -jnp.dot(sfn_ref[...], x, preferred_element_type=f32)
+    real_b = (real_a * cos_twist + imag_a * sin_twist).astype(bf16)
+    imag_b = (imag_a * cos_twist - real_a * sin_twist).astype(bf16)
+    cos_second = cs_ref[...]
+    sin_second = ss_ref[...]
+    temp_real = jnp.dot(real_b, cos_second, preferred_element_type=f32) + jnp.dot(
+        imag_b, sin_second, preferred_element_type=f32
+    )
+    temp_imag = jnp.dot(imag_b, cos_second, preferred_element_type=f32) - jnp.dot(
+        real_b, sin_second, preferred_element_type=f32
+    )
+    power = temp_real * temp_real + temp_imag * temp_imag
+    cos_back = cb_ref[...]
+    sin_back = sb_ref[...]
+
+    def back_half(d):
+        sigma = jnp.sum(w2_ref[d] * power, axis=(0, 1), keepdims=True)
+        data_real = pr_ref[d]
+        data_imag = pi_ref[d]
+        q_real = (temp_real * data_real + temp_imag * data_imag).astype(bf16)
+        q_imag = (temp_real * data_imag - temp_imag * data_real).astype(bf16)
+        d_real = jnp.dot(q_real, cos_back, preferred_element_type=f32) - jnp.dot(
+            q_imag, sin_back, preferred_element_type=f32
+        )
+        d_imag = jnp.dot(q_real, sin_back, preferred_element_type=f32) + jnp.dot(
+            q_imag, cos_back, preferred_element_type=f32
+        )
+        e_real = (d_real * cos_twist - d_imag * sin_twist).astype(bf16)
+        e_imag = (d_real * sin_twist + d_imag * cos_twist).astype(bf16)
+        return sigma, e_real, e_imag
+
+    sigma0, e_real, e_imag = back_half(0)
+    cos_first = cf_ref[...]
+    sin_first = sf_ref[...]
+    z_real = jnp.dot(cos_first, e_real, preferred_element_type=f32) - jnp.dot(
+        sin_first, e_imag, preferred_element_type=f32
+    )
+    z_imag = jnp.dot(sin_first, e_real, preferred_element_type=f32) + jnp.dot(
+        cos_first, e_imag, preferred_element_type=f32
+    )
+    first = (z_real * z_real + z_imag * z_imag) / (NFFT * sigma0)
+    sigma1, e_real, e_imag = back_half(1)
+    er_ref[...] = e_real
+    ei_ref[...] = e_imag
+    rem = rem_ref[0]
+    tiles = first.shape[1] // BLK
+    for col in range(tiles):
+        src = lax.rem(col + rem, tiles)
+        carry = (col + rem) // tiles
+        cols = pl.ds(pl.multiple_of(src * BLK, BLK), BLK)
+        e_r = er_ref[:, cols]
+        e_i = ei_ref[:, cols]
+        cos_rows = cfr_ref[carry]
+        sin_rows = sfr_ref[carry]
+        z_real = jnp.dot(cos_rows, e_r, preferred_element_type=f32) - jnp.dot(
+            sin_rows, e_i, preferred_element_type=f32
+        )
+        z_imag = jnp.dot(sin_rows, e_r, preferred_element_type=f32) + jnp.dot(
+            cos_rows, e_i, preferred_element_type=f32
+        )
+        second = (z_real * z_real + z_imag * z_imag) / (NFFT * sigma1)
+        network = first[:, col * BLK:(col + 1) * BLK] + second
+        out_ref[0, :, col:col + 1] = jnp.max(network, axis=1, keepdims=True)
+
+
+def filter_bank(windowed, tables, spectra, weights, shift):
     cos_first, sin_first, cos_twist, sin_twist, cos_second, sin_second, cos_back, sin_back = tables
-    sigma = jnp.sum(weight2d * weight2d * (temp_real * temp_real + temp_imag * temp_imag))
-    data_real, data_imag = spectrum
-    q_real = (temp_real * data_real + temp_imag * data_imag).astype(jnp.bfloat16)
-    q_imag = (temp_real * data_imag - temp_imag * data_real).astype(jnp.bfloat16)
-    d_real = jnp.dot(q_real, cos_back, preferred_element_type=jnp.float32) - jnp.dot(
-        q_imag, sin_back, preferred_element_type=jnp.float32
-    )
-    d_imag = jnp.dot(q_real, sin_back, preferred_element_type=jnp.float32) + jnp.dot(
-        q_imag, cos_back, preferred_element_type=jnp.float32
-    )
-    e_real = (d_real * cos_twist - d_imag * sin_twist).astype(jnp.bfloat16)
-    e_imag = (d_real * sin_twist + d_imag * cos_twist).astype(jnp.bfloat16)
-    z_real = jnp.dot(cos_first, e_real, preferred_element_type=jnp.float32) - jnp.dot(
-        sin_first, e_imag, preferred_element_type=jnp.float32
-    )
-    z_imag = jnp.dot(sin_first, e_real, preferred_element_type=jnp.float32) + jnp.dot(
-        cos_first, e_imag, preferred_element_type=jnp.float32
-    )
-    return (z_real * z_real + z_imag * z_imag) / (NFFT * sigma)
+    count, rows_used, width = windowed.shape
+    pad_rows = 128
+    x = jnp.concatenate(
+        [windowed, jnp.zeros((count, pad_rows - rows_used, width), windowed.dtype)], axis=1
+    )
+    tiles = N2 // BLK
+    quot = shift // tiles
+    rem = lax.rem(shift, tiles).reshape(1)
+    cos_rolled = jnp.stack(
+        [jnp.roll(cos_first, -quot, axis=0), jnp.roll(cos_first, -(quot + 1), axis=0)]
+    )
+    sin_rolled = jnp.stack(
+        [jnp.roll(sin_first, -quot, axis=0), jnp.roll(sin_first, -(quot + 1), axis=0)]
+    )
+    data_real = jnp.stack([spectra[0][0], spectra[1][0]])
+    data_imag = jnp.stack([spectra[0][1], spectra[1][1]])
+    weight2 = jnp.stack([weights[0] * weights[0], weights[1] * weights[1]])
+    operands = [
+        cos_first[:, :pad_rows], sin_first[:, :pad_rows], cos_twist, sin_twist,
+        cos_second, sin_second, cos_back, sin_back, cos_first, sin_first,
+        cos_rolled, sin_rolled, data_real, data_imag, weight2,
+    ]
+
+    def whole(array):
+        nd = array.ndim
+        return pl.BlockSpec(array.shape, lambda i, r, nd=nd: (0,) * nd)
+
+    grid_spec = pltpu.PrefetchScalarGridSpec(
+        num_scalar_prefetch=1,
+        grid=(count,),
+        in_specs=[pl.BlockSpec((1, pad_rows, width), lambda i, r: (i, 0, 0))]
+        + [whole(a) for a in operands],
+        out_specs=pl.BlockSpec((1, N1, tiles), lambda i, r: (i, 0, 0)),
+        scratch_shapes=[pltpu.VMEM((N1, N2), jnp.bfloat16), pltpu.VMEM((N1, N2), jnp.bfloat16)],
+    )
+    matmuls = 2 * N1 * pad_rows * N2 + 4 * N1 * N2 * (N2 // 2) + 16 * N1 * (N2 // 2) * N2
+    out = pl.pallas_call(
+        filter_kernel,
+        out_shape=jax.ShapeDtypeStruct((count, N1, tiles), jnp.float32),
+        grid_spec=grid_spec,
+        compiler_params=pltpu.CompilerParams(vmem_limit_bytes=48 * 1024 * 1024),
+        cost_estimate=pl.CostEstimate(
+            flops=2 * matmuls * count, transcendentals=0, bytes_accessed=8 * 1024 * 1024
+        ),
+    )(rem, x, *operands)
+    return out.reshape(count, N1 * tiles)
 
 
 def shards(strain, inv_asd, templates, chirp_blocks, owner, slide):
@@ -230,17 +327,7 @@
     asd_both = lax.all_gather(inv_asd[0], "det")
     spec_0, weight_0 = data_spectrum(strain_both[0], asd_both[0], tables)
     spec_1, weight_1 = data_spectrum(strain_both[1], asd_both[1], tables)
-    shift = slide[0]
-
-    def filter_template(kept_row):
-        temp_real, temp_imag = template_transform(kept_row, tables)
-        first = correlate_with(temp_real, temp_imag, spec_0, weight_0, tables)
-        second = correlate_with(temp_real, temp_imag, spec_1, weight_1, tables)
-        second = jnp.roll(second.reshape(n_blk, BLK), -shift, axis=0)
-        network = first.reshape(n_blk, BLK) + second
-        return jnp.max(network, axis=1)
-
-    full = lax.map(filter_template, windowed)
+    full = filter_bank(windowed, tables, (spec_0, spec_1), (weight_0, weight_1), slide[0])
     keep = lax.dynamic_slice_in_dim(full, detector * half_blk, half_blk, axis=1)
     give = lax.dynamic_slice_in_dim(full, (1 - detector) * half_blk, half_blk, axis=1)
     got = lax.ppermute(give, "det", [(0, 1), (1, 0)])

time: 275 us -> 118 us (0.43)
  matrix products: 146 us -> 14 us
  local copies, waits for them, and re-layouts: 52 us -> 25 us
  Pallas kernels: 22.7 us -> 40 us
  loops' own time: 8.76 us -> 0 us
  other arithmetic: 22.1 us -> 17.8 us
    dot_general x96 -> x0, matrix products: 102 us -> none  [the longest x12 27.1 us: correlate_with(): jnp.dot(cos_first, e_imag, preferred_element_type=jnp.float32)]
    pallas_call x0 -> x1, Pallas kernels: none -> 17.2 us  [filter_bank(): pl.pallas_call(filter_kernel, out_shape=jax.ShapeDtypeStruct((count, N1,...]
    div x12 -> x0, local copies, waits for them, and re-layouts: 14.8 us -> none  [correlate_with(): return (z_real * z_real + z_imag * z_imag) / (NFFT * sigma)]
    dot_general x8 -> x2, matrix products: 15.6 us -> 1.86 us  [forward(): jnp.dot(real_b, sin_second, preferred_element_type=jnp.float32)]
    reduce_max x6 -> x0, other arithmetic: 9.36 us -> none  [filter_template(): return jnp.max(network, axis=1)]
    another operation x1 -> x0, loops' own time: 8.76 us -> none  [shards(): full = lax.map(filter_template, windowed)]
    dynamic_update_slice x6 -> x0, local copies, waits for them, and re-layouts: 8.39 us -> none  [shards(): full = lax.map(filter_template, windowed)]
    unnamed x25 -> x49, local copies, waits for them, and re-layouts: 5.86 us -> 13.5 us
  transfers between devices with their start and end apart: 2 -> 2, of which waited for: 1 -> 1; matrix products, arithmetic and copies ran while one was open for 11% -> 33% of each run, Pallas kernels for 0% -> 0%
where the time goes in v3:
time: 118 us; the launch traced here: 116 us
  Pallas kernels  40 us (34%)
  local copies, waits for them, and re-layouts  25 us (21%)
  other arithmetic  17.8 us (15%)
  matrix products  14 us (12%)
  starting transfers between devices  11.6 us (10%)
  blocking collectives  4.91 us (4%)
  between operations  1.68 us (1%)
    pallas_call x1, Pallas kernels, group_max(): pl.pallas_call(functools.partial(loudest_kernel, n_grp, n_filt), out_shap...  22.8 us
    pallas_call x1, Pallas kernels, filter_bank(): pl.pallas_call(filter_kernel, out_shape=jax.ShapeDtypeStruct((count, N1,...  17.2 us
    unnamed x49, local copies, waits for them, and re-layouts  13.5 us
    all_to_all x1, starting transfers between devices, shards(): lax.all_to_all(send_rows, 'filt', split_axis=0, concat_axis=0, tiled=True)  11.4 us
    slice x2, local copies, waits for them, and re-layouts, shards(): spec_0, weight_0 = data_spectrum(strain_both[0], asd_both[0], tables)  5.71 us
    dot_general x2, matrix products, forward(): real_a = jnp.dot(cos_rows, signal, preferred_element_type=jnp.float32)  3.44 us
    convert_element_type x1, other arithmetic, make_tables(): jnp.sin(back).astype(jnp.bfloat16)  2.86 us
    all_gather x1, blocking collectives, shards(): strain_both = lax.all_gather(strain[0].astype(jnp.bfloat16), 'det')  2.56 us
  transfers between devices with their start and end apart: 2, of which 1 were waited for; matrix products, arithmetic and copies ran while one was open for 33% of the time, Pallas kernels for 0%

profile of v3, /device:TPU:32, one launch (start us, length us, event | category | flops | bytes accessed | tf_op | source)
XLA Modules:
  0.0 116.0 jit_solution(5951136713024618696)
XLA Ops:
  4.9 11.4 %all-to-all-start = ((bf16[32,2,2112]{2,1,0:T(2,128)(2,1)}), bf16[32,2,2112]{2,1,0:T(2,128)(2,1)}, u32[]{:S(2)}, u32[]{:S(2)}) async-start(bf16[32,2,2112]{2,1,0:T(2,128)(2,1)} %reshape.92), calls=%async_computation | async-start | bytes 557056 | tf_op jit(solution)/shard_map/all_to_all | solution.py:321
  16.3 2.1 %fusion.32 = (f32[256,512]{1,0:T(8,128)S(1)}, f32[256,512]{1,0:T(8,128)S(1)}) fusion(), kind=kLoop, calls=%fused_computation.73 | loop fusion | flops 1835008 | bytes 1048576 | tf_op jit(solution)/shard_map/sin | solution.py:41
  18.4 2.9 %sine_convert_fusion = (bf16[256,512]{1,0:T(8,128)(2,1)S(1)}, bf16[256,512]{1,0:T(8,128)(2,1)}) fusion(), kind=kLoop, calls=%fused_computation.42 | loop fusion | flops 2097152 | bytes 524288 | tf_op jit(solution)/shard_map/convert_element_type | solution.py:45
  21.3 2.2 %sine_convert_fusion.1 = (bf16[512,256]{1,0:T(8,128)(2,1)S(1)}, bf16[512,256]{1,0:T(8,128)(2,1)S(1)}) fusion(), kind=kLoop, calls=%fused_computation.44 | loop fusion | flops 2097152 | bytes 524288 | tf_op jit(solution)/shard_map/convert_element_type | solution.py:43
  23.4 1.1 sine_convert_fusion.2
  25.6 2.6 %all-gather.1 = bf16[2,1,131072]{2,1,0:T(2,128)(2,1)S(1)} all-gather(bf16[1,1,131072]{2,1,0:T(2,128)(2,1)S(1)} %convert_bitcast_fusion), channel_id=1, replica_groups=mesh['det'=2,'grp'=4,'filt'=32] {'det'}, dimensions={0}, use_global_device_ids=true | all-gather | bytes 786432 | tf_op jit(solution)/shard_map/all_gather | solution.py:326
  28.2 3.7 %slice_reduce_fusion.1 = (bf16[131072]{0:T(1024)(128)(2,1)S(1)}, bf16[131072]{0:T(1024)(128)(2,1)}) fusion(bf16[2,1,131072]{2,1,0:T(2,128)(2,1)S(1)} %all-gather.1), kind=kLoop, calls=%fused_computation.33 | loop fusion | bytes 1048576 | tf_op jit(solution)/shard_map/slice | solution.py:328
  31.9 1.1 reshape_squeeze.15
  33.6 1.0 convolution_negate_fusion
  34.7 1.0 fusion.51
  36.5 1.0 convolution_negate_fusion.1
  37.6 2.3 %all-gather = f32[2,1,65536]{2,1,0:T(1,128)S(1)} all-gather(f32[1,1,65536]{2,1,0:T(1,128)S(1)} %bitcast.78), channel_id=1, replica_groups=mesh['det'=2,'grp'=4,'filt'=32] {'det'}, dimensions={0}, use_global_device_ids=true | all-gather | bytes 786432 | tf_op jit(solution)/shard_map/all_gather | solution.py:327
  39.9 2.0 %slice_reduce_fusion.3 = (f32[65536]{0:T(1024)S(1)}, f32[65536]{0:T(1024)}) fusion(f32[2,1,65536]{2,1,0:T(1,128)S(1)} %all-gather), kind=kLoop, calls=%fused_computation.65 | loop fusion | bytes 1048576 | tf_op jit(solution)/shard_map/slice | solution.py:328
  42.2 2.4 %subtract_convert_fusion.1 = (bf16[256,512]{1,0:T(8,128)(2,1)S(1)}, bf16[256,512]{1,0:T(8,128)(2,1)}, bf16[256,512]{1,0:T(8,128)(2,1)S(1)}, bf16[256,512]{1,0:T(8,128)(2,1)S(1)}) fusion(f32[256,512]{1,0:T(8,128)S(1)} %get-tuple-element.14.st_ref, f32[256,512]{1,0:T(8,128)} %convolution_negate_fusion.1, f32[256,512]{1,0:T(8,128)S(1)} %get-tuple-element.13.ct_ref, ...), kind=kOutput, calls=%fused_computation.39 | convolution fusion | flops 69206016 | bytes 4063232 | tf_op jit(solution)/shard_map/dot_general | solution.py:51
  47.2 1.1 copy.18
  48.3 1.2 %fusion.50 = f32[256,256]{1,0:T(8,128)S(1)} fusion(bf16[256,512]{1,0:T(8,128)(2,1)} %get-tuple-element.26, bf16[512,256]{1,0:T(8,128)(2,1)S(1)} %get-tuple-element.15.cs_ref), kind=kOutput, calls=%fused_computation.113 | convolution fusion | flops 67108864 | bytes 786432 | tf_op jit(solution)/shard_map/dot_general | solution.py:55
  56.9 1.0 pad_maximum_fusion.1.pi_ref
  60.7 1.8 %pad_maximum_fusion.pr_ref = f32[2,256,256]{2,1,0:T(8,128)} fusion(f32[1,256,256]{2,1,0:T(8,128)} %fusion.6, f32[1,256,256]{2,1,0:T(8,128)S(1)} %copy-done.9), kind=kLoop, calls=%fused_computation.34 | loop fusion | flops 131072 | bytes 1048576 | tf_op jit(solution)/shard_map/stack | solution.py:263
  63.4 2.3 %reshape.93 = bf16[32,1,4224]{2,1,0:T(2,128)(2,1)S(1)} reshape(bf16[32,2,2112]{2,1,0:T(2,128)(2,1)} %all-to-all-done) | data formatting | bytes 540672
  66.7 1.2 %convolution_convert_fusion.1 = bf16[6,4096]{1,0:T(8,128)(2,1)S(1)} fusion(bf16[32,4224]{1,0:T(8,128)(2,1)} %bitcast.77, s32[32]{0:T(128)S(1)} %add_reduce_fusion, s32[6]{0:T(128)S(1)} %iota_add_fusion, pred[32]{0:T(512)(128)(4,1)S(1)} %get-tuple-element.31), kind=kOutput, calls=%fused_computation.2 | convolution fusion | flops 1597824 | bytes 311480 | tf_op jit(solution)/shard_map/dot_general | solution.py:101
  71.8 17.2 %shard_map.77 = f32[6,256,4]{2,1,0:T(8,128)S(1)} custom-call(s32[1]{0:T(128)} %bitcast.1.rem_ref, bf16[6,128,512]{2,1,0:T(8,128)(2,1)S(1)} %concatenate.16.x_ref, bf16[256,128]{1,0:T(8,128)(2,1)S(1)} %slice.26.cfn_ref, bf16[256,128]{1,0:T(8,128)(2,1)S(1)} %slice.27.sfn_ref, f32[256,512]{1,0:T(8,128)S(1)} %get-tuple-element.13.ct_ref, ...), custom_call_target="tpu_custom_call" | custom-call | flops 8455716864 | bytes 8388608 | tf_op jit(solution)/shard_map/pallas_call | solution.py:285
  89.7 1.0 collective-permute-done
  90.7 1.2 %fusion.49 = (f32[512]{0:T(512)}, f32[12,512]{1,0:T(8,128)}) fusion(f32[6,512]{1,0:T(8,128)S(1)} %get-tuple-element.38, f32[6,512]{1,0:T(8,128)S(1)} %collective-permute-done, pred[]{:T(512)S(6)} %eq.29), kind=kLoop, calls=%fused_computation.112 | loop fusion | flops 24064 | bytes 51201 | tf_op jit(solution)/shard_map/reduce_max | solution.py:337
  91.9 22.8 %shard_map.78 = f32[1,512]{1,0:T(1,128)} custom-call(f32[1,512]{1,0:T(1,128)} %bitcast.81), custom_call_target="tpu_custom_call" | custom-call | tf_op jit(solution)/shard_map/pallas_call | solution.py:157
  (86 shorter events, 26.7 us)
Async XLA Ops:
  0.6 0.7 copy-start.20
  4.9 58.4 %all-to-all-start = ((bf16[32,2,2112]{2,1,0:T(2,128)(2,1)}), bf16[32,2,2112]{2,1,0:T(2,128)(2,1)}, u32[]{:S(2)}, u32[]{:S(2)}) async-start(bf16[32,2,2112]{2,1,0:T(2,128)(2,1)} %reshape.92), calls=%async_computation | async-start | bytes 557056 | tf_op jit(solution)/shard_map/all_to_all | solution.py:321
  21.2 4.0 %copy-start.14 = (f32[1,131072]{1,0:T(1,128)S(1)}, f32[1,131072]{1,0:T(1,128)}, u32[]{:S(2)}) copy-start(f32[1,131072]{1,0:T(1,128)} %param.8) | copy-start | bytes 1572868
  36.5 1.1 copy-start.18
  45.5 0.9 copy-start.11
  48.3 1.3 %copy-start.5 = (bf16[256,512]{1,0:T(8,128)(2,1)S(1)}, bf16[256,512]{1,0:T(8,128)(2,1)}, u32[]{:S(2)}) copy-start(bf16[256,512]{1,0:T(8,128)(2,1)} %get-tuple-element.26) | copy-start | bytes 786436
  48.3 1.3 %copy-start.8 = (f32[256,256]{1,0:T(8,128)S(1)}, f32[256,256]{1,0:T(8,128)}, u32[]{:S(2)}) copy-start(f32[256,256]{1,0:T(8,128)} %fusion.53) | copy-start | bytes 786436
  51.5 0.9 copy-start.7
  53.3 0.9 copy-start.12
  54.3 1.0 copy-start.13
  56.0 0.9 copy-start.10
  56.9 1.0 copy-start.15
  58.0 0.9 copy-start.16
  58.0 1.1 copy-start.17
  59.8 0.9 copy-start.9
  65.7 0.7 copy-start.6
  66.7 1.3 %copy-start.1 = (f32[2,256,256]{2,1,0:T(8,128)S(1)}, f32[2,256,256]{2,1,0:T(8,128)}, u32[]{:S(2)}) copy-start(f32[2,256,256]{2,1,0:T(8,128)} %pad_maximum_fusion.2.w2_ref) | copy-start | bytes 1572868
  67.9 1.1 copy-start
  69.0 0.9 copy-start.2
  69.9 0.9 copy-start.3
  70.9 0.9 copy-start.4
  89.5 1.3 %collective-permute-start = (f32[6,512]{1,0:T(8,128)S(1)}, f32[6,512]{1,0:T(8,128)S(1)}, u32[]{:S(2)}, u32[]{:S(2)}) collective-permute-start(f32[6,512]{1,0:T(8,128)S(1)} %get-tuple-element.37), channel_id=1, source_target_pairs={{0,128},{128,0},{1,129},{129,1},{2,130},{130,2},{3,131},{131,3},{4... | collective-permute-start | bytes 36872 | tf_op jit(solution)/shard_map/ppermute | solution.py:333
  114.8 0.7 copy-start.19

commit v4 on v3

--- a/solution.py
+++ b/solution.py
@@ -30,69 +30,18 @@
 
 
 def make_tables():
-    first = angle_table(N1, N1, N1)
     twist = angle_table(N1, N2, NFFT)
     second = angle_table(N2, N2 // 2, N2)
-    back = angle_table(N2 // 2, N2, N2)
+    cos_second = jnp.cos(second).astype(jnp.bfloat16)
+    sin_second = jnp.sin(second).astype(jnp.bfloat16)
     return (
-        jnp.cos(first).astype(jnp.bfloat16),
-        jnp.sin(first).astype(jnp.bfloat16),
+        cos_second[0::2],
+        sin_second[0::2],
         jnp.cos(twist),
         jnp.sin(twist),
-        jnp.cos(second).astype(jnp.bfloat16),
-        jnp.sin(second).astype(jnp.bfloat16),
-        jnp.cos(back).astype(jnp.bfloat16),
-        jnp.sin(back).astype(jnp.bfloat16),
-    )
-
-
-def forward(signal, cos_rows, sin_rows, tables):
-    cos_first, sin_first, cos_twist, sin_twist, cos_second, sin_second, cos_back, sin_back = tables
-    real_a = jnp.dot(cos_rows, signal, preferred_element_type=jnp.float32)
-    imag_a = -jnp.dot(sin_rows, signal, preferred_element_type=jnp.float32)
-    real_b = (real_a * cos_twist + imag_a * sin_twist).astype(jnp.bfloat16)
-    imag_b = (imag_a * cos_twist - real_a * sin_twist).astype(jnp.bfloat16)
-    real_x = jnp.dot(real_b, cos_second, preferred_element_type=jnp.float32) + jnp.dot(
-        imag_b, sin_second, preferred_element_type=jnp.float32
-    )
-    imag_x = jnp.dot(imag_b, cos_second, preferred_element_type=jnp.float32) - jnp.dot(
-        real_b, sin_second, preferred_element_type=jnp.float32
-    )
-    return (real_x, imag_x)
-
-
-def correlate(windowed, spectrum, weight2d, tables):
-    cos_first, sin_first, cos_twist, sin_twist, cos_second, sin_second, cos_back, sin_back = tables
-    rows_used = windowed.shape[0]
-    temp_real, temp_imag = forward(
-        windowed, cos_first[:, :rows_used], sin_first[:, :rows_used], tables
-    )
-    sigma = jnp.sum(weight2d * weight2d * (temp_real * temp_real + temp_imag * temp_imag))
-    data_real, data_imag = spectrum
-    q_real = (temp_real * data_real + temp_imag * data_imag).astype(jnp.bfloat16)
-    q_imag = (temp_real * data_imag - temp_imag * data_real).astype(jnp.bfloat16)
-    d_real = jnp.dot(q_real, cos_back, preferred_element_type=jnp.float32) - jnp.dot(
-        q_imag, sin_back, preferred_element_type=jnp.float32
-    )
-    d_imag = jnp.dot(q_real, sin_back, preferred_element_type=jnp.float32) + jnp.dot(
-        q_imag, cos_back, preferred_element_type=jnp.float32
-    )
-    e_real = (d_real * cos_twist - d_imag * sin_twist).astype(jnp.bfloat16)
-    e_imag = (d_real * sin_twist + d_imag * cos_twist).astype(jnp.bfloat16)
-    z_real = jnp.dot(cos_first, e_real, preferred_element_type=jnp.float32) - jnp.dot(
-        sin_first, e_imag, preferred_element_type=jnp.float32
-    )
-    z_imag = jnp.dot(sin_first, e_real, preferred_element_type=jnp.float32) + jnp.dot(
-        cos_first, e_imag, preferred_element_type=jnp.float32
-    )
-    return ((z_real * z_real + z_imag * z_imag) / (NFFT * sigma)).reshape(NFFT)
-
-
-def data_spectrum(strain_row, weight_row, tables):
-    weight2d = weight_row.reshape(N2 // 2, N1).T
-    signal = strain_row.astype(jnp.bfloat16).reshape(N1, N2)
-    real_s, imag_s = forward(signal, tables[0], tables[1], tables)
-    return ((weight2d * real_s, weight2d * imag_s), weight2d)
+        cos_second,
+        sin_second,
+    )
 
 
 def compact(rows, valid, wanted):
@@ -169,43 +118,62 @@
     return out.reshape(width)
 
 
+def dot_nt(left, right):
+    return lax.dot_general(
+        left, right, (((1,), (1,)), ((), ())), preferred_element_type=jnp.float32
+    )
+
+
 def filter_kernel(
-    rem_ref, x_ref, cfn_ref, sfn_ref, ct_ref, st_ref, cs_ref, ss_ref, cb_ref, sb_ref,
-    cf_ref, sf_ref, cfr_ref, sfr_ref, pr_ref, pi_ref, w2_ref, out_ref, er_ref, ei_ref,
+    scalar_ref, x_ref, cfn_ref, sfn_ref, ct_ref, st_ref, cs_ref, ss_ref, cf_ref, sf_ref,
+    cfr_ref, sfr_ref, sown_ref, soth_ref, wown_ref, woth_ref, out_ref,
+    er_ref, ei_ref, pr_ref, pi_ref, w2_ref,
 ):
     f32 = jnp.float32
     bf16 = jnp.bfloat16
-    x = x_ref[0]
-    cos_twist = ct_ref[...]
-    sin_twist = st_ref[...]
-    real_a = jnp.dot(cfn_ref[...], x, preferred_element_type=f32)
-    imag_a = -jnp.dot(sfn_ref[...], x, preferred_element_type=f32)
-    real_b = (real_a * cos_twist + imag_a * sin_twist).astype(bf16)
-    imag_b = (imag_a * cos_twist - real_a * sin_twist).astype(bf16)
-    cos_second = cs_ref[...]
-    sin_second = ss_ref[...]
-    temp_real = jnp.dot(real_b, cos_second, preferred_element_type=f32) + jnp.dot(
-        imag_b, sin_second, preferred_element_type=f32
-    )
-    temp_imag = jnp.dot(imag_b, cos_second, preferred_element_type=f32) - jnp.dot(
-        real_b, sin_second, preferred_element_type=f32
-    )
+
+    def first_stage(cos_rows, sin_rows, x):
+        cos_twist = ct_ref[...]
+        sin_twist = st_ref[...]
+        real_a = jnp.dot(cos_rows, x, preferred_element_type=f32)
+        imag_a = -jnp.dot(sin_rows, x, preferred_element_type=f32)
+        real_b = (real_a * cos_twist + imag_a * sin_twist).astype(bf16)
+        imag_b = (imag_a * cos_twist - real_a * sin_twist).astype(bf16)
+        cos_second = cs_ref[...]
+        sin_second = ss_ref[...]
+        real_x = jnp.dot(real_b, cos_second, preferred_element_type=f32) + jnp.dot(
+            imag_b, sin_second, preferred_element_type=f32
+        )
+        imag_x = jnp.dot(imag_b, cos_second, preferred_element_type=f32) - jnp.dot(
+            real_b, sin_second, preferred_element_type=f32
+        )
+        return real_x, imag_x
+
+    @pl.when(pl.program_id(0) == 0)
+    def _():
+        det = scalar_ref[1]
+        for slot, sig_ref, w_ref in ((det, sown_ref, wown_ref), (1 - det, soth_ref, woth_ref)):
+            real_s, imag_s = first_stage(cf_ref[...], sf_ref[...], sig_ref[...])
+            weight = jnp.transpose(w_ref[...])
+            pr_ref[slot] = weight * real_s
+            pi_ref[slot] = weight * imag_s
+            w2_ref[slot] = weight * weight
+
+    temp_real, temp_imag = first_stage(cfn_ref[...], sfn_ref[...], x_ref[0])
     power = temp_real * temp_real + temp_imag * temp_imag
-    cos_back = cb_ref[...]
-    sin_back = sb_ref[...]
+    cos_back = cs_ref[...]
+    sin_back = ss_ref[...]
 
     def back_half(d):
+        cos_twist = ct_ref[...]
+        sin_twist = st_ref[...]
         sigma = jnp.sum(w2_ref[d] * power, axis=(0, 1), keepdims=True)
         data_real = pr_ref[d]
         data_imag = pi_ref[d]
         q_real = (temp_real * data_real + temp_imag * data_imag).astype(bf16)
         q_imag = (temp_real * data_imag - temp_imag * data_real).astype(bf16)
-        d_real = jnp.dot(q_real, cos_back, preferred_element_type=f32) - jnp.dot(
-            q_imag, sin_back, preferred_element_type=f32
-        )
-        d_imag = jnp.dot(q_real, sin_back, preferred_element_type=f32) + jnp.dot(
-            q_imag, cos_back, preferred_element_type=f32
-        )
+        d_real = dot_nt(q_real, cos_back) - dot_nt(q_imag, sin_back)
+        d_imag = dot_nt(q_real, sin_back) + dot_nt(q_imag, cos_back)
         e_real = (d_real * cos_twist - d_imag * sin_twist).astype(bf16)
         e_imag = (d_real * sin_twist + d_imag * cos_twist).astype(bf16)
         return sigma, e_real, e_imag
@@ -223,7 +191,7 @@
     sigma1, e_real, e_imag = back_half(1)
     er_ref[...] = e_real
     ei_ref[...] = e_imag
-    rem = rem_ref[0]
+    rem = scalar_ref[0]
     tiles = first.shape[1] // BLK
     for col in range(tiles):
         src = lax.rem(col + rem, tiles)
@@ -244,8 +212,8 @@
         out_ref[0, :, col:col + 1] = jnp.max(network, axis=1, keepdims=True)
 
 
-def filter_bank(windowed, tables, spectra, weights, shift):
-    cos_first, sin_first, cos_twist, sin_twist, cos_second, sin_second, cos_back, sin_back = tables
+def filter_bank(windowed, tables, signals, weights, shift, det):
+    cos_first, sin_first, cos_twist, sin_twist, cos_second, sin_second = tables
     count, rows_used, width = windowed.shape
     pad_rows = 128
     x = jnp.concatenate(
@@ -253,20 +221,19 @@
     )
     tiles = N2 // BLK
     quot = shift // tiles
-    rem = lax.rem(shift, tiles).reshape(1)
+    scalars = jnp.stack([lax.rem(shift, tiles), det]).astype(jnp.int32)
+    doubled_cos = jnp.concatenate([cos_first, cos_first], axis=0)
+    doubled_sin = jnp.concatenate([sin_first, sin_first], axis=0)
     cos_rolled = jnp.stack(
-        [jnp.roll(cos_first, -quot, axis=0), jnp.roll(cos_first, -(quot + 1), axis=0)]
+        [lax.dynamic_slice_in_dim(doubled_cos, quot + v, N1) for v in range(2)]
     )
     sin_rolled = jnp.stack(
-        [jnp.roll(sin_first, -quot, axis=0), jnp.roll(sin_first, -(quot + 1), axis=0)]
-    )
-    data_real = jnp.stack([spectra[0][0], spectra[1][0]])
-    data_imag = jnp.stack([spectra[0][1], spectra[1][1]])
-    weight2 = jnp.stack([weights[0] * weights[0], weights[1] * weights[1]])
+        [lax.dynamic_slice_in_dim(doubled_sin, quot + v, N1) for v in range(2)]
+    )
     operands = [
         cos_first[:, :pad_rows], sin_first[:, :pad_rows], cos_twist, sin_twist,
-        cos_second, sin_second, cos_back, sin_back, cos_first, sin_first,
-        cos_rolled, sin_rolled, data_real, data_imag, weight2,
+        cos_second, sin_second, cos_first, sin_first, cos_rolled, sin_rolled,
+        signals[0], signals[1], weights[0], weights[1],
     ]
 
     def whole(array):
@@ -279,7 +246,13 @@
         in_specs=[pl.BlockSpec((1, pad_rows, width), lambda i, r: (i, 0, 0))]
         + [whole(a) for a in operands],
         out_specs=pl.BlockSpec((1, N1, tiles), lambda i, r: (i, 0, 0)),
-        scratch_shapes=[pltpu.VMEM((N1, N2), jnp.bfloat16), pltpu.VMEM((N1, N2), jnp.bfloat16)],
+        scratch_shapes=[
+            pltpu.VMEM((N1, N2), jnp.bfloat16),
+            pltpu.VMEM((N1, N2), jnp.bfloat16),
+            pltpu.VMEM((2, N1, N2 // 2), jnp.float32),
+            pltpu.VMEM((2, N1, N2 // 2), jnp.float32),
+            pltpu.VMEM((2, N1, N2 // 2), jnp.float32),
+        ],
     )
     matmuls = 2 * N1 * pad_rows * N2 + 4 * N1 * N2 * (N2 // 2) + 16 * N1 * (N2 // 2) * N2
     out = pl.pallas_call(
@@ -290,7 +263,7 @@
         cost_estimate=pl.CostEstimate(
             flops=2 * matmuls * count, transcendentals=0, bytes_accessed=8 * 1024 * 1024
         ),
-    )(rem, x, *operands)
+    )(scalars, x, *operands)
     return out.reshape(count, N1 * tiles)
 
 
@@ -323,14 +296,18 @@
     wanted = detector * mine + jnp.arange(mine, dtype=jnp.int32)
     my_rows = compact(recv_rows[:, :TL], valid, wanted)
     windowed = my_rows.reshape(mine, TL // N2, N2)
-    strain_both = lax.all_gather(strain[0].astype(jnp.bfloat16), "det")
-    asd_both = lax.all_gather(inv_asd[0], "det")
-    spec_0, weight_0 = data_spectrum(strain_both[0], asd_both[0], tables)
-    spec_1, weight_1 = data_spectrum(strain_both[1], asd_both[1], tables)
-    full = filter_bank(windowed, tables, (spec_0, spec_1), (weight_0, weight_1), slide[0])
+    swap = [(0, 1), (1, 0)]
+    own_signal = strain[0].astype(jnp.bfloat16).reshape(N1, N2)
+    own_weight = inv_asd[0].reshape(N2 // 2, N1)
+    other_signal = lax.ppermute(own_signal, "det", swap)
+    other_weight = lax.ppermute(own_weight, "det", swap)
+    full = filter_bank(
+        windowed, tables, (own_signal, other_signal), (own_weight, other_weight),
+        slide[0], detector,
+    )
     keep = lax.dynamic_slice_in_dim(full, detector * half_blk, half_blk, axis=1)
     give = lax.dynamic_slice_in_dim(full, (1 - detector) * half_blk, half_blk, axis=1)
-    got = lax.ppermute(give, "det", [(0, 1), (1, 0)])
+    got = lax.ppermute(give, "det", swap)
     peaks = jnp.where(
         detector == 0, jnp.concatenate([keep, got], axis=0), jnp.concatenate([got, keep], axis=0)
     )

time: 118 us -> 85.4 us (0.72)
  matrix products: 14 us -> 1.37 us
  local copies, waits for them, and re-layouts: 25 us -> 13 us
  other arithmetic: 17.8 us -> 12.6 us
  blocking collectives: 4.91 us -> 0 us
  waiting for transfers between devices: 1.04 us -> 2.66 us
    dot_general x12 -> x0, matrix products: 12.5 us -> none  [the longest x2 3.44 us: forward(): real_a = jnp.dot(cos_rows, signal, preferred_element_type=jnp.float32)]
    slice x2, local copies, waits for them, and re-layouts: 5.71 us -> 0.78 us  [the longest x1 0.39 us: make_tables(): cos_second[0::2]]
    all_gather x2 -> x0, blocking collectives: 4.91 us -> none  [the longest x1 2.56 us: shards(): strain_both = lax.all_gather(strain[0].astype(jnp.bfloat16), 'det')]
    another operation x8 -> x3, local copies, waits for them, and re-layouts: 4.82 us -> 0.22 us  [the longest x1 0.07 us: shards(): own_weight = inv_asd[0].reshape(N2 // 2, N1)]
    another operation x7 -> x4, other arithmetic: 5.16 us -> 0.89 us  [the longest x1 0.73 us: filter_bank(): jnp.stack([lax.dynamic_slice_in_dim(doubled_cos, quot + v, N1) for v in r...]
    unnamed x49 -> x26, local copies, waits for them, and re-layouts: 13.5 us -> 10.8 us
    convert_element_type x3 -> x2, other arithmetic: 6.13 us -> 3.56 us  [the longest x1 2.17 us: make_tables(): sin_second = jnp.sin(second).astype(jnp.bfloat16)]
    pallas_call x1, Pallas kernels: 17.2 us -> 18.8 us  [filter_bank(): pl.pallas_call(filter_kernel, out_shape=jax.ShapeDtypeStruct((count, N1,...]
  transfers between devices with their start and end apart: 2 -> 4, of which waited for: 1 -> 2; matrix products, arithmetic and copies ran while one was open for 33% -> 19% of each run, Pallas kernels for 0% -> 0%
where the time goes in v4:
time: 85.4 us; the launch traced here: 84.5 us
  Pallas kernels  40.9 us (48%)
  local copies, waits for them, and re-layouts  13 us (15%)
  other arithmetic  12.6 us (15%)
  starting transfers between devices  12.5 us (15%)
  waiting for transfers between devices  2.66 us (3%)
  between operations  1.6 us (2%)
  matrix products  1.37 us (2%)
    pallas_call x1, Pallas kernels, group_max(): pl.pallas_call(functools.partial(loudest_kernel, n_grp, n_filt), out_shap...  22.1 us
    pallas_call x1, Pallas kernels, filter_bank(): pl.pallas_call(filter_kernel, out_shape=jax.ShapeDtypeStruct((count, N1,...  18.8 us
    all_to_all x1, starting transfers between devices, shards(): lax.all_to_all(send_rows, 'filt', split_axis=0, concat_axis=0, tiled=True)  11.5 us
    unnamed x26, local copies, waits for them, and re-layouts  10.8 us
    convert_element_type x1, other arithmetic, make_tables(): sin_second = jnp.sin(second).astype(jnp.bfloat16)  2.17 us
    sin x1, other arithmetic, make_tables(): jnp.sin(twist)  2.05 us
  transfers between devices with their start and end apart: 4, of which 2 were waited for; matrix products, arithmetic and copies ran while one was open for 19% of the time, Pallas kernels for 0%

profile of v4, /device:TPU:32, one launch (start us, length us, event | category | flops | bytes accessed | tf_op | source)
XLA Modules:
  0.0 84.5 jit_solution(15238784588401719813)
XLA Ops:
  1.5 1.0 %fusion.16 = bf16[12,4096]{1,0:T(8,128)(2,1)S(1)} fusion(bf16[12,4096]{1,0:T(8,128)(2,1)} %param.8, s32[12]{0:T(128)S(1)} %broadcast_multiply_fusion), kind=kLoop, calls=%fused_computation.31 | loop fusion | flops 98304 | bytes 196656 | tf_op jit(solution)/shard_map/jit(_where)/select_n | solution.py:287
  3.2 0.8 reduce.10
  4.0 0.9 %reshape.75 = bf16[32,2,2112]{2,1,0:T(2,128)(2,1)} reshape(bf16[32,4224]{1,0:T(8,128)(2,1)S(1)} %reduce.10) | data formatting | bytes 540672
  4.9 11.5 %all-to-all-start = ((bf16[32,2,2112]{2,1,0:T(2,128)(2,1)}), bf16[32,2,2112]{2,1,0:T(2,128)(2,1)}, u32[]{:S(2)}, u32[]{:S(2)}) async-start(bf16[32,2,2112]{2,1,0:T(2,128)(2,1)} %reshape.75), calls=%async_computation | async-start | bytes 557056 | tf_op jit(solution)/shard_map/all_to_all | solution.py:294
  17.0 1.3 %reduce.9 = f32[65536]{0:T(1024)S(1)} reduce(f32[1,65536]{1,0:T(1,128)S(1)} %copy-done.6, f32[]{:T(128)} %broadcast.67), dimensions={0}, to_apply=%param.7.reduce_sub_computation.3 | reduce | bytes 524292 | tf_op args[1]
  18.5 1.4 %convert_reduce_fusion = bf16[131072]{0:T(1024)(128)(2,1)S(1)} fusion(f32[1,131072]{1,0:T(1,128)S(1)} %copy-done.5), kind=kLoop, calls=%fused_computation.15 | loop fusion | flops 131072 | bytes 786432 | tf_op jit(solution)/shard_map/convert_element_type | solution.py:300
  20.1 0.8 collective-permute-start
  20.8 2.2 %sine_convert_fusion = (bf16[512,256]{1,0:T(8,128)(2,1)S(1)}, bf16[512,256]{1,0:T(8,128)(2,1)S(1)}) fusion(), kind=kLoop, calls=%fused_computation.18 | loop fusion | flops 2097152 | bytes 524288 | tf_op jit(solution)/shard_map/convert_element_type | solution.py:36
  23.0 2.1 %fusion.14 = (f32[256,512]{1,0:T(8,128)S(1)}, f32[256,512]{1,0:T(8,128)S(1)}) fusion(), kind=kLoop, calls=%fused_computation.28 | loop fusion | flops 1835008 | bytes 1048576 | tf_op jit(solution)/shard_map/sin | solution.py:41
  26.9 0.7 pad_maximum_fusion.cfr_ref
  27.6 1.5 %all-to-all-done = bf16[32,2,2112]{2,1,0:T(2,128)(2,1)} async-done(((bf16[32,2,2112]{2,1,0:T(2,128)(2,1)}), bf16[32,2,2112]{2,1,0:T(2,128)(2,1)}, u32[]{:S(2)}, u32[]{:S(2)}) %all-to-all-start) | async-done | bytes 270368 | tf_op jit(solution)/shard_map/all_to_all | solution.py:294
  29.1 3.0 %reshape.76 = bf16[32,1,4224]{2,1,0:T(2,128)(2,1)} reshape(bf16[32,2,2112]{2,1,0:T(2,128)(2,1)} %all-to-all-done) | data formatting | bytes 540672
  32.1 1.8 %copy.15 = bf16[32,1,4224]{2,0,1:T(8,128)(2,1)} copy(bf16[32,1,4224]{2,1,0:T(2,128)(2,1)} %reshape.76) | data formatting | bytes 540672
  33.9 0.8 fusion.26
  34.8 1.2 %convolution_convert_fusion.1 = bf16[6,4096]{1,0:T(8,128)(2,1)S(1)} fusion(bf16[32,4224]{1,0:T(8,128)(2,1)} %bitcast.20, s32[32]{0:T(128)S(1)} %add_reduce_fusion, s32[6]{0:T(128)S(1)} %iota_add_fusion, pred[32]{0:T(512)(128)(4,1)S(1)} %get-tuple-element.16), kind=kOutput, calls=%fused_computation.2 | convolution fusion | flops 1597824 | bytes 311480 | tf_op jit(solution)/shard_map/dot_general | solution.py:50
  36.1 0.7 copy-done.1
  36.8 0.7 copy-done.3
  37.5 0.9 %copy-done.2 = f32[256,256]{1,0:T(8,128)S(1)} copy-done((f32[256,256]{1,0:T(8,128)S(1)}, f32[256,256]{1,0:T(8,128)}, u32[]{:S(2)}) %copy-start.2) | copy-done | bytes 262168
  38.5 0.9 %copy-done.4 = bf16[256,512]{1,0:T(8,128)(2,1)S(1)} copy-done((bf16[256,512]{1,0:T(8,128)(2,1)S(1)}, bf16[256,512]{1,0:T(8,128)(2,1)}, u32[]{:S(2)}) %copy-start.4) | copy-done | bytes 262168
  39.4 18.8 %shard_map.77 = f32[6,256,4]{2,1,0:T(8,128)S(1)} custom-call(s32[2]{0:T(128)S(1)} %pad_add_fusion.scalar_ref, bf16[6,128,512]{2,1,0:T(8,128)(2,1)S(1)} %concatenate.19.x_ref, bf16[256,128]{1,0:T(8,128)(2,1)S(1)} %slice.22.cfn_ref, bf16[256,128]{1,0:T(8,128)(2,1)S(1)} %slice.23.sfn_ref, f32[256,512]{1,0:T(8,128)S(1)} %get-tuple-element.10.ct_ref, ...), custom_call_target="tpu_custom_call" | custom-call | flops 8455716864 | bytes 8388608 | tf_op jit(solution)/shard_map/pallas_call | solution.py:258
  58.7 1.2 %collective-permute-done.2 = f32[6,512]{1,0:T(8,128)S(1)} collective-permute-done((f32[6,512]{1,0:T(8,128)S(1)}, f32[6,512]{1,0:T(8,128)S(1)}, u32[]{:S(2)}, u32[]{:S(2)}) %collective-permute-start.2) | collective-permute-done | bytes 12320 | tf_op jit(solution)/shard_map/ppermute | solution.py:310
  59.9 1.2 %fusion.28 = (f32[512]{0:T(512)}, f32[12,512]{1,0:T(8,128)}) fusion(f32[6,512]{1,0:T(8,128)S(1)} %get-tuple-element.23, f32[6,512]{1,0:T(8,128)S(1)} %collective-permute-done.2, pred[]{:T(512)S(6)} %eq.24), kind=kLoop, calls=%fused_computation.63 | loop fusion | flops 24064 | bytes 51201 | tf_op jit(solution)/shard_map/reduce_max | solution.py:314
  61.1 22.1 %shard_map.78 = f32[1,512]{1,0:T(1,128)} custom-call(f32[1,512]{1,0:T(1,128)} %bitcast.28), custom_call_target="tpu_custom_call" | custom-call | tf_op jit(solution)/shard_map/pallas_call | solution.py:106
  83.3 0.7 copy-done.7
  (45 shorter events, 4.9 us)
Async XLA Ops:
  0.6 0.7 copy-start.8
  4.9 12.1 %copy-start.6 = (f32[1,65536]{1,0:T(1,128)S(1)}, f32[1,65536]{1,0:T(1,128)}, u32[]{:S(2)}) copy-start(f32[1,65536]{1,0:T(1,128)} %param.7) | copy-start | bytes 786436
  4.9 24.2 %all-to-all-start = ((bf16[32,2,2112]{2,1,0:T(2,128)(2,1)}), bf16[32,2,2112]{2,1,0:T(2,128)(2,1)}, u32[]{:S(2)}, u32[]{:S(2)}) async-start(bf16[32,2,2112]{2,1,0:T(2,128)(2,1)} %reshape.75), calls=%async_computation | async-start | bytes 557056 | tf_op jit(solution)/shard_map/all_to_all | solution.py:294
  17.0 1.5 %copy-start.5 = (f32[1,131072]{1,0:T(1,128)S(1)}, f32[1,131072]{1,0:T(1,128)}, u32[]{:S(2)}) copy-start(f32[1,131072]{1,0:T(1,128)} %param.6) | copy-start | bytes 1572868
  18.4 17.7 %collective-permute-start.1 = (f32[256,256]{1,0:T(8,128)S(1)}, f32[256,256]{1,0:T(8,128)S(1)}, u32[]{:S(2)}, u32[]{:S(2)}) collective-permute-start(f32[256,256]{1,0:T(8,128)S(1)} %reshape_squeeze.3.wown_ref), channel_id=1, source_target_pairs={{0,128},{128,0},{1,129},{129,1},{2,130},{130,2},{3,131},{131,3},{4... | collective-permute-start | bytes 786440 | tf_op jit(solution)/shard_map/ppermute | solution.py:303
  20.1 16.8 %collective-permute-start = (bf16[256,512]{1,0:T(8,128)(2,1)S(1)}, bf16[256,512]{1,0:T(8,128)(2,1)S(1)}, u32[]{:S(2)}, u32[]{:S(2)}) collective-permute-start(bf16[256,512]{1,0:T(8,128)(2,1)S(1)} %convert_element_type.55.sown_ref), channel_id=1, source_target_pairs={{0,128},{128,0},{1,129},{129,1},{2,130},{130,2},{3,131},{131,3},{4... | collective-permute-start | bytes 786440 | tf_op jit(solution)/shard_map/ppermute | solution.py:302
  36.0 1.5 %copy-start = (bf16[2,256,256]{2,1,0:T(8,128)(2,1)S(1)}, bf16[2,256,256]{2,1,0:T(8,128)(2,1)}, u32[]{:S(2)}) copy-start(bf16[2,256,256]{2,1,0:T(8,128)(2,1)} %pad_maximum_fusion.cfr_ref) | copy-start | bytes 786436
  36.1 0.7 copy-start.1
  36.8 0.7 copy-start.3
  37.5 1.0 %copy-start.2 = (f32[256,256]{1,0:T(8,128)S(1)}, f32[256,256]{1,0:T(8,128)}, u32[]{:S(2)}) copy-start(f32[256,256]{1,0:T(8,128)} %copy-done.1) | copy-start | bytes 786436
  38.5 0.9 %copy-start.4 = (bf16[256,512]{1,0:T(8,128)(2,1)S(1)}, bf16[256,512]{1,0:T(8,128)(2,1)}, u32[]{:S(2)}) copy-start(bf16[256,512]{1,0:T(8,128)(2,1)} %copy-done.3) | copy-start | bytes 786436
  58.6 1.3 %collective-permute-start.2 = (f32[6,512]{1,0:T(8,128)S(1)}, f32[6,512]{1,0:T(8,128)S(1)}, u32[]{:S(2)}, u32[]{:S(2)}) collective-permute-start(f32[6,512]{1,0:T(8,128)S(1)} %get-tuple-element.22), channel_id=1, source_target_pairs={{0,128},{128,0},{1,129},{129,1},{2,130},{130,2},{3,131},{131,3},{4... | collective-permute-start | bytes 36872 | tf_op jit(solution)/shard_map/ppermute | solution.py:310
  83.3 0.7 copy-start.7

commit v5 on v4

--- a/solution.py
+++ b/solution.py
@@ -52,67 +52,84 @@
     )
 
 
-def loudest_kernel(n_grp, n_filt, local_ref, out_ref, held, send_sems, recv_sems):
+def stage_layout(n_grp, n_filt):
+    inner = 8 if n_filt % 8 == 0 else n_filt
+    return ((inner, 1), (n_filt // inner, inner), (n_grp, 0))
+
+
+def loudest_kernel(stages, local_ref, out_ref, acc_ref, *scratch):
     det = lax.axis_index("det")
-    size = n_grp * n_filt
-    me = lax.axis_index("grp") * n_filt + lax.axis_index("filt")
+    grp = lax.axis_index("grp")
+    filt = lax.axis_index("filt")
     mesh_ids = pl.DeviceIdType.MESH
 
-    def peer_of(i):
-        peer = lax.rem(me + 1 + i, size)
-        return (det, peer // n_filt, lax.rem(peer, n_filt))
-
-    def copy_to(i):
-        row = size - 2 - i
-        return pltpu.make_async_remote_copy(
-            src_ref=local_ref,
-            dst_ref=held.at[row],
-            send_sem=send_sems.at[i],
-            recv_sem=recv_sems.at[row],
-            device_id=peer_of(i),
-            device_id_type=mesh_ids,
-        )
-
+    def position(size, stride):
+        if stride == 0:
+            return grp
+        return lax.rem(filt // stride, size)
+
+    def peer(size, stride, target):
+        if stride == 0:
+            return (det, target, filt)
+        here = position(size, stride)
+        return (det, grp, filt + (target - here) * stride)
+
+    live = [(size, stride) for size, stride in stages if size > 1]
     barrier = pltpu.get_barrier_semaphore()
-
-    def greet(i, carry):
-        pl.semaphore_signal(barrier, inc=1, device_id=peer_of(i), device_id_type=mesh_ids)
-        return carry
-
-    lax.fori_loop(0, size - 1, greet, 0)
-    pl.semaphore_wait(barrier, size - 1)
-
-    def send(i, carry):
-        copy_to(i).start()
-        return carry
-
-    lax.fori_loop(0, size - 1, send, 0)
-
-    def finish(i, carry):
-        copy = copy_to(i)
-        copy.wait_send()
-        copy.wait_recv()
-        return carry
-
-    lax.fori_loop(0, size - 1, finish, 0)
-    out_ref[...] = jnp.maximum(local_ref[...], jnp.max(held[...], axis=0))
+    for size, stride in live:
+        here = position(size, stride)
+        for i in range(size - 1):
+            target = lax.rem(here + 1 + i, size)
+            pl.semaphore_signal(
+                barrier, inc=1, device_id=peer(size, stride, target), device_id_type=mesh_ids
+            )
+    pl.semaphore_wait(barrier, sum(size - 1 for size, _ in live))
+    value = local_ref[...]
+    source = local_ref
+    for k, (size, stride) in enumerate(live):
+        held, send_sems, recv_sems = scratch[3 * k:3 * k + 3]
+        here = position(size, stride)
+        copies = []
+        for i in range(size - 1):
+            target = lax.rem(here + 1 + i, size)
+            row = size - 2 - i
+            copy = pltpu.make_async_remote_copy(
+                src_ref=source,
+                dst_ref=held.at[row],
+                send_sem=send_sems.at[i],
+                recv_sem=recv_sems.at[row],
+                device_id=peer(size, stride, target),
+                device_id_type=mesh_ids,
+            )
+            copy.start()
+            copies.append(copy)
+        for copy in copies:
+            copy.wait_send()
+            copy.wait_recv()
+        value = jnp.maximum(value, jnp.max(held[...], axis=0))
+        if k + 1 < len(live):
+            acc_ref[k] = value
+            source = acc_ref.at[k]
+    out_ref[...] = value
 
 
 def group_max(local_max):
-    n_grp = lax.axis_size("grp")
-    n_filt = lax.axis_size("filt")
-    size = n_grp * n_filt
+    stages = stage_layout(lax.axis_size("grp"), lax.axis_size("filt"))
+    live = [size for size, _ in stages if size > 1]
     width = local_max.shape[-1]
+    scratch = [pltpu.VMEM((max(len(live), 1), 1, width), jnp.float32)]
+    for size in live:
+        scratch += [
+            pltpu.VMEM((size - 1, 1, width), jnp.float32),
+            pltpu.SemaphoreType.DMA((size - 1,)),
+            pltpu.SemaphoreType.DMA((size - 1,)),
+        ]
     out = pl.pallas_call(
-        functools.partial(loudest_kernel, n_grp, n_filt),
+        functools.partial(loudest_kernel, stages),
         out_shape=jax.ShapeDtypeStruct((1, width), jnp.float32),
         in_specs=[pl.BlockSpec(memory_space=pltpu.VMEM)],
         out_specs=pl.BlockSpec(memory_space=pltpu.VMEM),
-        scratch_shapes=[
-            pltpu.VMEM((size - 1, 1, width), jnp.float32),
-            pltpu.SemaphoreType.DMA((size - 1,)),
-            pltpu.SemaphoreType.DMA((size - 1,)),
-        ],
+        scratch_shapes=scratch,
         compiler_params=pltpu.CompilerParams(collective_id=0, has_side_effects=True),
     )(local_max.reshape(1, width))
     return out.reshape(width)

time: 85.4 us -> 80.2 us (0.939)
  Pallas kernels: 40.9 us -> 35.6 us
    pallas_call x1, Pallas kernels: 22.1 us -> 16.8 us  [group_max(): pl.pallas_call(functools.partial(loudest_kernel, stages), out_shape=jax.S...]
  transfers between devices with their start and end apart: 4 -> 4, of which waited for: 2 -> 2; matrix products, arithmetic and copies ran while one was open for 19% -> 21% of each run, Pallas kernels for 0% -> 0%
where the time goes in v5:
time: 80.2 us; the launch traced here: 79.2 us
  Pallas kernels  35.6 us (44%)
  local copies, waits for them, and re-layouts  13 us (16%)
  other arithmetic  12.6 us (16%)
  starting transfers between devices  12.5 us (16%)
  waiting for transfers between devices  2.66 us (3%)
  between operations  1.59 us (2%)
  matrix products  1.37 us (2%)
    pallas_call x1, Pallas kernels, filter_bank(): pl.pallas_call(filter_kernel, out_shape=jax.ShapeDtypeStruct((count, N1,...  18.8 us
    pallas_call x1, Pallas kernels, group_max(): pl.pallas_call(functools.partial(loudest_kernel, stages), out_shape=jax.S...  16.8 us
    all_to_all x1, starting transfers between devices, shards(): lax.all_to_all(send_rows, 'filt', split_axis=0, concat_axis=0, tiled=True)  11.5 us
    unnamed x26, local copies, waits for them, and re-layouts  10.8 us
    convert_element_type x1, other arithmetic, make_tables(): sin_second = jnp.sin(second).astype(jnp.bfloat16)  2.17 us
    sin x1, other arithmetic, make_tables(): jnp.sin(twist)  2.05 us
  transfers between devices with their start and end apart: 4, of which 2 were waited for; matrix products, arithmetic and copies ran while one was open for 21% of the time, Pallas kernels for 0%

profile of v5, /device:TPU:32, one launch (start us, length us, event | category | flops | bytes accessed | tf_op | source)
XLA Modules:
  0.0 79.2 jit_solution(15708069898354130660)
XLA Ops:
  1.5 1.0 %fusion.16 = bf16[12,4096]{1,0:T(8,128)(2,1)S(1)} fusion(bf16[12,4096]{1,0:T(8,128)(2,1)} %param.8, s32[12]{0:T(128)S(1)} %broadcast_multiply_fusion), kind=kLoop, calls=%fused_computation.31 | loop fusion | flops 98304 | bytes 196656 | tf_op jit(solution)/shard_map/jit(_where)/select_n | solution.py:304
  3.2 0.8 reduce.10
  4.0 0.9 %reshape.75 = bf16[32,2,2112]{2,1,0:T(2,128)(2,1)} reshape(bf16[32,4224]{1,0:T(8,128)(2,1)S(1)} %reduce.10) | data formatting | bytes 540672
  4.9 11.5 %all-to-all-start = ((bf16[32,2,2112]{2,1,0:T(2,128)(2,1)}), bf16[32,2,2112]{2,1,0:T(2,128)(2,1)}, u32[]{:S(2)}, u32[]{:S(2)}) async-start(bf16[32,2,2112]{2,1,0:T(2,128)(2,1)} %reshape.75), calls=%async_computation | async-start | bytes 557056 | tf_op jit(solution)/shard_map/all_to_all | solution.py:311
  17.0 1.3 %reduce.9 = f32[65536]{0:T(1024)S(1)} reduce(f32[1,65536]{1,0:T(1,128)S(1)} %copy-done.6, f32[]{:T(128)} %broadcast.67), dimensions={0}, to_apply=%param.7.reduce_sub_computation.3 | reduce | bytes 524292 | tf_op args[1]
  18.5 1.4 %convert_reduce_fusion = bf16[131072]{0:T(1024)(128)(2,1)S(1)} fusion(f32[1,131072]{1,0:T(1,128)S(1)} %copy-done.5), kind=kLoop, calls=%fused_computation.15 | loop fusion | flops 131072 | bytes 786432 | tf_op jit(solution)/shard_map/convert_element_type | solution.py:317
  20.1 0.8 collective-permute-start
  20.8 2.2 %sine_convert_fusion = (bf16[512,256]{1,0:T(8,128)(2,1)S(1)}, bf16[512,256]{1,0:T(8,128)(2,1)S(1)}) fusion(), kind=kLoop, calls=%fused_computation.18 | loop fusion | flops 2097152 | bytes 524288 | tf_op jit(solution)/shard_map/convert_element_type | solution.py:36
  23.0 2.1 %fusion.14 = (f32[256,512]{1,0:T(8,128)S(1)}, f32[256,512]{1,0:T(8,128)S(1)}) fusion(), kind=kLoop, calls=%fused_computation.28 | loop fusion | flops 1835008 | bytes 1048576 | tf_op jit(solution)/shard_map/sin | solution.py:41
  26.9 0.7 pad_maximum_fusion.cfr_ref
  27.6 1.5 %all-to-all-done = bf16[32,2,2112]{2,1,0:T(2,128)(2,1)} async-done(((bf16[32,2,2112]{2,1,0:T(2,128)(2,1)}), bf16[32,2,2112]{2,1,0:T(2,128)(2,1)}, u32[]{:S(2)}, u32[]{:S(2)}) %all-to-all-start) | async-done | bytes 270368 | tf_op jit(solution)/shard_map/all_to_all | solution.py:311
  29.1 3.0 %reshape.76 = bf16[32,1,4224]{2,1,0:T(2,128)(2,1)} reshape(bf16[32,2,2112]{2,1,0:T(2,128)(2,1)} %all-to-all-done) | data formatting | bytes 540672
  32.1 1.8 %copy.15 = bf16[32,1,4224]{2,0,1:T(8,128)(2,1)} copy(bf16[32,1,4224]{2,1,0:T(2,128)(2,1)} %reshape.76) | data formatting | bytes 540672
  33.9 0.8 %fusion.26 = (pred[32]{0:T(512)(128)(4,1)S(1)}, s32[32,1]{1,0:T(8,128)S(1)}) fusion(bf16[32,4224]{1,0:T(8,128)(2,1)} %bitcast.20), kind=kLoop, calls=%fused_computation.60 | loop fusion | flops 64 | bytes 224 | tf_op jit(solution)/shard_map/gt | solution.py:312
  34.8 1.2 %convolution_convert_fusion.1 = bf16[6,4096]{1,0:T(8,128)(2,1)S(1)} fusion(bf16[32,4224]{1,0:T(8,128)(2,1)} %bitcast.20, s32[32]{0:T(128)S(1)} %add_reduce_fusion, s32[6]{0:T(128)S(1)} %iota_add_fusion, pred[32]{0:T(512)(128)(4,1)S(1)} %get-tuple-element.16), kind=kOutput, calls=%fused_computation.2 | convolution fusion | flops 1597824 | bytes 311480 | tf_op jit(solution)/shard_map/dot_general | solution.py:50
  36.1 0.7 copy-done.1
  36.8 0.7 copy-done.3
  37.5 0.9 %copy-done.2 = f32[256,256]{1,0:T(8,128)S(1)} copy-done((f32[256,256]{1,0:T(8,128)S(1)}, f32[256,256]{1,0:T(8,128)}, u32[]{:S(2)}) %copy-start.2) | copy-done | bytes 262168
  38.5 0.9 %copy-done.4 = bf16[256,512]{1,0:T(8,128)(2,1)S(1)} copy-done((bf16[256,512]{1,0:T(8,128)(2,1)S(1)}, bf16[256,512]{1,0:T(8,128)(2,1)}, u32[]{:S(2)}) %copy-start.4) | copy-done | bytes 262168
  39.4 18.8 %shard_map.77 = f32[6,256,4]{2,1,0:T(8,128)S(1)} custom-call(s32[2]{0:T(128)S(1)} %pad_add_fusion.scalar_ref, bf16[6,128,512]{2,1,0:T(8,128)(2,1)S(1)} %concatenate.19.x_ref, bf16[256,128]{1,0:T(8,128)(2,1)S(1)} %slice.22.cfn_ref, bf16[256,128]{1,0:T(8,128)(2,1)S(1)} %slice.23.sfn_ref, f32[256,512]{1,0:T(8,128)S(1)} %get-tuple-element.10.ct_ref, ...), custom_call_target="tpu_custom_call" | custom-call | flops 8455716864 | bytes 8388608 | tf_op jit(solution)/shard_map/pallas_call | solution.py:275
  58.8 1.2 %collective-permute-done.2 = f32[6,512]{1,0:T(8,128)S(1)} collective-permute-done((f32[6,512]{1,0:T(8,128)S(1)}, f32[6,512]{1,0:T(8,128)S(1)}, u32[]{:S(2)}, u32[]{:S(2)}) %collective-permute-start.2) | collective-permute-done | bytes 12320 | tf_op jit(solution)/shard_map/ppermute | solution.py:327
  60.0 1.2 %fusion.28 = (f32[512]{0:T(512)}, f32[12,512]{1,0:T(8,128)}) fusion(f32[6,512]{1,0:T(8,128)S(1)} %get-tuple-element.23, f32[6,512]{1,0:T(8,128)S(1)} %collective-permute-done.2, pred[]{:T(512)S(6)} %eq.24), kind=kLoop, calls=%fused_computation.63 | loop fusion | flops 24064 | bytes 51201 | tf_op jit(solution)/shard_map/reduce_max | solution.py:331
  61.2 16.8 %shard_map.78 = f32[1,512]{1,0:T(1,128)} custom-call(f32[1,512]{1,0:T(1,128)} %bitcast.28), custom_call_target="tpu_custom_call" | custom-call | tf_op jit(solution)/shard_map/pallas_call | solution.py:127
  78.0 0.7 copy-done.7
  (45 shorter events, 4.9 us)
Async XLA Ops:
  0.6 0.7 copy-start.8
  4.9 12.1 %copy-start.6 = (f32[1,65536]{1,0:T(1,128)S(1)}, f32[1,65536]{1,0:T(1,128)}, u32[]{:S(2)}) copy-start(f32[1,65536]{1,0:T(1,128)} %param.7) | copy-start | bytes 786436
  4.9 24.2 %all-to-all-start = ((bf16[32,2,2112]{2,1,0:T(2,128)(2,1)}), bf16[32,2,2112]{2,1,0:T(2,128)(2,1)}, u32[]{:S(2)}, u32[]{:S(2)}) async-start(bf16[32,2,2112]{2,1,0:T(2,128)(2,1)} %reshape.75), calls=%async_computation | async-start | bytes 557056 | tf_op jit(solution)/shard_map/all_to_all | solution.py:311
  17.0 1.5 %copy-start.5 = (f32[1,131072]{1,0:T(1,128)S(1)}, f32[1,131072]{1,0:T(1,128)}, u32[]{:S(2)}) copy-start(f32[1,131072]{1,0:T(1,128)} %param.6) | copy-start | bytes 1572868
  18.4 17.7 %collective-permute-start.1 = (f32[256,256]{1,0:T(8,128)S(1)}, f32[256,256]{1,0:T(8,128)S(1)}, u32[]{:S(2)}, u32[]{:S(2)}) collective-permute-start(f32[256,256]{1,0:T(8,128)S(1)} %reshape_squeeze.3.wown_ref), channel_id=1, source_target_pairs={{0,128},{128,0},{1,129},{129,1},{2,130},{130,2},{3,131},{131,3},{4... | collective-permute-start | bytes 786440 | tf_op jit(solution)/shard_map/ppermute | solution.py:320
  20.1 16.8 %collective-permute-start = (bf16[256,512]{1,0:T(8,128)(2,1)S(1)}, bf16[256,512]{1,0:T(8,128)(2,1)S(1)}, u32[]{:S(2)}, u32[]{:S(2)}) collective-permute-start(bf16[256,512]{1,0:T(8,128)(2,1)S(1)} %convert_element_type.55.sown_ref), channel_id=1, source_target_pairs={{0,128},{128,0},{1,129},{129,1},{2,130},{130,2},{3,131},{131,3},{4... | collective-permute-start | bytes 786440 | tf_op jit(solution)/shard_map/ppermute | solution.py:319
  36.0 1.5 %copy-start = (bf16[2,256,256]{2,1,0:T(8,128)(2,1)S(1)}, bf16[2,256,256]{2,1,0:T(8,128)(2,1)}, u32[]{:S(2)}) copy-start(bf16[2,256,256]{2,1,0:T(8,128)(2,1)} %pad_maximum_fusion.cfr_ref) | copy-start | bytes 786436
  36.1 0.7 copy-start.1
  36.8 0.7 copy-start.3
  37.5 1.0 %copy-start.2 = (f32[256,256]{1,0:T(8,128)S(1)}, f32[256,256]{1,0:T(8,128)}, u32[]{:S(2)}) copy-start(f32[256,256]{1,0:T(8,128)} %copy-done.1) | copy-start | bytes 786436
  38.5 0.9 %copy-start.4 = (bf16[256,512]{1,0:T(8,128)(2,1)S(1)}, bf16[256,512]{1,0:T(8,128)(2,1)}, u32[]{:S(2)}) copy-start(bf16[256,512]{1,0:T(8,128)(2,1)} %copy-done.3) | copy-start | bytes 786436
  58.7 1.3 %collective-permute-start.2 = (f32[6,512]{1,0:T(8,128)S(1)}, f32[6,512]{1,0:T(8,128)S(1)}, u32[]{:S(2)}, u32[]{:S(2)}) collective-permute-start(f32[6,512]{1,0:T(8,128)S(1)} %get-tuple-element.22), channel_id=1, source_target_pairs={{0,128},{128,0},{1,129},{129,1},{2,130},{130,2},{3,131},{131,3},{4... | collective-permute-start | bytes 36872 | tf_op jit(solution)/shard_map/ppermute | solution.py:327
  78.0 0.7 copy-start.7

commit v6 on v5

--- a/solution.py
+++ b/solution.py
@@ -1,6 +1,8 @@
 import functools
 
 import jax
+import ml_dtypes
+import numpy as np
 import jax.numpy as jnp
 from jax import lax
 from jax.experimental import pallas as pl
@@ -24,23 +26,27 @@
 
 
 def angle_table(rows, cols, period):
-    left = jnp.arange(rows, dtype=jnp.int32)[:, None]
-    right = jnp.arange(cols, dtype=jnp.int32)[None, :]
-    return TWO_PI / period * (left * right % period).astype(jnp.float32)
+    left = np.arange(rows, dtype=np.int64)[:, None]
+    right = np.arange(cols, dtype=np.int64)[None, :]
+    turns = (left * right % period).astype(np.float32)
+    return np.float32(TWO_PI / period) * turns
 
 
 def make_tables():
-    twist = angle_table(N1, N2, NFFT)
-    second = angle_table(N2, N2 // 2, N2)
-    cos_second = jnp.cos(second).astype(jnp.bfloat16)
-    sin_second = jnp.sin(second).astype(jnp.bfloat16)
-    return (
-        cos_second[0::2],
-        sin_second[0::2],
-        jnp.cos(twist),
-        jnp.sin(twist),
-        cos_second,
-        sin_second,
+    twist = angle_table(N1, N2, NFFT).astype(np.float64)
+    second = angle_table(N2, N2 // 2, N2).astype(np.float64)
+    cos_second = np.cos(second).astype(np.float32).astype(ml_dtypes.bfloat16)
+    sin_second = np.sin(second).astype(np.float32).astype(ml_dtypes.bfloat16)
+    return tuple(
+        jnp.asarray(table)
+        for table in (
+            cos_second[0::2],
+            sin_second[0::2],
+            np.cos(twist).astype(np.float32),
+            np.sin(twist).astype(np.float32),
+            cos_second,
+            sin_second,
+        )
     )
 
 
@@ -285,7 +291,7 @@
 
 
 def shards(strain, inv_asd, templates, chirp_blocks, owner, slide):
-    tables = lax.optimization_barrier(make_tables())
+    tables = make_tables()
     detector = lax.axis_index("det")
     per_dev = templates.shape[0]
     mine = per_dev // 2

time: 80.2 us -> 71.4 us (0.89)
  local copies, waits for them, and re-layouts: 13 us -> 5.49 us
  waiting for transfers between devices: 2.66 us -> 8.61 us
  other arithmetic: 12.6 us -> 6.93 us
  matrix products: 1.37 us -> 0.41 us
    unnamed x26 -> x34, local copies, waits for them, and re-layouts: 10.8 us -> 4.12 us
    all_to_all x1, waiting for transfers between devices: 1.49 us -> 7.44 us  [shards(): lax.all_to_all(send_rows, 'filt', split_axis=0, concat_axis=0, tiled=True)]
    convert_element_type x1 -> x0, other arithmetic: 2.17 us -> none  [make_tables(): sin_second = jnp.sin(second).astype(jnp.bfloat16)]
    sin x1 -> x0, other arithmetic: 2.05 us -> none  [make_tables(): jnp.sin(twist)]
    dot_general x1, matrix products: 1.16 us -> 0.21 us  [compact(): jnp.dot(picker.astype(jnp.bfloat16), rows, preferred_element_type=jnp.flo...]
  transfers between devices with their start and end apart: 4 -> 4, of which waited for: 2 -> 2; matrix products, arithmetic and copies ran while one was open for 21% -> 6% of each run, Pallas kernels for 0% -> 0%
where the time goes in v6:
time: 71.4 us; the launch traced here: 71.1 us
  Pallas kernels  35.8 us (50%)
  starting transfers between devices  12.2 us (17%)
  waiting for transfers between devices  8.61 us (12%)
  other arithmetic  6.93 us (10%)
  local copies, waits for them, and re-layouts  5.49 us (8%)
  between operations  1.61 us (2%)
    pallas_call x1, Pallas kernels, filter_bank(): pl.pallas_call(filter_kernel, out_shape=jax.ShapeDtypeStruct((count, N1,...  19.2 us
    pallas_call x1, Pallas kernels, group_max(): pl.pallas_call(functools.partial(loudest_kernel, stages), out_shape=jax.S...  16.5 us
    all_to_all x1, starting transfers between devices, shards(): lax.all_to_all(send_rows, 'filt', split_axis=0, concat_axis=0, tiled=True)  11.5 us
    all_to_all x1, waiting for transfers between devices, shards(): lax.all_to_all(send_rows, 'filt', split_axis=0, concat_axis=0, tiled=True)  7.44 us
    unnamed x34, local copies, waits for them, and re-layouts  4.12 us
  transfers between devices with their start and end apart: 4, of which 2 were waited for; matrix products, arithmetic and copies ran while one was open for 6% of the time, Pallas kernels for 0%

profile of v6, /device:TPU:32, one launch (start us, length us, event | category | flops | bytes accessed | tf_op | source)
XLA Modules:
  0.0 71.1 jit_solution(18207199619084079237)
XLA Ops:
  0.6 0.7 broadcast_multiply_fusion
  1.5 1.0 %fusion.2 = bf16[12,4096]{1,0:T(8,128)(2,1)S(1)} fusion(bf16[12,4096]{1,0:T(8,128)(2,1)} %param.14, s32[12]{0:T(128)S(1)} %broadcast_multiply_fusion), kind=kLoop, calls=%fused_computation.9 | loop fusion | flops 98304 | bytes 196656 | tf_op jit(solution)/shard_map/jit(_where)/select_n | solution.py:310
  2.5 0.2 fusion
  2.7 0.5 broadcast.44
  3.2 0.8 %reduce.10 = bf16[32,4224]{1,0:T(8,128)(2,1)S(1)} reduce(bf16[32,1,4224]{2,0,1:T(8,128)(2,1)S(1)} %fusion, bf16[]{:T(256)} %broadcast.44), dimensions={1}, to_apply=%copy.16.reduce_sub_computation | reduce | bytes 540674 | tf_op jit(solution)/shard_map/all_to_all | solution.py:317
  4.0 0.9 %reshape.75 = bf16[32,2,2112]{2,1,0:T(2,128)(2,1)} reshape(bf16[32,4224]{1,0:T(8,128)(2,1)S(1)} %reduce.10) | data formatting | bytes 540672
  4.9 11.5 %all-to-all-start = ((bf16[32,2,2112]{2,1,0:T(2,128)(2,1)}), bf16[32,2,2112]{2,1,0:T(2,128)(2,1)S(1)}, u32[]{:S(2)}, u32[]{:S(2)}) async-start(bf16[32,2,2112]{2,1,0:T(2,128)(2,1)} %reshape.75), calls=%async_computation | async-start | bytes 557056 | tf_op jit(solution)/shard_map/all_to_all | solution.py:317
  16.4 0.5 broadcast.43
  16.9 1.3 %reduce.9 = f32[65536]{0:T(1024)S(1)} reduce(f32[1,65536]{1,0:T(1,128)S(1)} %copy-done.11, f32[]{:T(128)} %broadcast.43), dimensions={0}, to_apply=%param.13.reduce_sub_computation.3 | reduce | bytes 524292 | tf_op args[1]
  18.4 1.4 %convert_reduce_fusion = bf16[131072]{0:T(1024)(128)(2,1)S(1)} fusion(f32[1,131072]{1,0:T(1,128)S(1)} %copy-done.8), kind=kLoop, calls=%fused_computation.3 | loop fusion | flops 131072 | bytes 786432 | tf_op jit(solution)/shard_map/convert_element_type | solution.py:323
  20.0 0.6 collective-permute-start
  21.6 7.4 %all-to-all-done = bf16[32,2,2112]{2,1,0:T(2,128)(2,1)S(1)} async-done(((bf16[32,2,2112]{2,1,0:T(2,128)(2,1)}), bf16[32,2,2112]{2,1,0:T(2,128)(2,1)S(1)}, u32[]{:S(2)}, u32[]{:S(2)}) %all-to-all-start) | async-done | bytes 270368 | tf_op jit(solution)/shard_map/all_to_all | solution.py:317
  29.0 0.3 reshape.76
  29.7 0.2 convolution_convert_fusion.1
  30.1 0.2 copy-done.2
  30.4 0.4 copy-done.1
  30.8 0.3 copy-done
  31.1 19.2 %shard_map.131 = f32[6,256,4]{2,1,0:T(8,128)S(1)} custom-call(s32[2]{0:T(128)S(1)} %pad_add_fusion.scalar_ref, bf16[6,128,512]{2,1,0:T(8,128)(2,1)S(1)} %concatenate.19.x_ref, bf16[256,128]{1,0:T(8,128)(2,1)S(1)} %copy-done.6, bf16[256,128]{1,0:T(8,128)(2,1)S(1)} %copy-done.7, f32[256,512]{1,0:T(8,128)S(1)} %copy-done, f32[256,512]{1,0:T(8,128)S(1)} %copy-done.1, ...), custom_call_target="tpu_custom_call" | custom-call | flops 8455716864 | bytes 8388608 | tf_op jit(solution)/shard_map/pallas_call | solution.py:281
  50.3 0.4 reshape.60
  50.9 1.2 %collective-permute-done.2 = f32[6,512]{1,0:T(8,128)S(1)} collective-permute-done((f32[6,512]{1,0:T(8,128)S(1)}, f32[6,512]{1,0:T(8,128)S(1)}, u32[]{:S(2)}, u32[]{:S(2)}) %collective-permute-start.2) | collective-permute-done | bytes 12320 | tf_op jit(solution)/shard_map/ppermute | solution.py:333
  52.1 1.2 %fusion.14 = (f32[512]{0:T(512)}, f32[12,512]{1,0:T(8,128)}) fusion(f32[6,512]{1,0:T(8,128)S(1)} %get-tuple-element.11, f32[6,512]{1,0:T(8,128)S(1)} %collective-permute-done.2, pred[]{:T(512)S(6)} %eq.20), kind=kLoop, calls=%fused_computation.37 | loop fusion | flops 24064 | bytes 51201 | tf_op jit(solution)/shard_map/reduce_max | solution.py:337
  53.3 16.5 %shard_map.132 = f32[1,512]{1,0:T(1,128)} custom-call(f32[1,512]{1,0:T(1,128)} %bitcast.30), custom_call_target="tpu_custom_call" | custom-call | tf_op jit(solution)/shard_map/pallas_call | solution.py:133
  69.8 0.7 copy-done.12
  70.5 0.6 copy.26
  (44 shorter events, 1.5 us)
Async XLA Ops:
  0.6 0.7 copy-start.13
  4.9 12.0 %copy-start.11 = (f32[1,65536]{1,0:T(1,128)S(1)}, f32[1,65536]{1,0:T(1,128)}, u32[]{:S(2)}) copy-start(f32[1,65536]{1,0:T(1,128)} %param.13) | copy-start | bytes 786436
  4.9 24.1 %all-to-all-start = ((bf16[32,2,2112]{2,1,0:T(2,128)(2,1)}), bf16[32,2,2112]{2,1,0:T(2,128)(2,1)S(1)}, u32[]{:S(2)}, u32[]{:S(2)}) async-start(bf16[32,2,2112]{2,1,0:T(2,128)(2,1)} %reshape.75), calls=%async_computation | async-start | bytes 557056 | tf_op jit(solution)/shard_map/all_to_all | solution.py:317
  16.9 1.5 %copy-start.8 = (f32[1,131072]{1,0:T(1,128)S(1)}, f32[1,131072]{1,0:T(1,128)}, u32[]{:S(2)}) copy-start(f32[1,131072]{1,0:T(1,128)} %param.12) | copy-start | bytes 1572868
  18.3 11.7 %collective-permute-start.1 = (f32[256,256]{1,0:T(8,128)S(1)}, f32[256,256]{1,0:T(8,128)S(1)}, u32[]{:S(2)}, u32[]{:S(2)}) collective-permute-start(f32[256,256]{1,0:T(8,128)S(1)} %reshape_squeeze.3.wown_ref), channel_id=1, source_target_pairs={{0,128},{128,0},{1,129},{129,1},{2,130},{130,2},{3,131},{131,3},{4... | collective-permute-start | bytes 786440 | tf_op jit(solution)/shard_map/ppermute | solution.py:326
  19.8 1.5 %copy-start.9 = (bf16[512,256]{1,0:T(8,128)(2,1)S(1)}, bf16[512,256]{1,0:T(8,128)(2,1)}, u32[]{:S(2)}) copy-start(bf16[512,256]{1,0:T(8,128)(2,1)} %constant.78) | copy-start | bytes 786436
  19.9 1.5 %copy-start.10 = (bf16[512,256]{1,0:T(8,128)(2,1)S(1)}, bf16[512,256]{1,0:T(8,128)(2,1)}, u32[]{:S(2)}) copy-start(bf16[512,256]{1,0:T(8,128)(2,1)} %constant.79) | copy-start | bytes 786436
  20.0 10.0 %collective-permute-start = (bf16[256,512]{1,0:T(8,128)(2,1)S(1)}, bf16[256,512]{1,0:T(8,128)(2,1)S(1)}, u32[]{:S(2)}, u32[]{:S(2)}) collective-permute-start(bf16[256,512]{1,0:T(8,128)(2,1)S(1)} %convert_element_type.27.sown_ref), channel_id=1, source_target_pairs={{0,128},{128,0},{1,129},{129,1},{2,130},{130,2},{3,131},{131,3},{4... | collective-permute-start | bytes 786440 | tf_op jit(solution)/shard_map/ppermute | solution.py:325
  29.3 1.0 %copy-start.2 = (bf16[512,256]{1,0:T(8,128)(2,1)S(1)}, bf16[512,256]{1,0:T(8,128)(2,1)}, u32[]{:S(2)}) copy-start(bf16[512,256]{1,0:T(8,128)(2,1)} %constant.64.clone.cs_ref) | copy-start | bytes 786436
  29.3 1.0 %copy-start.3 = (bf16[512,256]{1,0:T(8,128)(2,1)S(1)}, bf16[512,256]{1,0:T(8,128)(2,1)}, u32[]{:S(2)}) copy-start(bf16[512,256]{1,0:T(8,128)(2,1)} %constant.65.clone.ss_ref) | copy-start | bytes 786436
  29.4 1.0 %copy-start.5 = (bf16[256,256]{1,0:T(8,128)(2,1)S(1)}, bf16[256,256]{1,0:T(8,128)(2,1)}, u32[]{:S(2)}) copy-start(bf16[256,256]{1,0:T(8,128)(2,1)} %constant.61.clone.sf_ref) | copy-start | bytes 393220
  29.4 1.0 %copy-start.7 = (bf16[256,128]{1,0:T(8,128)(2,1)S(1)}, bf16[256,128]{1,0:T(8,128)(2,1)}, u32[]{:S(2)}) copy-start(bf16[256,128]{1,0:T(8,128)(2,1)} %constant.77.sfn_ref) | copy-start | bytes 196612
  29.7 1.1 %copy-start.1 = (f32[256,512]{1,0:T(8,128)S(1)}, f32[256,512]{1,0:T(8,128)}, u32[]{:S(2)}) copy-start(f32[256,512]{1,0:T(8,128)} %constant.63.clone.st_ref) | copy-start | bytes 1572868
  29.9 1.1 %copy-start = (f32[256,512]{1,0:T(8,128)S(1)}, f32[256,512]{1,0:T(8,128)}, u32[]{:S(2)}) copy-start(f32[256,512]{1,0:T(8,128)} %constant.62.clone.ct_ref) | copy-start | bytes 1572868
  30.0 1.1 %copy-start.4 = (bf16[256,256]{1,0:T(8,128)(2,1)S(1)}, bf16[256,256]{1,0:T(8,128)(2,1)}, u32[]{:S(2)}) copy-start(bf16[256,256]{1,0:T(8,128)(2,1)} %constant.60.clone.cf_ref) | copy-start | bytes 393220
  30.0 1.1 %copy-start.6 = (bf16[256,128]{1,0:T(8,128)(2,1)S(1)}, bf16[256,128]{1,0:T(8,128)(2,1)}, u32[]{:S(2)}) copy-start(bf16[256,128]{1,0:T(8,128)(2,1)} %constant.76.cfn_ref) | copy-start | bytes 196612
  50.8 1.3 %collective-permute-start.2 = (f32[6,512]{1,0:T(8,128)S(1)}, f32[6,512]{1,0:T(8,128)S(1)}, u32[]{:S(2)}, u32[]{:S(2)}) collective-permute-start(f32[6,512]{1,0:T(8,128)S(1)} %get-tuple-element.10), channel_id=1, source_target_pairs={{0,128},{128,0},{1,129},{129,1},{2,130},{130,2},{3,131},{131,3},{4... | collective-permute-start | bytes 36872 | tf_op jit(solution)/shard_map/ppermute | solution.py:333
  69.8 0.7 copy-start.12

commit v7 on v6

--- a/solution.py
+++ b/solution.py
@@ -141,6 +141,91 @@
     return out.reshape(width)
 
 
+def exchange_kernel(
+    n_filt, send_ref, sig_ref, w_ref, recv_out, sig_out, w_out,
+    recv_buf, sig_buf, w_buf, send_sems, recv_sems, pair_sems,
+):
+    det = lax.axis_index("det")
+    grp = lax.axis_index("grp")
+    me = lax.axis_index("filt")
+    mesh_ids = pl.DeviceIdType.MESH
+    partner = (1 - det, grp, me)
+    barrier = pltpu.get_barrier_semaphore()
+    for i in range(n_filt - 1):
+        target = lax.rem(me + 1 + i, n_filt)
+        pl.semaphore_signal(barrier, inc=1, device_id=(det, grp, target), device_id_type=mesh_ids)
+    pl.semaphore_signal(barrier, inc=1, device_id=partner, device_id_type=mesh_ids)
+    pl.semaphore_wait(barrier, n_filt)
+    sends = []
+    for i in range(n_filt - 1):
+        target = lax.rem(me + 1 + i, n_filt)
+        copy = pltpu.make_async_remote_copy(
+            src_ref=send_ref.at[target],
+            dst_ref=recv_buf.at[me],
+            send_sem=send_sems.at[i],
+            recv_sem=recv_sems.at[me],
+            device_id=(det, grp, target),
+            device_id_type=mesh_ids,
+        )
+        copy.start()
+        sends.append(copy)
+    pair = []
+    for k, (src, dst) in enumerate(((sig_ref, sig_buf), (w_ref, w_buf))):
+        copy = pltpu.make_async_remote_copy(
+            src_ref=src,
+            dst_ref=dst,
+            send_sem=pair_sems.at[2 * k],
+            recv_sem=pair_sems.at[2 * k + 1],
+            device_id=partner,
+            device_id_type=mesh_ids,
+        )
+        copy.start()
+        pair.append(copy)
+    for copy in sends:
+        copy.wait_send()
+    for i in range(n_filt - 1):
+        source = lax.rem(me + 1 + i, n_filt)
+        pltpu.make_async_remote_copy(
+            src_ref=send_ref.at[source],
+            dst_ref=recv_buf.at[source],
+            send_sem=send_sems.at[i],
+            recv_sem=recv_sems.at[source],
+            device_id=(det, grp, source),
+            device_id_type=mesh_ids,
+        ).wait_recv()
+    for copy in pair:
+        copy.wait_send()
+        copy.wait_recv()
+    recv_buf[me] = send_ref[me]
+    recv_out[...] = recv_buf[...]
+    sig_out[...] = sig_buf[...]
+    w_out[...] = w_buf[...]
+
+
+def exchange(send_rows, signal, weight):
+    n_filt = send_rows.shape[0]
+    vmem = pl.BlockSpec(memory_space=pltpu.VMEM)
+    return pl.pallas_call(
+        functools.partial(exchange_kernel, n_filt),
+        out_shape=(
+            jax.ShapeDtypeStruct(send_rows.shape, send_rows.dtype),
+            jax.ShapeDtypeStruct(signal.shape, signal.dtype),
+            jax.ShapeDtypeStruct(weight.shape, weight.dtype),
+        ),
+        in_specs=[vmem, vmem, vmem],
+        out_specs=(vmem, vmem, vmem),
+        scratch_shapes=[
+            pltpu.VMEM(send_rows.shape, send_rows.dtype),
+            pltpu.VMEM(signal.shape, signal.dtype),
+            pltpu.VMEM(weight.shape, weight.dtype),
+            pltpu.SemaphoreType.DMA((n_filt,)),
+            pltpu.SemaphoreType.DMA((n_filt,)),
+            pltpu.SemaphoreType.DMA((4,)),
+        ],
+        compiler_params=pltpu.CompilerParams(collective_id=1, has_side_effects=True),
+    )(send_rows, signal, weight)
+
+
 def dot_nt(left, right):
     return lax.dot_general(
         left, right, (((1,), (1,)), ((), ())), preferred_element_type=jnp.float32
@@ -310,20 +395,28 @@
     windowed = jnp.where(
         samples[None, :] < BLK * chirp_blocks[:, None], templates, jnp.zeros_like(templates)
     )
-    payload = jnp.concatenate([windowed, jnp.ones((per_dev, 128), jnp.bfloat16)], axis=1)
-    send_rows = jnp.dot(
-        placing.astype(jnp.bfloat16), payload, preferred_element_type=jnp.float32
+    lanes = 128
+    body_rows = TL // lanes
+    slot_rows = 48
+    payload = jnp.concatenate(
+        [
+            windowed.reshape(per_dev, body_rows, lanes),
+            jnp.ones((per_dev, 1, lanes), jnp.bfloat16),
+            jnp.zeros((per_dev, slot_rows - body_rows - 1, lanes), jnp.bfloat16),
+        ],
+        axis=1,
+    )
+    send_rows = jnp.einsum(
+        "js,srl->jrl", placing.astype(jnp.bfloat16), payload, preferred_element_type=jnp.float32
     ).astype(jnp.bfloat16)
-    recv_rows = lax.all_to_all(send_rows, "filt", split_axis=0, concat_axis=0, tiled=True)
-    valid = recv_rows[:, TL] > 0.5
+    own_signal = strain[0].astype(jnp.bfloat16).reshape(N1, N2)
+    own_weight = inv_asd[0].reshape(N2 // 2, N1)
+    recv_rows, other_signal, other_weight = exchange(send_rows, own_signal, own_weight)
+    valid = recv_rows[:, body_rows, 0] > 0.5
     wanted = detector * mine + jnp.arange(mine, dtype=jnp.int32)
-    my_rows = compact(recv_rows[:, :TL], valid, wanted)
+    my_rows = compact(recv_rows[:, :body_rows, :].reshape(filt_count * capacity, TL), valid, wanted)
     windowed = my_rows.reshape(mine, TL // N2, N2)
     swap = [(0, 1), (1, 0)]
-    own_signal = strain[0].astype(jnp.bfloat16).reshape(N1, N2)
-    own_weight = inv_asd[0].reshape(N2 // 2, N1)
-    other_signal = lax.ppermute(own_signal, "det", swap)
-    other_weight = lax.ppermute(own_weight, "det", swap)
     full = filter_bank(
         windowed, tables, (own_signal, other_signal), (own_weight, other_weight),
         slide[0], detector,

time: 71.4 us -> 78.6 us (1.10)
  Pallas kernels: 35.8 us -> 58.6 us
  starting transfers between devices: 12.2 us -> 0.09 us
  waiting for transfers between devices: 8.61 us -> 1.17 us
  local copies, waits for them, and re-layouts: 5.49 us -> 8.65 us
    pallas_call x0 -> x1, Pallas kernels: none -> 21.9 us  [exchange(): pl.pallas_call(functools.partial(exchange_kernel, n_filt), out_shape=(jax...]
    all_to_all x1 -> x0, starting transfers between devices: 11.5 us -> none  [shards(): lax.all_to_all(send_rows, 'filt', split_axis=0, concat_axis=0, tiled=True)]
    all_to_all x1 -> x0, waiting for transfers between devices: 7.44 us -> none  [shards(): lax.all_to_all(send_rows, 'filt', split_axis=0, concat_axis=0, tiled=True)]
    gt x1, other arithmetic: 0.11 us -> 1.52 us  [shards(): valid = recv_rows[:, body_rows, 0] > 0.5]
    slice x0 -> x1, local copies, waits for them, and re-layouts: none -> 1.01 us  [shards(): recv_rows[:, :body_rows, :].reshape(filt_count * capacity, TL)]
    unnamed x1, other arithmetic: 1.32 us -> 2.28 us
    pallas_call x1, Pallas kernels: 16.5 us -> 17.4 us  [group_max(): pl.pallas_call(functools.partial(loudest_kernel, stages), out_shape=jax.S...]
    select_n x1, other arithmetic: 1.01 us -> 0.1 us  [shards(): jnp.where(samples[None, :] < BLK * chirp_blocks[:, None], templates, jnp....]
  transfers between devices with their start and end apart: 4 -> 1, of which waited for: 2 -> 1; matrix products, arithmetic and copies ran while one was open for 6% -> 0% of each run, Pallas kernels for 0% -> 0%
where the time goes in v7:
time: 78.6 us; the launch traced here: 77.7 us
  Pallas kernels  58.6 us (75%)
  local copies, waits for them, and re-layouts  8.65 us (11%)
  other arithmetic  6.99 us (9%)
  between operations  1.62 us (2%)
  waiting for transfers between devices  1.17 us (1%)
    pallas_call x1, Pallas kernels, exchange(): pl.pallas_call(functools.partial(exchange_kernel, n_filt), out_shape=(jax...  21.9 us
    pallas_call x1, Pallas kernels, filter_bank(): pl.pallas_call(filter_kernel, out_shape=jax.ShapeDtypeStruct((count, N1,...  19.2 us
    pallas_call x1, Pallas kernels, group_max(): pl.pallas_call(functools.partial(loudest_kernel, stages), out_shape=jax.S...  17.4 us
    unnamed x42, local copies, waits for them, and re-layouts  4.27 us
    unnamed x1, other arithmetic  2.28 us
  transfers between devices with their start and end apart: 1, of which 1 were waited for; matrix products, arithmetic and copies ran while one was open for 0% of the time, Pallas kernels for 0%

profile of v7, /device:TPU:32, one launch (start us, length us, event | category | flops | bytes accessed | tf_op | source)
XLA Modules:
  0.0 77.7 jit_solution(15739908503627030422)
XLA Ops:
  1.3 0.5 broadcast.61
  1.8 2.3 %reduce.9 = f32[65536]{0:T(1024)S(1)} reduce(f32[1,65536]{1,0:T(1,128)} %param.13, f32[]{:T(128)} %broadcast.61), dimensions={0}, to_apply=%param.13.reduce_sub_computation.3 | reduce | bytes 524292 | tf_op args[1]
  4.1 0.8 reshape_squeeze.3.w_ref.wown_ref
  4.9 1.4 %convert_reduce_fusion = bf16[131072]{0:T(1024)(128)(2,1)S(1)} fusion(f32[1,131072]{1,0:T(1,128)S(1)} %copy-done.12), kind=kLoop, calls=%fused_computation.2 | loop fusion | flops 131072 | bytes 786432 | tf_op jit(solution)/shard_map/convert_element_type | solution.py:412
  6.3 0.9 %convert_element_type.36.sig_ref.sown_ref = bf16[256,512]{1,0:T(8,128)(2,1)} reshape(bf16[131072]{0:T(1024)(128)(2,1)S(1)} %convert_reduce_fusion) | data formatting | bytes 524288 | tf_op jit(solution)/shard_map/convert_element_type | solution.py:412
  7.4 0.6 copy-done.18
  8.0 0.2 convert_reduce_fusion.1
  8.3 0.4 fusion.3
  8.7 0.9 %copy.31.send_ref = bf16[32,48,128]{2,1,0:T(8,128)(2,1)} copy(bf16[32,48,128]{2,0,1:T(8,128)(2,1)S(1)} %fusion.3) | data formatting | bytes 786432 | tf_op jit(solution)/shard_map/js,srl->jrl/dot_general | solution.py:409
  9.6 21.9 %shard_map.131 = (bf16[32,48,128]{2,1,0:T(8,128)(2,1)}, bf16[256,512]{1,0:T(8,128)(2,1)}, f32[256,256]{1,0:T(8,128)}) custom-call(bf16[32,48,128]{2,1,0:T(8,128)(2,1)} %copy.31.send_ref, bf16[256,512]{1,0:T(8,128)(2,1)} %convert_element_type.36.sig_ref.sown_ref, f32[256,256]{1,0:T(8,128)} %reshape_squeeze.3.w_ref.wown_ref), custom_call_target="tpu_custom_call" | custom-call | tf_op jit(solution)/shard_map/pallas_call | solution.py:208
  31.6 1.5 %compare_reduce_fusion = (pred[32]{0:T(512)(128)(4,1)S(1)}, s32[32,1,1]{2,1,0:T(1,128)S(1)}) fusion(bf16[32,48,128]{2,1,0:T(8,128)(2,1)} %get-tuple-element.5), kind=kLoop, calls=%fused_computation.21 | loop fusion | flops 64 | bytes 224 | tf_op jit(solution)/shard_map/gt | solution.py:415
  33.1 1.0 %slice.13 = bf16[32,32,128]{2,1,0:T(8,128)(2,1)S(1)} slice(bf16[32,48,128]{2,1,0:T(8,128)(2,1)} %get-tuple-element.5), slice={[0:32], [0:32], [0:128]} | slice | bytes 524288 | tf_op jit(solution)/shard_map/slice | solution.py:417
  34.3 0.2 convolution_convert_fusion
  34.7 0.5 copy-done.13
  35.3 0.1 dynamic-slice_bitcast_fusion.1
  35.7 0.7 copy-done.4
  36.4 0.2 copy-done.5
  36.8 19.2 %shard_map.132 = f32[6,256,4]{2,1,0:T(8,128)S(1)} custom-call(s32[2]{0:T(128)S(1)} %pad_add_fusion.scalar_ref, bf16[6,128,512]{2,1,0:T(8,128)(2,1)S(1)} %concatenate.19.x_ref, bf16[256,128]{1,0:T(8,128)(2,1)S(1)} %copy-done.10, bf16[256,128]{1,0:T(8,128)(2,1)S(1)} %copy-done.11, f32[256,512]{1,0:T(8,128)S(1)} %copy-done.4, f32[256,512]{1,0:T(8,128)S(1)} %copy-done.5, ...), custom_call_target="tpu_custom_call" | custom-call | flops 8455716864 | bytes 8388608 | tf_op jit(solution)/shard_map/pallas_call | solution.py:366
  56.1 0.4 reshape.84
  56.6 1.2 %collective-permute-done = f32[6,512]{1,0:T(8,128)S(1)} collective-permute-done((f32[6,512]{1,0:T(8,128)S(1)}, f32[6,512]{1,0:T(8,128)S(1)}, u32[]{:S(2)}, u32[]{:S(2)}) %collective-permute-start) | collective-permute-done | bytes 12320 | tf_op jit(solution)/shard_map/ppermute | solution.py:426
  57.8 1.2 %fusion.19 = (f32[512]{0:T(512)}, f32[12,512]{1,0:T(8,128)}) fusion(f32[6,512]{1,0:T(8,128)S(1)} %get-tuple-element.17, f32[6,512]{1,0:T(8,128)S(1)} %collective-permute-done, pred[]{:T(512)S(6)} %eq.20), kind=kLoop, calls=%fused_computation.41 | loop fusion | flops 24064 | bytes 51201 | tf_op jit(solution)/shard_map/reduce_max | solution.py:430
  59.0 17.4 %shard_map.133 = f32[1,512]{1,0:T(1,128)} custom-call(f32[1,512]{1,0:T(1,128)} %bitcast.39), custom_call_target="tpu_custom_call" | custom-call | tf_op jit(solution)/shard_map/pallas_call | solution.py:133
  76.5 0.7 copy-done.16
  77.1 0.6 copy.35
  (52 shorter events, 1.4 us)
Async XLA Ops:
  1.8 3.1 %copy-start.12 = (f32[1,131072]{1,0:T(1,128)S(1)}, f32[1,131072]{1,0:T(1,128)}, u32[]{:S(2)}) copy-start(f32[1,131072]{1,0:T(1,128)} %param.12) | copy-start | bytes 1572868
  6.3 0.9 %copy-start.17 = (s32[12]{0:T(128)S(1)}, s32[12]{0:T(128)}, u32[]{:S(2)}) copy-start(s32[12]{0:T(128)} %param.15) | copy-start | bytes 148
  6.3 0.9 %copy-start.15 = (bf16[12,4096]{1,0:T(8,128)(2,1)S(1)}, bf16[12,4096]{1,0:T(8,128)(2,1)}, u32[]{:S(2)}) copy-start(bf16[12,4096]{1,0:T(8,128)(2,1)} %param.14) | copy-start | bytes 294916
  7.3 0.7 copy-start.18
  33.1 1.6 %copy-start.14 = (bf16[512,256]{1,0:T(8,128)(2,1)S(1)}, bf16[512,256]{1,0:T(8,128)(2,1)}, u32[]{:S(2)}) copy-start(bf16[512,256]{1,0:T(8,128)(2,1)} %constant.78) | copy-start | bytes 786436
  34.3 1.0 %copy-start.13 = (bf16[512,256]{1,0:T(8,128)(2,1)S(1)}, bf16[512,256]{1,0:T(8,128)(2,1)}, u32[]{:S(2)}) copy-start(bf16[512,256]{1,0:T(8,128)(2,1)} %constant.77) | copy-start | bytes 786436
  34.5 1.1 %copy-start.11 = (bf16[256,128]{1,0:T(8,128)(2,1)S(1)}, bf16[256,128]{1,0:T(8,128)(2,1)}, u32[]{:S(2)}) copy-start(bf16[256,128]{1,0:T(8,128)(2,1)} %constant.76.sfn_ref) | copy-start | bytes 196612
  34.6 1.0 %copy-start.6 = (bf16[512,256]{1,0:T(8,128)(2,1)S(1)}, bf16[512,256]{1,0:T(8,128)(2,1)}, u32[]{:S(2)}) copy-start(bf16[512,256]{1,0:T(8,128)(2,1)} %constant.65.clone.cs_ref) | copy-start | bytes 786436
  34.6 1.0 %copy-start.7 = (bf16[512,256]{1,0:T(8,128)(2,1)S(1)}, bf16[512,256]{1,0:T(8,128)(2,1)}, u32[]{:S(2)}) copy-start(bf16[512,256]{1,0:T(8,128)(2,1)} %constant.66.clone.ss_ref) | copy-start | bytes 786436
  34.6 1.1 %copy-start.8 = (bf16[256,256]{1,0:T(8,128)(2,1)S(1)}, bf16[256,256]{1,0:T(8,128)(2,1)}, u32[]{:S(2)}) copy-start(bf16[256,256]{1,0:T(8,128)(2,1)} %constant.61.clone.cf_ref) | copy-start | bytes 393220
  34.6 1.1 %copy-start.9 = (bf16[256,256]{1,0:T(8,128)(2,1)S(1)}, bf16[256,256]{1,0:T(8,128)(2,1)}, u32[]{:S(2)}) copy-start(bf16[256,256]{1,0:T(8,128)(2,1)} %constant.62.clone.sf_ref) | copy-start | bytes 393220
  34.6 1.1 %copy-start.10 = (bf16[256,128]{1,0:T(8,128)(2,1)S(1)}, bf16[256,128]{1,0:T(8,128)(2,1)}, u32[]{:S(2)}) copy-start(bf16[256,128]{1,0:T(8,128)(2,1)} %constant.75.cfn_ref) | copy-start | bytes 196612
  35.2 1.1 %copy-start.4 = (f32[256,512]{1,0:T(8,128)S(1)}, f32[256,512]{1,0:T(8,128)}, u32[]{:S(2)}) copy-start(f32[256,512]{1,0:T(8,128)} %constant.63.clone.ct_ref) | copy-start | bytes 1572868
  35.3 1.3 %copy-start.5 = (f32[256,512]{1,0:T(8,128)S(1)}, f32[256,512]{1,0:T(8,128)}, u32[]{:S(2)}) copy-start(f32[256,512]{1,0:T(8,128)} %constant.64.clone.st_ref) | copy-start | bytes 1572868
  35.4 1.2 %copy-start.2 = (bf16[256,512]{1,0:T(8,128)(2,1)S(1)}, bf16[256,512]{1,0:T(8,128)(2,1)}, u32[]{:S(2)}) copy-start(bf16[256,512]{1,0:T(8,128)(2,1)} %get-tuple-element.6.soth_ref) | copy-start | bytes 786436
  35.4 1.3 %copy-start.3 = (f32[256,256]{1,0:T(8,128)S(1)}, f32[256,256]{1,0:T(8,128)}, u32[]{:S(2)}) copy-start(f32[256,256]{1,0:T(8,128)} %get-tuple-element.7.woth_ref) | copy-start | bytes 786436
  35.4 1.3 %copy-start = (f32[256,256]{1,0:T(8,128)S(1)}, f32[256,256]{1,0:T(8,128)}, u32[]{:S(2)}) copy-start(f32[256,256]{1,0:T(8,128)} %reshape_squeeze.3.w_ref.wown_ref) | copy-start | bytes 786436
  35.4 1.4 %copy-start.1 = (bf16[256,512]{1,0:T(8,128)(2,1)S(1)}, bf16[256,512]{1,0:T(8,128)(2,1)}, u32[]{:S(2)}) copy-start(bf16[256,512]{1,0:T(8,128)(2,1)} %convert_element_type.36.sig_ref.sown_ref) | copy-start | bytes 786436
  56.5 1.3 %collective-permute-start = (f32[6,512]{1,0:T(8,128)S(1)}, f32[6,512]{1,0:T(8,128)S(1)}, u32[]{:S(2)}, u32[]{:S(2)}) collective-permute-start(f32[6,512]{1,0:T(8,128)S(1)} %get-tuple-element.16), channel_id=1, source_target_pairs={{0,128},{128,0},{1,129},{129,1},{2,130},{130,2},{3,131},{131,3},{4... | collective-permute-start | bytes 36872 | tf_op jit(solution)/shard_map/ppermute | solution.py:426
  76.5 0.7 copy-start.16

commit v8 on v6

--- a/solution.py
+++ b/solution.py
@@ -147,42 +147,73 @@
     )
 
 
+def first_transform(ct_ref, st_ref, cs_ref, ss_ref, cos_rows, sin_rows, x):
+    f32 = jnp.float32
+    bf16 = jnp.bfloat16
+    cos_twist = ct_ref[...]
+    sin_twist = st_ref[...]
+    real_a = jnp.dot(cos_rows, x, preferred_element_type=f32)
+    imag_a = -jnp.dot(sin_rows, x, preferred_element_type=f32)
+    real_b = (real_a * cos_twist + imag_a * sin_twist).astype(bf16)
+    imag_b = (imag_a * cos_twist - real_a * sin_twist).astype(bf16)
+    cos_second = cs_ref[...]
+    sin_second = ss_ref[...]
+    real_x = jnp.dot(real_b, cos_second, preferred_element_type=f32) + jnp.dot(
+        imag_b, sin_second, preferred_element_type=f32
+    )
+    imag_x = jnp.dot(imag_b, cos_second, preferred_element_type=f32) - jnp.dot(
+        real_b, sin_second, preferred_element_type=f32
+    )
+    return real_x, imag_x
+
+
+def spectrum_kernel(
+    det_ref, ct_ref, st_ref, cs_ref, ss_ref, cf_ref, sf_ref,
+    sown_ref, soth_ref, wown_ref, woth_ref, pr_ref, pi_ref, w2_ref,
+):
+    det = det_ref[0]
+    for slot, sig_ref, w_ref in ((det, sown_ref, wown_ref), (1 - det, soth_ref, woth_ref)):
+        real_s, imag_s = first_transform(
+            ct_ref, st_ref, cs_ref, ss_ref, cf_ref[...], sf_ref[...], sig_ref[...]
+        )
+        weight = jnp.transpose(w_ref[...])
+        pr_ref[slot] = weight * real_s
+        pi_ref[slot] = weight * imag_s
+        w2_ref[slot] = weight * weight
+
+
+def spectra(tables, signals, weights, det):
+    cos_first, sin_first, cos_twist, sin_twist, cos_second, sin_second = tables
+    vmem = pl.BlockSpec(memory_space=pltpu.VMEM)
+    smem = pl.BlockSpec(memory_space=pltpu.SMEM)
+    part = jax.ShapeDtypeStruct((2, N1, N2 // 2), jnp.float32)
+    flops = 2 * 2 * (2 * N1 * N1 * N2 + 4 * N1 * N2 * (N2 // 2))
+    return pl.pallas_call(
+        spectrum_kernel,
+        out_shape=(part, part, part),
+        in_specs=[smem] + [vmem] * 10,
+        out_specs=(vmem, vmem, vmem),
+        cost_estimate=pl.CostEstimate(
+            flops=flops, transcendentals=0, bytes_accessed=4 * 1024 * 1024
+        ),
+    )(
+        det.reshape(1).astype(jnp.int32), cos_twist, sin_twist, cos_second, sin_second,
+        cos_first, sin_first, signals[0], signals[1], weights[0], weights[1],
+    )
+
+
 def filter_kernel(
     scalar_ref, x_ref, cfn_ref, sfn_ref, ct_ref, st_ref, cs_ref, ss_ref, cf_ref, sf_ref,
-    cfr_ref, sfr_ref, sown_ref, soth_ref, wown_ref, woth_ref, out_ref,
-    er_ref, ei_ref, pr_ref, pi_ref, w2_ref,
+    cfr_ref, sfr_ref, pr_ref, pi_ref, w2_ref, out_ref, er_ref, ei_ref,
 ):
     f32 = jnp.float32
     bf16 = jnp.bfloat16
 
-    def first_stage(cos_rows, sin_rows, x):
-        cos_twist = ct_ref[...]
-        sin_twist = st_ref[...]
-        real_a = jnp.dot(cos_rows, x, preferred_element_type=f32)
-        imag_a = -jnp.dot(sin_rows, x, preferred_element_type=f32)
-        real_b = (real_a * cos_twist + imag_a * sin_twist).astype(bf16)
-        imag_b = (imag_a * cos_twist - real_a * sin_twist).astype(bf16)
-        cos_second = cs_ref[...]
-        sin_second = ss_ref[...]
-        real_x = jnp.dot(real_b, cos_second, preferred_element_type=f32) + jnp.dot(
-            imag_b, sin_second, preferred_element_type=f32
-        )
-        imag_x = jnp.dot(imag_b, cos_second, preferred_element_type=f32) - jnp.dot(
-            real_b, sin_second, preferred_element_type=f32
-        )
-        return real_x, imag_x
-
-    @pl.when(pl.program_id(0) == 0)
-    def _():
-        det = scalar_ref[1]
-        for slot, sig_ref, w_ref in ((det, sown_ref, wown_ref), (1 - det, soth_ref, woth_ref)):
-            real_s, imag_s = first_stage(cf_ref[...], sf_ref[...], sig_ref[...])
-            weight = jnp.transpose(w_ref[...])
-            pr_ref[slot] = weight * real_s
-            pi_ref[slot] = weight * imag_s
-            w2_ref[slot] = weight * weight
-
-    temp_real, temp_imag = first_stage(cfn_ref[...], sfn_ref[...], x_ref[0])
+    f32 = jnp.float32
+    bf16 = jnp.bfloat16
+    temp_real, temp_imag = first_transform(
+        ct_ref, st_ref, cs_ref, ss_ref, cfn_ref[...], sfn_ref[...], x_ref[0]
+    )
     power = temp_real * temp_real + temp_imag * temp_imag
     cos_back = cs_ref[...]
     sin_back = ss_ref[...]
@@ -210,8 +241,9 @@
     z_imag = jnp.dot(sin_first, e_real, preferred_element_type=f32) + jnp.dot(
         cos_first, e_imag, preferred_element_type=f32
     )
-    first = (z_real * z_real + z_imag * z_imag) / (NFFT * sigma0)
+    first = (z_real * z_real + z_imag * z_imag) * (1.0 / (NFFT * sigma0))
     sigma1, e_real, e_imag = back_half(1)
+    scale1 = 1.0 / (NFFT * sigma1)
     er_ref[...] = e_real
     ei_ref[...] = e_imag
     rem = scalar_ref[0]
@@ -230,12 +262,12 @@
         z_imag = jnp.dot(sin_rows, e_r, preferred_element_type=f32) + jnp.dot(
             cos_rows, e_i, preferred_element_type=f32
         )
-        second = (z_real * z_real + z_imag * z_imag) / (NFFT * sigma1)
+        second = (z_real * z_real + z_imag * z_imag) * scale1
         network = first[:, col * BLK:(col + 1) * BLK] + second
         out_ref[0, :, col:col + 1] = jnp.max(network, axis=1, keepdims=True)
 
 
-def filter_bank(windowed, tables, signals, weights, shift, det):
+def filter_bank(windowed, tables, spectrum, shift):
     cos_first, sin_first, cos_twist, sin_twist, cos_second, sin_second = tables
     count, rows_used, width = windowed.shape
     pad_rows = 128
@@ -244,7 +276,7 @@
     )
     tiles = N2 // BLK
     quot = shift // tiles
-    scalars = jnp.stack([lax.rem(shift, tiles), det]).astype(jnp.int32)
+    scalars = lax.rem(shift, tiles).reshape(1).astype(jnp.int32)
     doubled_cos = jnp.concatenate([cos_first, cos_first], axis=0)
     doubled_sin = jnp.concatenate([sin_first, sin_first], axis=0)
     cos_rolled = jnp.stack(
@@ -256,7 +288,7 @@
     operands = [
         cos_first[:, :pad_rows], sin_first[:, :pad_rows], cos_twist, sin_twist,
         cos_second, sin_second, cos_first, sin_first, cos_rolled, sin_rolled,
-        signals[0], signals[1], weights[0], weights[1],
+        *spectrum,
     ]
 
     def whole(array):
@@ -269,13 +301,7 @@
         in_specs=[pl.BlockSpec((1, pad_rows, width), lambda i, r: (i, 0, 0))]
         + [whole(a) for a in operands],
         out_specs=pl.BlockSpec((1, N1, tiles), lambda i, r: (i, 0, 0)),
-        scratch_shapes=[
-            pltpu.VMEM((N1, N2), jnp.bfloat16),
-            pltpu.VMEM((N1, N2), jnp.bfloat16),
-            pltpu.VMEM((2, N1, N2 // 2), jnp.float32),
-            pltpu.VMEM((2, N1, N2 // 2), jnp.float32),
-            pltpu.VMEM((2, N1, N2 // 2), jnp.float32),
-        ],
+        scratch_shapes=[pltpu.VMEM((N1, N2), jnp.bfloat16), pltpu.VMEM((N1, N2), jnp.bfloat16)],
     )
     matmuls = 2 * N1 * pad_rows * N2 + 4 * N1 * N2 * (N2 // 2) + 16 * N1 * (N2 // 2) * N2
     out = pl.pallas_call(
@@ -324,10 +350,8 @@
     own_weight = inv_asd[0].reshape(N2 // 2, N1)
     other_signal = lax.ppermute(own_signal, "det", swap)
     other_weight = lax.ppermute(own_weight, "det", swap)
-    full = filter_bank(
-        windowed, tables, (own_signal, other_signal), (own_weight, other_weight),
-        slide[0], detector,
-    )
+    spectrum = spectra(tables, (own_signal, other_signal), (own_weight, other_weight), detector)
+    full = filter_bank(windowed, tables, spectrum, slide[0])
     keep = lax.dynamic_slice_in_dim(full, detector * half_blk, half_blk, axis=1)
     give = lax.dynamic_slice_in_dim(full, (1 - detector) * half_blk, half_blk, axis=1)
     got = lax.ppermute(give, "det", swap)

time: 71.4 us -> 75.5 us (1.057)
  local copies, waits for them, and re-layouts: 5.49 us -> 8.48 us
  Pallas kernels: 35.8 us -> 37.5 us
    pallas_call x0 -> x1, Pallas kernels: none -> 4.2 us  [spectra(): pl.pallas_call(spectrum_kernel, out_shape=(part, part, part), in_specs=[s...]
    unnamed x34 -> x50, local copies, waits for them, and re-layouts: 4.12 us -> 7.1 us
    pallas_call x1, Pallas kernels: 19.2 us -> 16.8 us  [filter_bank(): pl.pallas_call(filter_kernel, out_shape=jax.ShapeDtypeStruct((count, N1,...]
    unnamed x1, other arithmetic: 1.32 us -> 2.28 us
    select_n x1, other arithmetic: 1.01 us -> 0.1 us  [shards(): jnp.where(samples[None, :] < BLK * chirp_blocks[:, None], templates, jnp....]
  transfers between devices with their start and end apart: 4 -> 4, of which waited for: 2 -> 2; matrix products, arithmetic and copies ran while one was open for 6% -> 6% of each run, Pallas kernels for 0% -> 6%
where the time goes in v8:
time: 75.5 us; the launch traced here: 75 us
  Pallas kernels  37.5 us (50%)
  starting transfers between devices  12.2 us (16%)
  waiting for transfers between devices  8.51 us (11%)
  local copies, waits for them, and re-layouts  8.48 us (11%)
  other arithmetic  6.26 us (8%)
  between operations  1.69 us (2%)
    pallas_call x1, Pallas kernels, filter_bank(): pl.pallas_call(filter_kernel, out_shape=jax.ShapeDtypeStruct((count, N1,...  16.8 us
    pallas_call x1, Pallas kernels, group_max(): pl.pallas_call(functools.partial(loudest_kernel, stages), out_shape=jax.S...  16.5 us
    all_to_all x1, starting transfers between devices, shards(): lax.all_to_all(send_rows, 'filt', split_axis=0, concat_axis=0, tiled=True)  11.5 us
    all_to_all x1, waiting for transfers between devices, shards(): lax.all_to_all(send_rows, 'filt', split_axis=0, concat_axis=0, tiled=True)  7.34 us
    unnamed x50, local copies, waits for them, and re-layouts  7.1 us
    pallas_call x1, Pallas kernels, spectra(): pl.pallas_call(spectrum_kernel, out_shape=(part, part, part), in_specs=[s...  4.2 us
    unnamed x1, other arithmetic  2.28 us
  transfers between devices with their start and end apart: 4, of which 2 were waited for; matrix products, arithmetic and copies ran while one was open for 6% of the time, Pallas kernels for 6%

profile of v8, /device:TPU:32, one launch (start us, length us, event | category | flops | bytes accessed | tf_op | source)
XLA Modules:
  0.0 75.0 jit_solution(6142342379930111752)
XLA Ops:
  0.6 0.5 broadcast.43
  1.1 2.3 %reduce.9 = f32[65536]{0:T(1024)S(1)} reduce(f32[1,65536]{1,0:T(1,128)} %param.13, f32[]{:T(128)} %broadcast.43), dimensions={0}, to_apply=%param.13.reduce_sub_computation.3 | reduce | bytes 524292 | tf_op args[1]
  3.6 1.4 %convert_reduce_fusion = bf16[131072]{0:T(1024)(128)(2,1)S(1)} fusion(f32[1,131072]{1,0:T(1,128)S(1)} %copy-done.11), kind=kLoop, calls=%fused_computation.3 | loop fusion | flops 131072 | bytes 786432 | tf_op jit(solution)/shard_map/convert_element_type | solution.py:349
  5.2 0.6 collective-permute-start
  6.4 0.5 broadcast.44
  7.0 0.8 %reduce.10 = bf16[32,4224]{1,0:T(8,128)(2,1)S(1)} reduce(bf16[32,1,4224]{2,0,1:T(8,128)(2,1)S(1)} %fusion, bf16[]{:T(256)} %broadcast.44), dimensions={1}, to_apply=%copy.16.reduce_sub_computation | reduce | bytes 540674 | tf_op jit(solution)/shard_map/all_to_all | solution.py:343
  7.7 0.9 %reshape.83 = bf16[32,2,2112]{2,1,0:T(2,128)(2,1)} reshape(bf16[32,4224]{1,0:T(8,128)(2,1)S(1)} %reduce.10) | data formatting | bytes 540672
  8.6 11.5 %all-to-all-start = ((bf16[32,2,2112]{2,1,0:T(2,128)(2,1)}), bf16[32,2,2112]{2,1,0:T(2,128)(2,1)S(1)}, u32[]{:S(2)}, u32[]{:S(2)}) async-start(bf16[32,2,2112]{2,1,0:T(2,128)(2,1)} %reshape.83), calls=%async_computation | async-start | bytes 557056 | tf_op jit(solution)/shard_map/all_to_all | solution.py:343
  21.1 0.7 copy-done.18
  21.9 4.2 %shard_map.131 = (f32[2,256,256]{2,1,0:T(8,128)}, f32[2,256,256]{2,1,0:T(8,128)}, f32[2,256,256]{2,1,0:T(8,128)}) custom-call(s32[1]{0:T(128)} %bitcast.7.det_ref, f32[256,512]{1,0:T(8,128)} %constant.62.clone.ct_ref, f32[256,512]{1,0:T(8,128)} %constant.63.clone.st_ref, bf16[512,256]{1,0:T(8,128)(2,1)} %constant.64.clone.cs_ref, ...), custom_call_target="tpu_custom_call" | custom-call | flops 805306368 | bytes 4194304 | tf_op jit(solution)/shard_map/pallas_call | solution.py:191
  26.1 7.3 %all-to-all-done = bf16[32,2,2112]{2,1,0:T(2,128)(2,1)S(1)} async-done(((bf16[32,2,2112]{2,1,0:T(2,128)(2,1)}), bf16[32,2,2112]{2,1,0:T(2,128)(2,1)S(1)}, u32[]{:S(2)}, u32[]{:S(2)}) %all-to-all-start) | async-done | bytes 270368 | tf_op jit(solution)/shard_map/all_to_all | solution.py:343
  33.4 0.3 reshape.84
  34.5 0.2 copy-done.2
  34.8 0.4 copy-done.1
  35.2 0.2 copy-done
  35.5 1.0 %copy-done.9 = f32[2,256,256]{2,1,0:T(8,128)S(1)} copy-done((f32[2,256,256]{2,1,0:T(8,128)S(1)}, f32[2,256,256]{2,1,0:T(8,128)}, u32[]{:S(2)}) %copy-start.9) | copy-done | bytes 524312
  36.5 1.0 %copy-done.10 = f32[2,256,256]{2,1,0:T(8,128)S(1)} copy-done((f32[2,256,256]{2,1,0:T(8,128)S(1)}, f32[2,256,256]{2,1,0:T(8,128)}, u32[]{:S(2)}) %copy-start.10) | copy-done | bytes 524312
  37.6 16.8 %shard_map.132 = f32[6,256,4]{2,1,0:T(8,128)S(1)} custom-call(s32[1]{0:T(128)} %bitcast.1.scalar_ref, bf16[6,128,512]{2,1,0:T(8,128)(2,1)S(1)} %concatenate.19.x_ref, bf16[256,128]{1,0:T(8,128)(2,1)S(1)} %copy-done.6, bf16[256,128]{1,0:T(8,128)(2,1)S(1)} %copy-done.7, f32[256,512]{1,0:T(8,128)S(1)} %copy-done, f32[256,512]{1,0:T(8,128)S(1)} %copy-done.1, ...), custom_call_target="tpu_custom_call" | custom-call | flops 8455716864 | bytes 8388608 | tf_op jit(solution)/shard_map/pallas_call | solution.py:307
  54.4 0.4 reshape.68
  54.9 1.2 %collective-permute-done.2 = f32[6,512]{1,0:T(8,128)S(1)} collective-permute-done((f32[6,512]{1,0:T(8,128)S(1)}, f32[6,512]{1,0:T(8,128)S(1)}, u32[]{:S(2)}, u32[]{:S(2)}) %collective-permute-start.2) | collective-permute-done | bytes 12320 | tf_op jit(solution)/shard_map/ppermute | solution.py:357
  56.1 1.2 %fusion.14 = (f32[512]{0:T(512)}, f32[12,512]{1,0:T(8,128)}) fusion(f32[6,512]{1,0:T(8,128)S(1)} %get-tuple-element.17, f32[6,512]{1,0:T(8,128)S(1)} %collective-permute-done.2, pred[]{:T(512)S(6)} %eq.20), kind=kLoop, calls=%fused_computation.36 | loop fusion | flops 24064 | bytes 51201 | tf_op jit(solution)/shard_map/reduce_max | solution.py:361
  57.3 16.5 %shard_map.133 = f32[1,512]{1,0:T(1,128)} custom-call(f32[1,512]{1,0:T(1,128)} %bitcast.30), custom_call_target="tpu_custom_call" | custom-call | tf_op jit(solution)/shard_map/pallas_call | solution.py:133
  73.8 0.7 copy-done.17
  74.5 0.6 copy.26
  (60 shorter events, 2.1 us)
Async XLA Ops:
  1.1 2.5 %copy-start.11 = (f32[1,131072]{1,0:T(1,128)S(1)}, f32[1,131072]{1,0:T(1,128)}, u32[]{:S(2)}) copy-start(f32[1,131072]{1,0:T(1,128)} %param.12) | copy-start | bytes 1572868
  3.5 1.5 %copy-start.14 = (f32[256,256]{1,0:T(8,128)}, f32[256,256]{1,0:T(8,128)S(1)}, u32[]{:S(2)}) copy-start(f32[256,256]{1,0:T(8,128)S(1)} %reshape_squeeze.3.wown_ref) | copy-start | bytes 786436
  3.5 17.6 %collective-permute-start.1 = (f32[256,256]{1,0:T(8,128)S(1)}, f32[256,256]{1,0:T(8,128)S(1)}, u32[]{:S(2)}, u32[]{:S(2)}) collective-permute-start(f32[256,256]{1,0:T(8,128)S(1)} %reshape_squeeze.3.wown_ref), channel_id=1, source_target_pairs={{0,128},{128,0},{1,129},{129,1},{2,130},{130,2},{3,131},{131,3},{4... | collective-permute-start | bytes 786440 | tf_op jit(solution)/shard_map/ppermute | solution.py:352
  5.0 0.8 %copy-start.20 = (s32[12]{0:T(128)S(1)}, s32[12]{0:T(128)}, u32[]{:S(2)}) copy-start(s32[12]{0:T(128)} %param.15) | copy-start | bytes 148
  5.0 1.1 %copy-start.16 = (bf16[12,4096]{1,0:T(8,128)(2,1)S(1)}, bf16[12,4096]{1,0:T(8,128)(2,1)}, u32[]{:S(2)}) copy-start(bf16[12,4096]{1,0:T(8,128)(2,1)} %param.14) | copy-start | bytes 294916
  5.2 1.2 %copy-start.15 = (bf16[256,512]{1,0:T(8,128)(2,1)}, bf16[256,512]{1,0:T(8,128)(2,1)S(1)}, u32[]{:S(2)}) copy-start(bf16[256,512]{1,0:T(8,128)(2,1)S(1)} %convert_element_type.27.sown_ref) | copy-start | bytes 786436
  5.2 15.8 %collective-permute-start = (bf16[256,512]{1,0:T(8,128)(2,1)S(1)}, bf16[256,512]{1,0:T(8,128)(2,1)S(1)}, u32[]{:S(2)}, u32[]{:S(2)}) collective-permute-start(bf16[256,512]{1,0:T(8,128)(2,1)S(1)} %convert_element_type.27.sown_ref), channel_id=1, source_target_pairs={{0,128},{128,0},{1,129},{129,1},{2,130},{130,2},{3,131},{131,3},{4... | collective-permute-start | bytes 786440 | tf_op jit(solution)/shard_map/ppermute | solution.py:351
  8.6 12.2 %copy-start.12 = (bf16[512,256]{1,0:T(8,128)(2,1)S(1)}, bf16[512,256]{1,0:T(8,128)(2,1)}, u32[]{:S(2)}) copy-start(bf16[512,256]{1,0:T(8,128)(2,1)} %constant.78) | copy-start | bytes 786436
  8.6 12.2 %copy-start.13 = (bf16[512,256]{1,0:T(8,128)(2,1)S(1)}, bf16[512,256]{1,0:T(8,128)(2,1)}, u32[]{:S(2)}) copy-start(bf16[512,256]{1,0:T(8,128)(2,1)} %constant.79) | copy-start | bytes 786436
  8.6 24.8 %all-to-all-start = ((bf16[32,2,2112]{2,1,0:T(2,128)(2,1)}), bf16[32,2,2112]{2,1,0:T(2,128)(2,1)S(1)}, u32[]{:S(2)}, u32[]{:S(2)}) async-start(bf16[32,2,2112]{2,1,0:T(2,128)(2,1)} %reshape.83), calls=%async_computation | async-start | bytes 557056 | tf_op jit(solution)/shard_map/all_to_all | solution.py:343
  21.1 0.7 copy-start.18
  21.1 0.8 %copy-start.19 = (bf16[256,512]{1,0:T(8,128)(2,1)}, bf16[256,512]{1,0:T(8,128)(2,1)S(1)}, u32[]{:S(2)}) copy-start(bf16[256,512]{1,0:T(8,128)(2,1)S(1)} %collective-permute-done.soth_ref) | copy-start | bytes 786436
  33.4 1.1 %copy-start.8 = (f32[2,256,256]{2,1,0:T(8,128)S(1)}, f32[2,256,256]{2,1,0:T(8,128)}, u32[]{:S(2)}) copy-start(f32[2,256,256]{2,1,0:T(8,128)} %get-tuple-element.5.pr_ref) | copy-start | bytes 1572868
  33.7 1.0 %copy-start.2 = (bf16[512,256]{1,0:T(8,128)(2,1)S(1)}, bf16[512,256]{1,0:T(8,128)(2,1)}, u32[]{:S(2)}) copy-start(bf16[512,256]{1,0:T(8,128)(2,1)} %constant.64.clone.cs_ref) | copy-start | bytes 786436
  33.7 1.1 %copy-start.3 = (bf16[512,256]{1,0:T(8,128)(2,1)S(1)}, bf16[512,256]{1,0:T(8,128)(2,1)}, u32[]{:S(2)}) copy-start(bf16[512,256]{1,0:T(8,128)(2,1)} %constant.65.clone.ss_ref) | copy-start | bytes 786436
  33.7 1.1 %copy-start.5 = (bf16[256,256]{1,0:T(8,128)(2,1)S(1)}, bf16[256,256]{1,0:T(8,128)(2,1)}, u32[]{:S(2)}) copy-start(bf16[256,256]{1,0:T(8,128)(2,1)} %constant.61.clone.sf_ref) | copy-start | bytes 393220
  33.8 1.1 %copy-start.7 = (bf16[256,128]{1,0:T(8,128)(2,1)S(1)}, bf16[256,128]{1,0:T(8,128)(2,1)}, u32[]{:S(2)}) copy-start(bf16[256,128]{1,0:T(8,128)(2,1)} %constant.77.sfn_ref) | copy-start | bytes 196612
  34.1 1.1 %copy-start.1 = (f32[256,512]{1,0:T(8,128)S(1)}, f32[256,512]{1,0:T(8,128)}, u32[]{:S(2)}) copy-start(f32[256,512]{1,0:T(8,128)} %constant.63.clone.st_ref) | copy-start | bytes 1572868
  34.3 1.2 %copy-start = (f32[256,512]{1,0:T(8,128)S(1)}, f32[256,512]{1,0:T(8,128)}, u32[]{:S(2)}) copy-start(f32[256,512]{1,0:T(8,128)} %constant.62.clone.ct_ref) | copy-start | bytes 1572868
  34.4 1.1 %copy-start.4 = (bf16[256,256]{1,0:T(8,128)(2,1)S(1)}, bf16[256,256]{1,0:T(8,128)(2,1)}, u32[]{:S(2)}) copy-start(bf16[256,256]{1,0:T(8,128)(2,1)} %constant.60.clone.cf_ref) | copy-start | bytes 393220
  34.4 1.1 %copy-start.6 = (bf16[256,128]{1,0:T(8,128)(2,1)S(1)}, bf16[256,128]{1,0:T(8,128)(2,1)}, u32[]{:S(2)}) copy-start(bf16[256,128]{1,0:T(8,128)(2,1)} %constant.76.cfn_ref) | copy-start | bytes 196612
  35.5 1.0 %copy-start.9 = (f32[2,256,256]{2,1,0:T(8,128)S(1)}, f32[2,256,256]{2,1,0:T(8,128)}, u32[]{:S(2)}) copy-start(f32[2,256,256]{2,1,0:T(8,128)} %get-tuple-element.6.pi_ref) | copy-start | bytes 1572868
  36.5 1.0 %copy-start.10 = (f32[2,256,256]{2,1,0:T(8,128)S(1)}, f32[2,256,256]{2,1,0:T(8,128)}, u32[]{:S(2)}) copy-start(f32[2,256,256]{2,1,0:T(8,128)} %get-tuple-element.7.w2_ref) | copy-start | bytes 1572868
  54.8 1.3 %collective-permute-start.2 = (f32[6,512]{1,0:T(8,128)S(1)}, f32[6,512]{1,0:T(8,128)S(1)}, u32[]{:S(2)}, u32[]{:S(2)}) collective-permute-start(f32[6,512]{1,0:T(8,128)S(1)} %get-tuple-element.16), channel_id=1, source_target_pairs={{0,128},{128,0},{1,129},{129,1},{2,130},{130,2},{3,131},{131,3},{4... | collective-permute-start | bytes 36872 | tf_op jit(solution)/shard_map/ppermute | solution.py:357
  (2 other events, 1.4 us)

commit v9 on v8

--- a/solution.py
+++ b/solution.py
@@ -324,42 +324,41 @@
     n_blk = NFFT // BLK
     half_blk = n_blk // 2
     filt_count = lax.axis_size("filt")
-    capacity = (per_dev + filt_count - 1) // filt_count
-    positions = jnp.arange(per_dev, dtype=jnp.int32)
-    same_owner = owner[:, None] == owner[None, :]
-    earlier = positions[None, :] < positions[:, None]
-    owner_rank = jnp.sum(jnp.logical_and(same_owner, earlier).astype(jnp.int32), axis=1)
-    dest_slot = owner * capacity + owner_rank
-    slot_ids = jnp.arange(filt_count * capacity, dtype=jnp.int32)[:, None]
-    placing = slot_ids == dest_slot[None, :]
-    samples = jnp.arange(TL, dtype=jnp.int32)
-    windowed = jnp.where(
-        samples[None, :] < BLK * chirp_blocks[:, None], templates, jnp.zeros_like(templates)
-    )
-    payload = jnp.concatenate([windowed, jnp.ones((per_dev, 128), jnp.bfloat16)], axis=1)
-    send_rows = jnp.dot(
-        placing.astype(jnp.bfloat16), payload, preferred_element_type=jnp.float32
-    ).astype(jnp.bfloat16)
-    recv_rows = lax.all_to_all(send_rows, "filt", split_axis=0, concat_axis=0, tiled=True)
-    valid = recv_rows[:, TL] > 0.5
-    wanted = detector * mine + jnp.arange(mine, dtype=jnp.int32)
-    my_rows = compact(recv_rows[:, :TL], valid, wanted)
-    windowed = my_rows.reshape(mine, TL // N2, N2)
     swap = [(0, 1), (1, 0)]
     own_signal = strain[0].astype(jnp.bfloat16).reshape(N1, N2)
     own_weight = inv_asd[0].reshape(N2 // 2, N1)
     other_signal = lax.ppermute(own_signal, "det", swap)
     other_weight = lax.ppermute(own_weight, "det", swap)
+    samples = jnp.arange(TL, dtype=jnp.int32)
+    my_rows = lax.dynamic_slice_in_dim(templates, detector * mine, mine)
+    my_blocks = lax.dynamic_slice_in_dim(chirp_blocks, detector * mine, mine)
+    windowed = jnp.where(
+        samples[None, :] < BLK * my_blocks[:, None], my_rows, jnp.zeros_like(my_rows)
+    )
+    windowed = windowed.reshape(mine, TL // N2, N2)
     spectrum = spectra(tables, (own_signal, other_signal), (own_weight, other_weight), detector)
     full = filter_bank(windowed, tables, spectrum, slide[0])
     keep = lax.dynamic_slice_in_dim(full, detector * half_blk, half_blk, axis=1)
     give = lax.dynamic_slice_in_dim(full, (1 - detector) * half_blk, half_blk, axis=1)
     got = lax.ppermute(give, "det", swap)
-    peaks = jnp.where(
+    local = jnp.where(
         detector == 0, jnp.concatenate([keep, got], axis=0), jnp.concatenate([got, keep], axis=0)
     )
-    local_max = jnp.max(peaks, axis=0)
+    local_max = jnp.max(local, axis=0)
     loudest = group_max(local_max)
+    positions = jnp.arange(per_dev, dtype=jnp.int32)
+    slots = jnp.arange(filt_count, dtype=jnp.int32)
+    placing = owner[None, :] == slots[:, None]
+    source = jnp.sum(jnp.where(placing, positions[None, :], 0), axis=1)
+    used = jnp.any(placing, axis=1)
+    flagged = jnp.concatenate([local, jnp.ones((per_dev, 128), jnp.float32)], axis=1)
+    send_rows = jnp.where(used[:, None], jnp.take(flagged, source, axis=0), 0.0)
+    recv_rows = lax.all_to_all(send_rows, "filt", split_axis=0, concat_axis=0, tiled=True)
+    valid = recv_rows[:, half_blk] > 0.5
+    rank = jnp.cumsum(valid.astype(jnp.int32)) - 1
+    hits = jnp.logical_and(valid[None, :], rank[None, :] == positions[:, None])
+    pick = jnp.sum(jnp.where(hits, slots[None, :], 0), axis=1)
+    peaks = jnp.take(recv_rows[:, :half_blk], pick, axis=0)
     return (peaks, loudest)
 
 

time: 75.5 us -> 75 us (level)
  waiting for transfers between devices: 8.51 us -> 1.03 us
  local copies, waits for them, and re-layouts: 8.48 us -> 13.4 us
  Pallas kernels: 37.5 us -> 39.9 us
    all_to_all x1, waiting for transfers between devices: 7.34 us -> 0.01 us  [shards(): lax.all_to_all(send_rows, 'filt', split_axis=0, concat_axis=0, tiled=True)]
    unnamed x50 -> x48, local copies, waits for them, and re-layouts: 7.1 us -> 10.6 us
    pallas_call x1, Pallas kernels: 16.5 us -> 18.5 us  [group_max(): pl.pallas_call(functools.partial(loudest_kernel, stages), out_shape=jax.S...]
    gather x0 -> x2, local copies, waits for them, and re-layouts: none -> 1.17 us  [the longest x1 0.6 us: shards(): send_rows = jnp.where(used[:, None], jnp.take(flagged, source, axis=0), 0.0)]
    convert_element_type x1, other arithmetic: 1.38 us -> 2.4 us  [shards(): own_signal = strain[0].astype(jnp.bfloat16).reshape(N1, N2)]
    unnamed x1, other arithmetic: 2.28 us -> 1.29 us
  transfers between devices with their start and end apart: 4 -> 4, of which waited for: 2 -> 1; matrix products, arithmetic and copies ran while one was open for 6% -> 3% of each run, Pallas kernels for 6% -> 25%
where the time goes in v9:
time: 75 us; the launch traced here: 74 us
  Pallas kernels  39.9 us (53%)
  local copies, waits for them, and re-layouts  13.4 us (18%)
  starting transfers between devices  12.1 us (16%)
  other arithmetic  5.9 us (8%)
  between operations  1.66 us (2%)
  waiting for transfers between devices  1.03 us (1%)
    pallas_call x1, Pallas kernels, group_max(): pl.pallas_call(functools.partial(loudest_kernel, stages), out_shape=jax.S...  18.5 us
    pallas_call x1, Pallas kernels, filter_bank(): pl.pallas_call(filter_kernel, out_shape=jax.ShapeDtypeStruct((count, N1,...  17.1 us
    all_to_all x1, starting transfers between devices, shards(): lax.all_to_all(send_rows, 'filt', split_axis=0, concat_axis=0, tiled=True)  11.4 us
    unnamed x48, local copies, waits for them, and re-layouts  10.6 us
    pallas_call x1, Pallas kernels, spectra(): pl.pallas_call(spectrum_kernel, out_shape=(part, part, part), in_specs=[s...  4.32 us
    convert_element_type x1, other arithmetic, shards(): own_signal = strain[0].astype(jnp.bfloat16).reshape(N1, N2)  2.4 us
  transfers between devices with their start and end apart: 4, of which 1 were waited for; matrix products, arithmetic and copies ran while one was open for 3% of the time, Pallas kernels for 25%

profile of v9, /device:TPU:32, one launch (start us, length us, event | category | flops | bytes accessed | tf_op | source)
XLA Modules:
  0.0 74.0 jit_solution(5238697186020951356)
XLA Ops:
  0.6 2.4 %convert_reduce_fusion = bf16[131072]{0:T(1024)(128)(2,1)S(1)} fusion(f32[1,131072]{1,0:T(1,128)} %param.12), kind=kLoop, calls=%fused_computation.2 | loop fusion | flops 131072 | bytes 786432 | tf_op jit(solution)/shard_map/convert_element_type | solution.py:328
  4.0 1.3 %reduce.8 = f32[65536]{0:T(1024)S(1)} reduce(f32[1,65536]{1,0:T(1,128)S(1)} %copy-done.13, f32[]{:T(128)} %broadcast.102), dimensions={0}, to_apply=%param.13.reduce_sub_computation.3 | reduce | bytes 524292 | tf_op args[1]
  6.6 0.6 copy-done.21
  7.3 0.6 copy-done.20
  8.6 0.7 copy-done.18
  9.3 0.7 copy-done.19
  10.0 4.3 %shard_map.131 = (f32[2,256,256]{2,1,0:T(8,128)}, f32[2,256,256]{2,1,0:T(8,128)}, f32[2,256,256]{2,1,0:T(8,128)}) custom-call(s32[1]{0:T(128)} %bitcast.6.det_ref, f32[256,512]{1,0:T(8,128)} %constant.96.clone.ct_ref, f32[256,512]{1,0:T(8,128)} %constant.97.clone.st_ref, bf16[512,256]{1,0:T(8,128)(2,1)} %constant.98.clone.cs_ref, ...), custom_call_target="tpu_custom_call" | custom-call | flops 805306368 | bytes 4194304 | tf_op jit(solution)/shard_map/pallas_call | solution.py:191
  14.3 0.9 %copy-done.3 = bf16[512,256]{1,0:T(8,128)(2,1)S(1)} copy-done((bf16[512,256]{1,0:T(8,128)(2,1)S(1)}, bf16[512,256]{1,0:T(8,128)(2,1)}, u32[]{:S(2)}) %copy-start.3) | copy-done | bytes 262168
  15.3 0.9 %copy-done.5 = bf16[256,256]{1,0:T(8,128)(2,1)S(1)} copy-done((bf16[256,256]{1,0:T(8,128)(2,1)S(1)}, bf16[256,256]{1,0:T(8,128)(2,1)}, u32[]{:S(2)}) %copy-start.5) | copy-done | bytes 131096
  16.2 0.8 %copy-done.6 = bf16[256,128]{1,0:T(8,128)(2,1)S(1)} copy-done((bf16[256,128]{1,0:T(8,128)(2,1)S(1)}, bf16[256,128]{1,0:T(8,128)(2,1)}, u32[]{:S(2)}) %copy-start.6) | copy-done | bytes 65560
  17.0 0.8 %copy-done.7 = bf16[256,128]{1,0:T(8,128)(2,1)S(1)} copy-done((bf16[256,128]{1,0:T(8,128)(2,1)S(1)}, bf16[256,128]{1,0:T(8,128)(2,1)}, u32[]{:S(2)}) %copy-start.7) | copy-done | bytes 65560
  17.9 1.0 %copy-done.8 = f32[2,256,256]{2,1,0:T(8,128)S(1)} copy-done((f32[2,256,256]{2,1,0:T(8,128)S(1)}, f32[2,256,256]{2,1,0:T(8,128)}, u32[]{:S(2)}) %copy-start.8) | copy-done | bytes 524312
  18.9 1.0 %copy-done.9 = f32[2,256,256]{2,1,0:T(8,128)S(1)} copy-done((f32[2,256,256]{2,1,0:T(8,128)S(1)}, f32[2,256,256]{2,1,0:T(8,128)}, u32[]{:S(2)}) %copy-start.9) | copy-done | bytes 524312
  20.0 1.0 %copy-done.10 = f32[2,256,256]{2,1,0:T(8,128)S(1)} copy-done((f32[2,256,256]{2,1,0:T(8,128)S(1)}, f32[2,256,256]{2,1,0:T(8,128)}, u32[]{:S(2)}) %copy-start.10) | copy-done | bytes 524312
  21.0 17.1 %shard_map.132 = f32[6,256,4]{2,1,0:T(8,128)S(1)} custom-call(s32[1]{0:T(128)} %bitcast.1.scalar_ref, bf16[6,128,512]{2,1,0:T(8,128)(2,1)S(1)} %concatenate.16.x_ref, bf16[256,128]{1,0:T(8,128)(2,1)S(1)} %copy-done.7, bf16[256,128]{1,0:T(8,128)(2,1)S(1)} %copy-done.6, f32[256,512]{1,0:T(8,128)S(1)} %copy-done.1, f32[256,512]{1,0:T(8,128)S(1)} %copy-done, ...), custom_call_target="tpu_custom_call" | custom-call | flops 8455716864 | bytes 8388608 | tf_op jit(solution)/shard_map/pallas_call | solution.py:307
  38.8 1.0 %collective-permute-done.2 = f32[6,512]{1,0:T(8,128)S(1)} collective-permute-done((f32[6,512]{1,0:T(8,128)S(1)}, f32[6,512]{1,0:T(8,128)S(1)}, u32[]{:S(2)}, u32[]{:S(2)}) %collective-permute-start.2) | collective-permute-done | bytes 12320 | tf_op jit(solution)/shard_map/ppermute | solution.py:343
  39.8 0.6 fusion.5
  40.4 0.6 gather_fusion
  41.1 0.7 copy.15
  41.8 11.4 %all-to-all-start = ((f32[32,1,640]{2,1,0:T(1,128)}), f32[32,1,640]{2,1,0:T(1,128)S(1)}, u32[]{:S(2)}, u32[]{:S(2)}) async-start(f32[32,1,640]{2,1,0:T(1,128)} %copy.15), calls=%async_computation | async-start | bytes 163840 | tf_op jit(solution)/shard_map/all_to_all | solution.py:356
  53.2 18.5 %shard_map.133 = f32[1,512]{1,0:T(1,128)} custom-call(f32[1,512]{1,0:T(1,128)} %bitcast.38), custom_call_target="tpu_custom_call" | custom-call | tf_op jit(solution)/shard_map/pallas_call | solution.py:133
  72.2 0.6 gather_fusion.1
  72.7 0.7 broadcast_select_fusion
  73.4 0.6 copy.24
  (67 shorter events, 3.3 us)
Async XLA Ops:
  3.0 1.0 %copy-start.13 = (f32[1,65536]{1,0:T(1,128)S(1)}, f32[1,65536]{1,0:T(1,128)}, u32[]{:S(2)}) copy-start(f32[1,65536]{1,0:T(1,128)} %param.13) | copy-start | bytes 786436
  3.2 2.1 %copy-start.14 = (bf16[256,512]{1,0:T(8,128)(2,1)}, bf16[256,512]{1,0:T(8,128)(2,1)S(1)}, u32[]{:S(2)}) copy-start(bf16[256,512]{1,0:T(8,128)(2,1)S(1)} %convert_element_type.12.sown_ref) | copy-start | bytes 786436
  3.2 5.3 %collective-permute-start = (bf16[256,512]{1,0:T(8,128)(2,1)S(1)}, bf16[256,512]{1,0:T(8,128)(2,1)S(1)}, u32[]{:S(2)}, u32[]{:S(2)}) collective-permute-start(bf16[256,512]{1,0:T(8,128)(2,1)S(1)} %convert_element_type.12.sown_ref), channel_id=1, source_target_pairs={{0,128},{128,0},{1,129},{129,1},{2,130},{130,2},{3,131},{131,3},{4... | collective-permute-start | bytes 786440 | tf_op jit(solution)/shard_map/ppermute | solution.py:330
  4.0 4.0 %copy-start.16 = (bf16[12,4096]{1,0:T(8,128)(2,1)S(1)}, bf16[12,4096]{1,0:T(8,128)(2,1)}, u32[]{:S(2)}) copy-start(bf16[12,4096]{1,0:T(8,128)(2,1)} %param.14) | copy-start | bytes 294916
  5.3 2.8 %copy-start.11 = (bf16[512,256]{1,0:T(8,128)(2,1)S(1)}, bf16[512,256]{1,0:T(8,128)(2,1)}, u32[]{:S(2)}) copy-start(bf16[512,256]{1,0:T(8,128)(2,1)} %constant.113) | copy-start | bytes 786436
  5.3 2.8 %copy-start.12 = (bf16[512,256]{1,0:T(8,128)(2,1)S(1)}, bf16[512,256]{1,0:T(8,128)(2,1)}, u32[]{:S(2)}) copy-start(bf16[512,256]{1,0:T(8,128)(2,1)} %constant.112) | copy-start | bytes 786436
  5.4 2.9 %copy-start.15 = (f32[256,256]{1,0:T(8,128)}, f32[256,256]{1,0:T(8,128)S(1)}, u32[]{:S(2)}) copy-start(f32[256,256]{1,0:T(8,128)S(1)} %reshape_squeeze.3.wown_ref) | copy-start | bytes 786436
  5.4 3.2 %collective-permute-start.1 = (f32[256,256]{1,0:T(8,128)S(1)}, f32[256,256]{1,0:T(8,128)S(1)}, u32[]{:S(2)}, u32[]{:S(2)}) collective-permute-start(f32[256,256]{1,0:T(8,128)S(1)} %reshape_squeeze.3.wown_ref), channel_id=1, source_target_pairs={{0,128},{128,0},{1,129},{129,1},{2,130},{130,2},{3,131},{131,3},{4... | collective-permute-start | bytes 786440 | tf_op jit(solution)/shard_map/ppermute | solution.py:331
  8.6 0.7 copy-start.18
  9.3 0.7 copy-start.19
  10.0 4.3 %copy-start = (f32[256,512]{1,0:T(8,128)S(1)}, f32[256,512]{1,0:T(8,128)}, u32[]{:S(2)}) copy-start(f32[256,512]{1,0:T(8,128)} %constant.97.clone.st_ref) | copy-start | bytes 1572868
  10.0 4.3 %copy-start.1 = (f32[256,512]{1,0:T(8,128)S(1)}, f32[256,512]{1,0:T(8,128)}, u32[]{:S(2)}) copy-start(f32[256,512]{1,0:T(8,128)} %constant.96.clone.ct_ref) | copy-start | bytes 1572868
  10.0 4.3 %copy-start.2 = (bf16[512,256]{1,0:T(8,128)(2,1)S(1)}, bf16[512,256]{1,0:T(8,128)(2,1)}, u32[]{:S(2)}) copy-start(bf16[512,256]{1,0:T(8,128)(2,1)} %constant.99.clone.ss_ref) | copy-start | bytes 786436
  10.0 4.3 %copy-start.4 = (bf16[256,256]{1,0:T(8,128)(2,1)S(1)}, bf16[256,256]{1,0:T(8,128)(2,1)}, u32[]{:S(2)}) copy-start(bf16[256,256]{1,0:T(8,128)(2,1)} %constant.95.clone.sf_ref) | copy-start | bytes 393220
  14.3 1.0 %copy-start.3 = (bf16[512,256]{1,0:T(8,128)(2,1)S(1)}, bf16[512,256]{1,0:T(8,128)(2,1)}, u32[]{:S(2)}) copy-start(bf16[512,256]{1,0:T(8,128)(2,1)} %constant.98.clone.cs_ref) | copy-start | bytes 786436
  15.3 0.9 %copy-start.5 = (bf16[256,256]{1,0:T(8,128)(2,1)S(1)}, bf16[256,256]{1,0:T(8,128)(2,1)}, u32[]{:S(2)}) copy-start(bf16[256,256]{1,0:T(8,128)(2,1)} %constant.94.clone.cf_ref) | copy-start | bytes 393220
  16.2 0.8 %copy-start.6 = (bf16[256,128]{1,0:T(8,128)(2,1)S(1)}, bf16[256,128]{1,0:T(8,128)(2,1)}, u32[]{:S(2)}) copy-start(bf16[256,128]{1,0:T(8,128)(2,1)} %constant.111.sfn_ref) | copy-start | bytes 196612
  17.0 0.8 %copy-start.7 = (bf16[256,128]{1,0:T(8,128)(2,1)S(1)}, bf16[256,128]{1,0:T(8,128)(2,1)}, u32[]{:S(2)}) copy-start(bf16[256,128]{1,0:T(8,128)(2,1)} %constant.110.cfn_ref) | copy-start | bytes 196612
  17.9 1.0 %copy-start.8 = (f32[2,256,256]{2,1,0:T(8,128)S(1)}, f32[2,256,256]{2,1,0:T(8,128)}, u32[]{:S(2)}) copy-start(f32[2,256,256]{2,1,0:T(8,128)} %get-tuple-element.5.pr_ref) | copy-start | bytes 1572868
  18.9 1.0 %copy-start.9 = (f32[2,256,256]{2,1,0:T(8,128)S(1)}, f32[2,256,256]{2,1,0:T(8,128)}, u32[]{:S(2)}) copy-start(f32[2,256,256]{2,1,0:T(8,128)} %get-tuple-element.6.pi_ref) | copy-start | bytes 1572868
  20.0 1.0 %copy-start.10 = (f32[2,256,256]{2,1,0:T(8,128)S(1)}, f32[2,256,256]{2,1,0:T(8,128)}, u32[]{:S(2)}) copy-start(f32[2,256,256]{2,1,0:T(8,128)} %get-tuple-element.7.w2_ref) | copy-start | bytes 1572868
  38.5 1.3 %collective-permute-start.2 = (f32[6,512]{1,0:T(8,128)S(1)}, f32[6,512]{1,0:T(8,128)S(1)}, u32[]{:S(2)}, u32[]{:S(2)}) collective-permute-start(f32[6,512]{1,0:T(8,128)S(1)} %get-tuple-element.16), channel_id=1, source_target_pairs={{0,128},{128,0},{1,129},{129,1},{2,130},{130,2},{3,131},{131,3},{4... | collective-permute-start | bytes 36872 | tf_op jit(solution)/shard_map/ppermute | solution.py:343
  41.8 29.9 %all-to-all-start = ((f32[32,1,640]{2,1,0:T(1,128)}), f32[32,1,640]{2,1,0:T(1,128)S(1)}, u32[]{:S(2)}, u32[]{:S(2)}) async-start(f32[32,1,640]{2,1,0:T(1,128)} %copy.15), calls=%async_computation | async-start | bytes 163840 | tf_op jit(solution)/shard_map/all_to_all | solution.py:356
  72.7 0.7 copy-start.17
  (2 other events, 1.3 us)

commit v10 on v6

--- a/solution.py
+++ b/solution.py
@@ -17,12 +17,6 @@
 
 
 TWO_PI = 6.283185307179586
-
-
-def partner_2(value, axis, stride):
-    mask = 2**stride
-    pairs = [(source, source ^ mask) for source in range(lax.axis_size(axis))]
-    return lax.ppermute(value, axis, pairs)
 
 
 def angle_table(rows, cols, period):
@@ -50,23 +44,15 @@
     )
 
 
-def compact(rows, valid, wanted):
-    slot_rank = jnp.cumsum(valid.astype(jnp.int32)) - 1
-    picker = jnp.logical_and(valid[None, :], slot_rank[None, :] == wanted[:, None])
-    return jnp.dot(picker.astype(jnp.bfloat16), rows, preferred_element_type=jnp.float32).astype(
-        jnp.bfloat16
-    )
-
-
-def stage_layout(n_grp, n_filt):
-    inner = 8 if n_filt % 8 == 0 else n_filt
-    return ((inner, 1), (n_filt // inner, inner), (n_grp, 0))
-
-
-def loudest_kernel(stages, local_ref, out_ref, acc_ref, *scratch):
+def route_kernel(
+    stages, send_ref, local_ref, recv_out, out_ref, recv_buf, slot_send, slot_recv, acc_ref,
+    *scratch,
+):
     det = lax.axis_index("det")
     grp = lax.axis_index("grp")
     filt = lax.axis_index("filt")
+    n_grp = lax.axis_size("grp")
+    n_filt = send_ref.shape[0]
     mesh_ids = pl.DeviceIdType.MESH
 
     def position(size, stride):
@@ -80,16 +66,28 @@
         here = position(size, stride)
         return (det, grp, filt + (target - here) * stride)
 
+    barrier = pltpu.get_barrier_semaphore()
+    for i in range(n_filt - 1):
+        target = lax.rem(filt + 1 + i, n_filt)
+        pl.semaphore_signal(barrier, inc=1, device_id=(det, grp, target), device_id_type=mesh_ids)
+    for i in range(n_grp - 1):
+        target = lax.rem(grp + 1 + i, n_grp)
+        pl.semaphore_signal(barrier, inc=1, device_id=(det, target, filt), device_id_type=mesh_ids)
+    pl.semaphore_wait(barrier, n_filt - 1 + n_grp - 1)
+    slots = []
+    for i in range(n_filt - 1):
+        target = lax.rem(filt + 1 + i, n_filt)
+        copy = pltpu.make_async_remote_copy(
+            src_ref=send_ref.at[target],
+            dst_ref=recv_buf.at[filt],
+            send_sem=slot_send.at[i],
+            recv_sem=slot_recv.at[filt],
+            device_id=(det, grp, target),
+            device_id_type=mesh_ids,
+        )
+        copy.start()
+        slots.append(copy)
     live = [(size, stride) for size, stride in stages if size > 1]
-    barrier = pltpu.get_barrier_semaphore()
-    for size, stride in live:
-        here = position(size, stride)
-        for i in range(size - 1):
-            target = lax.rem(here + 1 + i, size)
-            pl.semaphore_signal(
-                barrier, inc=1, device_id=peer(size, stride, target), device_id_type=mesh_ids
-            )
-    pl.semaphore_wait(barrier, sum(size - 1 for size, _ in live))
     value = local_ref[...]
     source = local_ref
     for k, (size, stride) in enumerate(live):
@@ -117,28 +115,57 @@
             acc_ref[k] = value
             source = acc_ref.at[k]
     out_ref[...] = value
-
-
-def group_max(local_max):
+    for copy in slots:
+        copy.wait_send()
+    for i in range(n_filt - 1):
+        origin = lax.rem(filt + 1 + i, n_filt)
+        pltpu.make_async_remote_copy(
+            src_ref=send_ref.at[origin],
+            dst_ref=recv_buf.at[origin],
+            send_sem=slot_send.at[i],
+            recv_sem=slot_recv.at[origin],
+            device_id=(det, grp, origin),
+            device_id_type=mesh_ids,
+        ).wait_recv()
+    recv_buf[filt] = send_ref[filt]
+    recv_out[...] = recv_buf[...]
+
+
+def stage_layout(n_grp, n_filt):
+    inner = 8 if n_filt % 8 == 0 else n_filt
+    return ((inner, 1), (n_filt // inner, inner), (n_grp, 0))
+
+
+def route_and_max(send_rows, local_max):
     stages = stage_layout(lax.axis_size("grp"), lax.axis_size("filt"))
     live = [size for size, _ in stages if size > 1]
     width = local_max.shape[-1]
-    scratch = [pltpu.VMEM((max(len(live), 1), 1, width), jnp.float32)]
+    n_filt = send_rows.shape[0]
+    scratch = [
+        pltpu.VMEM(send_rows.shape, send_rows.dtype),
+        pltpu.SemaphoreType.DMA((n_filt,)),
+        pltpu.SemaphoreType.DMA((n_filt,)),
+        pltpu.VMEM((max(len(live), 1), 1, width), jnp.float32),
+    ]
     for size in live:
         scratch += [
             pltpu.VMEM((size - 1, 1, width), jnp.float32),
             pltpu.SemaphoreType.DMA((size - 1,)),
             pltpu.SemaphoreType.DMA((size - 1,)),
         ]
-    out = pl.pallas_call(
-        functools.partial(loudest_kernel, stages),
-        out_shape=jax.ShapeDtypeStruct((1, width), jnp.float32),
-        in_specs=[pl.BlockSpec(memory_space=pltpu.VMEM)],
-        out_specs=pl.BlockSpec(memory_space=pltpu.VMEM),
+    vmem = pl.BlockSpec(memory_space=pltpu.VMEM)
+    recv, out = pl.pallas_call(
+        functools.partial(route_kernel, stages),
+        out_shape=(
+            jax.ShapeDtypeStruct(send_rows.shape, send_rows.dtype),
+            jax.ShapeDtypeStruct((1, width), jnp.float32),
+        ),
+        in_specs=[vmem, vmem],
+        out_specs=(vmem, vmem),
         scratch_shapes=scratch,
         compiler_params=pltpu.CompilerParams(collective_id=0, has_side_effects=True),
-    )(local_max.reshape(1, width))
-    return out.reshape(width)
+    )(send_rows, local_max.reshape(1, width))
+    return recv, out.reshape(width)
 
 
 def dot_nt(left, right):
@@ -298,32 +325,18 @@
     n_blk = NFFT // BLK
     half_blk = n_blk // 2
     filt_count = lax.axis_size("filt")
-    capacity = (per_dev + filt_count - 1) // filt_count
-    positions = jnp.arange(per_dev, dtype=jnp.int32)
-    same_owner = owner[:, None] == owner[None, :]
-    earlier = positions[None, :] < positions[:, None]
-    owner_rank = jnp.sum(jnp.logical_and(same_owner, earlier).astype(jnp.int32), axis=1)
-    dest_slot = owner * capacity + owner_rank
-    slot_ids = jnp.arange(filt_count * capacity, dtype=jnp.int32)[:, None]
-    placing = slot_ids == dest_slot[None, :]
-    samples = jnp.arange(TL, dtype=jnp.int32)
-    windowed = jnp.where(
-        samples[None, :] < BLK * chirp_blocks[:, None], templates, jnp.zeros_like(templates)
-    )
-    payload = jnp.concatenate([windowed, jnp.ones((per_dev, 128), jnp.bfloat16)], axis=1)
-    send_rows = jnp.dot(
-        placing.astype(jnp.bfloat16), payload, preferred_element_type=jnp.float32
-    ).astype(jnp.bfloat16)
-    recv_rows = lax.all_to_all(send_rows, "filt", split_axis=0, concat_axis=0, tiled=True)
-    valid = recv_rows[:, TL] > 0.5
-    wanted = detector * mine + jnp.arange(mine, dtype=jnp.int32)
-    my_rows = compact(recv_rows[:, :TL], valid, wanted)
-    windowed = my_rows.reshape(mine, TL // N2, N2)
     swap = [(0, 1), (1, 0)]
     own_signal = strain[0].astype(jnp.bfloat16).reshape(N1, N2)
     own_weight = inv_asd[0].reshape(N2 // 2, N1)
     other_signal = lax.ppermute(own_signal, "det", swap)
     other_weight = lax.ppermute(own_weight, "det", swap)
+    samples = jnp.arange(TL, dtype=jnp.int32)
+    my_rows = lax.dynamic_slice_in_dim(templates, detector * mine, mine)
+    my_blocks = lax.dynamic_slice_in_dim(chirp_blocks, detector * mine, mine)
+    windowed = jnp.where(
+        samples[None, :] < BLK * my_blocks[:, None], my_rows, jnp.zeros_like(my_rows)
+    )
+    windowed = windowed.reshape(mine, TL // N2, N2)
     full = filter_bank(
         windowed, tables, (own_signal, other_signal), (own_weight, other_weight),
         slide[0], detector,
@@ -331,11 +344,24 @@
     keep = lax.dynamic_slice_in_dim(full, detector * half_blk, half_blk, axis=1)
     give = lax.dynamic_slice_in_dim(full, (1 - detector) * half_blk, half_blk, axis=1)
     got = lax.ppermute(give, "det", swap)
-    peaks = jnp.where(
+    local = jnp.where(
         detector == 0, jnp.concatenate([keep, got], axis=0), jnp.concatenate([got, keep], axis=0)
     )
-    local_max = jnp.max(peaks, axis=0)
-    loudest = group_max(local_max)
+    local_max = jnp.max(local, axis=0)
+    positions = jnp.arange(per_dev, dtype=jnp.int32)
+    slots = jnp.arange(filt_count, dtype=jnp.int32)
+    placing = owner[None, :] == slots[:, None]
+    source = jnp.sum(jnp.where(placing, positions[None, :], 0), axis=1)
+    used = jnp.any(placing, axis=1)
+    flagged = jnp.concatenate([local, jnp.ones((per_dev, 128), jnp.float32)], axis=1)
+    send_rows = jnp.where(used[:, None], jnp.take(flagged, source, axis=0), 0.0)
+    recv_rows, loudest = route_and_max(send_rows[:, None, :], local_max)
+    recv_rows = recv_rows.reshape(filt_count, half_blk + 128)
+    valid = recv_rows[:, half_blk] > 0.5
+    rank = jnp.cumsum(valid.astype(jnp.int32)) - 1
+    hits = jnp.logical_and(valid[None, :], rank[None, :] == positions[:, None])
+    pick = jnp.sum(jnp.where(hits, slots[None, :], 0), axis=1)
+    peaks = jnp.take(recv_rows[:, :half_blk], pick, axis=0)
     return (peaks, loudest)
 
 

time: 71.4 us -> 65.6 us (0.919)
  starting transfers between devices: 12.2 us -> 0.78 us
  waiting for transfers between devices: 8.61 us -> 1.15 us
  local copies, waits for them, and re-layouts: 5.49 us -> 12.7 us
  Pallas kernels: 35.8 us -> 42.6 us
  other arithmetic: 6.93 us -> 5.94 us
    all_to_all x1 -> x0, starting transfers between devices: 11.5 us -> none  [shards(): lax.all_to_all(send_rows, 'filt', split_axis=0, concat_axis=0, tiled=True)]
    all_to_all x1 -> x0, waiting for transfers between devices: 7.44 us -> none  [shards(): lax.all_to_all(send_rows, 'filt', split_axis=0, concat_axis=0, tiled=True)]
    pallas_call x1, Pallas kernels: 16.5 us -> 23.2 us  [route_and_max(): pl.pallas_call(functools.partial(route_kernel, stages), out_shape=(jax.Sh...]
    unnamed x34, local copies, waits for them, and re-layouts: 4.12 us -> 9.93 us
    gather x0 -> x2, local copies, waits for them, and re-layouts: none -> 1.17 us  [the longest x1 0.6 us: shards(): send_rows = jnp.where(used[:, None], jnp.take(flagged, source, axis=0), 0.0)]
    unnamed x1, other arithmetic: 1.32 us -> 2.28 us
    all_to_all x1 -> x0, other arithmetic: 0.75 us -> none  [shards(): lax.all_to_all(send_rows, 'filt', split_axis=0, concat_axis=0, tiled=True)]
  transfers between devices with their start and end apart: 4 -> 3, of which waited for: 2 -> 1; matrix products, arithmetic and copies ran while one was open for 6% -> 3% of each run, Pallas kernels for 0% -> 0%
where the time goes in v10:
time: 65.6 us; the launch traced here: 64.7 us
  Pallas kernels  42.6 us (65%)
  local copies, waits for them, and re-layouts  12.7 us (19%)
  other arithmetic  5.94 us (9%)
  between operations  1.59 us (2%)
  waiting for transfers between devices  1.15 us (2%)
  starting transfers between devices  0.78 us (1%)
    pallas_call x1, Pallas kernels, route_and_max(): pl.pallas_call(functools.partial(route_kernel, stages), out_shape=(jax.Sh...  23.2 us
    pallas_call x1, Pallas kernels, filter_bank(): pl.pallas_call(filter_kernel, out_shape=jax.ShapeDtypeStruct((count, N1,...  19.3 us
    unnamed x34, local copies, waits for them, and re-layouts  9.93 us
    unnamed x1, other arithmetic  2.28 us
    convert_element_type x1, other arithmetic, shards(): own_signal = strain[0].astype(jnp.bfloat16).reshape(N1, N2)  1.38 us
  transfers between devices with their start and end apart: 3, of which 1 were waited for; matrix products, arithmetic and copies ran while one was open for 3% of the time, Pallas kernels for 0%

profile of v10, /device:TPU:32, one launch (start us, length us, event | category | flops | bytes accessed | tf_op | source)
XLA Modules:
  0.0 64.7 jit_solution(12531396200485394069)
XLA Ops:
  0.6 0.5 broadcast.102
  1.1 2.3 %reduce.8 = f32[65536]{0:T(1024)S(1)} reduce(f32[1,65536]{1,0:T(1,128)} %param.13, f32[]{:T(128)} %broadcast.102), dimensions={0}, to_apply=%param.13.reduce_sub_computation.3 | reduce | bytes 524292 | tf_op args[1]
  3.6 1.4 %convert_reduce_fusion = bf16[131072]{0:T(1024)(128)(2,1)S(1)} fusion(f32[1,131072]{1,0:T(1,128)S(1)} %copy-done.8), kind=kLoop, calls=%fused_computation.2 | loop fusion | flops 131072 | bytes 786432 | tf_op jit(solution)/shard_map/convert_element_type | solution.py:329
  5.2 0.6 collective-permute-start
  6.5 0.6 copy-done.13
  7.6 0.7 %copy-done.14 = s32[12]{0:T(128)S(1)} copy-done((s32[12]{0:T(128)S(1)}, s32[12]{0:T(128)}, u32[]{:S(2)}) %copy-start.14) | copy-done | bytes 72
  8.7 0.8 %copy-done.2 = bf16[512,256]{1,0:T(8,128)(2,1)S(1)} copy-done((bf16[512,256]{1,0:T(8,128)(2,1)S(1)}, bf16[512,256]{1,0:T(8,128)(2,1)}, u32[]{:S(2)}) %copy-start.2) | copy-done | bytes 262168
  9.6 1.0 %copy-done = f32[256,512]{1,0:T(8,128)S(1)} copy-done((f32[256,512]{1,0:T(8,128)S(1)}, f32[256,512]{1,0:T(8,128)}, u32[]{:S(2)}) %copy-start) | copy-done | bytes 524312
  10.6 1.0 %copy-done.1 = f32[256,512]{1,0:T(8,128)S(1)} copy-done((f32[256,512]{1,0:T(8,128)S(1)}, f32[256,512]{1,0:T(8,128)}, u32[]{:S(2)}) %copy-start.1) | copy-done | bytes 524312
  11.7 0.9 %copy-done.3 = bf16[512,256]{1,0:T(8,128)(2,1)S(1)} copy-done((bf16[512,256]{1,0:T(8,128)(2,1)S(1)}, bf16[512,256]{1,0:T(8,128)(2,1)}, u32[]{:S(2)}) %copy-start.3) | copy-done | bytes 262168
  12.6 0.9 %copy-done.5 = bf16[256,256]{1,0:T(8,128)(2,1)S(1)} copy-done((bf16[256,256]{1,0:T(8,128)(2,1)S(1)}, bf16[256,256]{1,0:T(8,128)(2,1)}, u32[]{:S(2)}) %copy-start.5) | copy-done | bytes 131096
  13.5 0.8 %copy-done.6 = bf16[256,128]{1,0:T(8,128)(2,1)S(1)} copy-done((bf16[256,128]{1,0:T(8,128)(2,1)S(1)}, bf16[256,128]{1,0:T(8,128)(2,1)}, u32[]{:S(2)}) %copy-start.6) | copy-done | bytes 65560
  14.4 0.8 %copy-done.7 = bf16[256,128]{1,0:T(8,128)(2,1)S(1)} copy-done((bf16[256,128]{1,0:T(8,128)(2,1)S(1)}, bf16[256,128]{1,0:T(8,128)(2,1)}, u32[]{:S(2)}) %copy-start.7) | copy-done | bytes 65560
  15.2 19.3 %shard_map.131 = f32[6,256,4]{2,1,0:T(8,128)S(1)} custom-call(s32[2]{0:T(128)S(1)} %pad_add_fusion.scalar_ref, bf16[6,128,512]{2,1,0:T(8,128)(2,1)S(1)} %concatenate.16.x_ref, bf16[256,128]{1,0:T(8,128)(2,1)S(1)} %copy-done.6, bf16[256,128]{1,0:T(8,128)(2,1)S(1)} %copy-done.7, f32[256,512]{1,0:T(8,128)S(1)} %copy-done, f32[256,512]{1,0:T(8,128)S(1)} %copy-done.1, ...), custom_call_target="tpu_custom_call" | custom-call | flops 8455716864 | bytes 8388608 | tf_op jit(solution)/shard_map/pallas_call | solution.py:308
  34.6 0.4 reshape.92
  35.1 1.1 %collective-permute-done.2 = f32[6,512]{1,0:T(8,128)S(1)} collective-permute-done((f32[6,512]{1,0:T(8,128)S(1)}, f32[6,512]{1,0:T(8,128)S(1)}, u32[]{:S(2)}, u32[]{:S(2)}) %collective-permute-start.2) | collective-permute-done | bytes 12320 | tf_op jit(solution)/shard_map/ppermute | solution.py:346
  36.3 0.6 fusion.6
  36.9 0.6 gather_fusion
  37.6 0.7 %broadcast_in_dim.81.send_ref = f32[32,1,640]{2,1,0:T(1,128)} reshape(f32[32,640]{1,0:T(8,128)S(1)} %select_select_fusion) | data formatting | bytes 163840 | tf_op jit(solution)/shard_map/broadcast_in_dim | solution.py:358
  38.2 23.2 %shard_map.132 = (f32[32,1,640]{2,1,0:T(1,128)}, f32[1,512]{1,0:T(1,128)}) custom-call(f32[32,1,640]{2,1,0:T(1,128)} %broadcast_in_dim.81.send_ref, f32[1,512]{1,0:T(1,128)} %bitcast.36), custom_call_target="tpu_custom_call" | custom-call | tf_op jit(solution)/shard_map/pallas_call | solution.py:157
  61.5 0.9 %copy.18 = f32[32,1,640]{2,0,1:T(8,128)S(1)} copy(f32[32,1,640]{2,1,0:T(1,128)} %get-tuple-element.4) | data formatting | bytes 163840
  62.9 0.6 gather_fusion.1
  63.4 0.7 %broadcast_select_fusion = f32[12,512]{1,0:T(8,128)} fusion(f32[12,512]{1,0:T(8,128)S(1)} %gather_fusion.1, pred[12]{0:T(512)(128)(4,1)S(1)} %compare_and_fusion), kind=kLoop, calls=%fused_computation.16 | loop fusion | flops 6144 | bytes 49164 | tf_op jit(solution)/shard_map/jit(_take)/select_n | solution.py:364
  64.1 0.6 copy.22
  (51 shorter events, 1.9 us)
Async XLA Ops:
  1.1 2.5 %copy-start.8 = (f32[1,131072]{1,0:T(1,128)S(1)}, f32[1,131072]{1,0:T(1,128)}, u32[]{:S(2)}) copy-start(f32[1,131072]{1,0:T(1,128)} %param.12) | copy-start | bytes 1572868
  3.5 5.2 %collective-permute-start.1 = (f32[256,256]{1,0:T(8,128)S(1)}, f32[256,256]{1,0:T(8,128)S(1)}, u32[]{:S(2)}, u32[]{:S(2)}) collective-permute-start(f32[256,256]{1,0:T(8,128)S(1)} %reshape_squeeze.3.wown_ref), channel_id=1, source_target_pairs={{0,128},{128,0},{1,129},{129,1},{2,130},{130,2},{3,131},{131,3},{4... | collective-permute-start | bytes 786440 | tf_op jit(solution)/shard_map/ppermute | solution.py:332
  5.0 2.3 %copy-start.9 = (bf16[512,256]{1,0:T(8,128)(2,1)S(1)}, bf16[512,256]{1,0:T(8,128)(2,1)}, u32[]{:S(2)}) copy-start(bf16[512,256]{1,0:T(8,128)(2,1)} %constant.112) | copy-start | bytes 786436
  5.0 2.3 %copy-start.10 = (bf16[512,256]{1,0:T(8,128)(2,1)S(1)}, bf16[512,256]{1,0:T(8,128)(2,1)}, u32[]{:S(2)}) copy-start(bf16[512,256]{1,0:T(8,128)(2,1)} %constant.113) | copy-start | bytes 786436
  5.2 3.5 %collective-permute-start = (bf16[256,512]{1,0:T(8,128)(2,1)S(1)}, bf16[256,512]{1,0:T(8,128)(2,1)S(1)}, u32[]{:S(2)}, u32[]{:S(2)}) collective-permute-start(bf16[256,512]{1,0:T(8,128)(2,1)S(1)} %convert_element_type.12.sown_ref), channel_id=1, source_target_pairs={{0,128},{128,0},{1,129},{129,1},{2,130},{130,2},{3,131},{131,3},{4... | collective-permute-start | bytes 786440 | tf_op jit(solution)/shard_map/ppermute | solution.py:331
  6.5 0.7 %copy-start.13 = (s32[12]{0:T(128)S(1)}, s32[12]{0:T(128)}, u32[]{:S(2)}) copy-start(s32[12]{0:T(128)} %param.16) | copy-start | bytes 148
  7.5 0.9 %copy-start.11 = (bf16[12,4096]{1,0:T(8,128)(2,1)S(1)}, bf16[12,4096]{1,0:T(8,128)(2,1)}, u32[]{:S(2)}) copy-start(bf16[12,4096]{1,0:T(8,128)(2,1)} %param.14) | copy-start | bytes 294916
  7.6 0.7 %copy-start.14 = (s32[12]{0:T(128)S(1)}, s32[12]{0:T(128)}, u32[]{:S(2)}) copy-start(s32[12]{0:T(128)} %param.15) | copy-start | bytes 148
  8.6 1.0 %copy-start.2 = (bf16[512,256]{1,0:T(8,128)(2,1)S(1)}, bf16[512,256]{1,0:T(8,128)(2,1)}, u32[]{:S(2)}) copy-start(bf16[512,256]{1,0:T(8,128)(2,1)} %constant.98.clone.cs_ref) | copy-start | bytes 786436
  8.6 1.0 %copy-start.4 = (bf16[256,256]{1,0:T(8,128)(2,1)S(1)}, bf16[256,256]{1,0:T(8,128)(2,1)}, u32[]{:S(2)}) copy-start(bf16[256,256]{1,0:T(8,128)(2,1)} %constant.94.clone.cf_ref) | copy-start | bytes 393220
  9.6 1.0 %copy-start = (f32[256,512]{1,0:T(8,128)S(1)}, f32[256,512]{1,0:T(8,128)}, u32[]{:S(2)}) copy-start(f32[256,512]{1,0:T(8,128)} %constant.96.clone.ct_ref) | copy-start | bytes 1572868
  10.6 1.0 %copy-start.1 = (f32[256,512]{1,0:T(8,128)S(1)}, f32[256,512]{1,0:T(8,128)}, u32[]{:S(2)}) copy-start(f32[256,512]{1,0:T(8,128)} %constant.97.clone.st_ref) | copy-start | bytes 1572868
  11.7 0.9 %copy-start.3 = (bf16[512,256]{1,0:T(8,128)(2,1)S(1)}, bf16[512,256]{1,0:T(8,128)(2,1)}, u32[]{:S(2)}) copy-start(bf16[512,256]{1,0:T(8,128)(2,1)} %constant.99.clone.ss_ref) | copy-start | bytes 786436
  12.6 0.9 %copy-start.5 = (bf16[256,256]{1,0:T(8,128)(2,1)S(1)}, bf16[256,256]{1,0:T(8,128)(2,1)}, u32[]{:S(2)}) copy-start(bf16[256,256]{1,0:T(8,128)(2,1)} %constant.95.clone.sf_ref) | copy-start | bytes 393220
  13.5 0.8 %copy-start.6 = (bf16[256,128]{1,0:T(8,128)(2,1)S(1)}, bf16[256,128]{1,0:T(8,128)(2,1)}, u32[]{:S(2)}) copy-start(bf16[256,128]{1,0:T(8,128)(2,1)} %constant.110.cfn_ref) | copy-start | bytes 196612
  14.4 0.8 %copy-start.7 = (bf16[256,128]{1,0:T(8,128)(2,1)S(1)}, bf16[256,128]{1,0:T(8,128)(2,1)}, u32[]{:S(2)}) copy-start(bf16[256,128]{1,0:T(8,128)(2,1)} %constant.111.sfn_ref) | copy-start | bytes 196612
  35.0 1.3 %collective-permute-start.2 = (f32[6,512]{1,0:T(8,128)S(1)}, f32[6,512]{1,0:T(8,128)S(1)}, u32[]{:S(2)}, u32[]{:S(2)}) collective-permute-start(f32[6,512]{1,0:T(8,128)S(1)} %get-tuple-element.14), channel_id=1, source_target_pairs={{0,128},{128,0},{1,129},{129,1},{2,130},{130,2},{3,131},{131,3},{4... | collective-permute-start | bytes 36872 | tf_op jit(solution)/shard_map/ppermute | solution.py:346
  63.4 0.7 %copy-start.12 = (f32[1,512]{1,0:T(1,128)S(1)}, f32[1,512]{1,0:T(1,128)}, u32[]{:S(2)}) copy-start(f32[1,512]{1,0:T(1,128)} %get-tuple-element.5) | copy-start | bytes 6148

commit v11 on v10

--- a/solution.py
+++ b/solution.py
@@ -174,11 +174,14 @@
     )
 
 
-def filter_kernel(
-    scalar_ref, x_ref, cfn_ref, sfn_ref, ct_ref, st_ref, cs_ref, ss_ref, cf_ref, sf_ref,
-    cfr_ref, sfr_ref, sown_ref, soth_ref, wown_ref, woth_ref, out_ref,
-    er_ref, ei_ref, pr_ref, pi_ref, w2_ref,
-):
+def filter_kernel(scalar_ref, x_ref, *refs):
+    count = 14
+    sources = refs[:count]
+    out_ref, er_ref, ei_ref, pr_ref, pi_ref, w2_ref = refs[count:count + 6]
+    held = refs[count + 6:2 * count + 6]
+    fetch_sems = refs[2 * count + 6]
+    (cfn_ref, sfn_ref, ct_ref, st_ref, cs_ref, ss_ref, cf_ref, sf_ref,
+     cfr_ref, sfr_ref, sown_ref, soth_ref, wown_ref, woth_ref) = held
     f32 = jnp.float32
     bf16 = jnp.bfloat16
 
@@ -201,6 +204,14 @@
 
     @pl.when(pl.program_id(0) == 0)
     def _():
+        fetches = [
+            pltpu.make_async_copy(src, dst, fetch_sems.at[k])
+            for k, (src, dst) in enumerate(zip(sources, held))
+        ]
+        for fetch in fetches:
+            fetch.start()
+        for fetch in fetches:
+            fetch.wait()
         det = scalar_ref[1]
         for slot, sig_ref, w_ref in ((det, sown_ref, wown_ref), (1 - det, soth_ref, woth_ref)):
             real_s, imag_s = first_stage(cf_ref[...], sf_ref[...], sig_ref[...])
@@ -286,15 +297,12 @@
         signals[0], signals[1], weights[0], weights[1],
     ]
 
-    def whole(array):
-        nd = array.ndim
-        return pl.BlockSpec(array.shape, lambda i, r, nd=nd: (0,) * nd)
 
     grid_spec = pltpu.PrefetchScalarGridSpec(
         num_scalar_prefetch=1,
         grid=(count,),
         in_specs=[pl.BlockSpec((1, pad_rows, width), lambda i, r: (i, 0, 0))]
-        + [whole(a) for a in operands],
+        + [pl.BlockSpec(memory_space=pl.ANY)] * len(operands),
         out_specs=pl.BlockSpec((1, N1, tiles), lambda i, r: (i, 0, 0)),
         scratch_shapes=[
             pltpu.VMEM((N1, N2), jnp.bfloat16),
@@ -302,14 +310,16 @@
             pltpu.VMEM((2, N1, N2 // 2), jnp.float32),
             pltpu.VMEM((2, N1, N2 // 2), jnp.float32),
             pltpu.VMEM((2, N1, N2 // 2), jnp.float32),
-        ],
+        ]
+        + [pltpu.VMEM(a.shape, a.dtype) for a in operands]
+        + [pltpu.SemaphoreType.DMA((len(operands),))],
     )
     matmuls = 2 * N1 * pad_rows * N2 + 4 * N1 * N2 * (N2 // 2) + 16 * N1 * (N2 // 2) * N2
     out = pl.pallas_call(
         filter_kernel,
         out_shape=jax.ShapeDtypeStruct((count, N1, tiles), jnp.float32),
         grid_spec=grid_spec,
-        compiler_params=pltpu.CompilerParams(vmem_limit_bytes=48 * 1024 * 1024),
+        compiler_params=pltpu.CompilerParams(vmem_limit_bytes=56 * 1024 * 1024),
         cost_estimate=pl.CostEstimate(
             flops=2 * matmuls * count, transcendentals=0, bytes_accessed=8 * 1024 * 1024
         ),

time: 65.6 us -> 67 us (1.021)
  local copies, waits for them, and re-layouts: 12.7 us -> 9.48 us
  Pallas kernels: 42.6 us -> 45.5 us
  other arithmetic: 5.94 us -> 7.83 us
    unnamed x34 -> x26, local copies, waits for them, and re-layouts: 9.93 us -> 4.74 us
    pallas_call x1, Pallas kernels: 19.3 us -> 22.2 us  [filter_bank(): pl.pallas_call(filter_kernel, out_shape=jax.ShapeDtypeStruct((count, N1,...]
    reshape x1, local copies, waits for them, and re-layouts: 0.43 us -> 1.56 us  [filter_bank(): return out.reshape(count, N1 * tiles)]
    concatenate x1, local copies, waits for them, and re-layouts: 0.06 us -> 0.95 us  [filter_bank(): jnp.concatenate([windowed, jnp.zeros((count, pad_rows - rows_used, width)...]
    another operation x1, other arithmetic: 0.03 us -> 0.73 us  [filter_bank(): jnp.stack([lax.dynamic_slice_in_dim(doubled_sin, quot + v, N1) for v in r...]
    another operation x1, other arithmetic: 0.03 us -> 0.73 us  [filter_bank(): jnp.stack([lax.dynamic_slice_in_dim(doubled_cos, quot + v, N1) for v in r...]
  transfers between devices with their start and end apart: 3 -> 3, of which waited for: 1 -> 1; matrix products, arithmetic and copies ran while one was open for 3% -> 8% of each run, Pallas kernels for 0% -> 0%
where the time goes in v11:
time: 67 us; the launch traced here: 66.3 us
  Pallas kernels  45.5 us (68%)
  local copies, waits for them, and re-layouts  9.48 us (14%)
  other arithmetic  7.83 us (12%)
  between operations  1.56 us (2%)
  waiting for transfers between devices  1.15 us (2%)
  starting transfers between devices  0.78 us (1%)
    pallas_call x1, Pallas kernels, route_and_max(): pl.pallas_call(functools.partial(route_kernel, stages), out_shape=(jax.Sh...  23.2 us
    pallas_call x1, Pallas kernels, filter_bank(): pl.pallas_call(filter_kernel, out_shape=jax.ShapeDtypeStruct((count, N1,...  22.2 us
    unnamed x26, local copies, waits for them, and re-layouts  4.74 us
    unnamed x1, other arithmetic  2.28 us
    reshape x1, local copies, waits for them, and re-layouts, filter_bank(): return out.reshape(count, N1 * tiles)  1.56 us
    convert_element_type x1, other arithmetic, shards(): own_signal = strain[0].astype(jnp.bfloat16).reshape(N1, N2)  1.38 us
  transfers between devices with their start and end apart: 3, of which 1 were waited for; matrix products, arithmetic and copies ran while one was open for 8% of the time, Pallas kernels for 0%

profile of v11, /device:TPU:32, one launch (start us, length us, event | category | flops | bytes accessed | tf_op | source)
XLA Modules:
  0.0 66.3 jit_solution(10316822685308705825)
XLA Ops:
  0.6 0.5 broadcast.102
  1.1 2.3 %reduce.8 = f32[65536]{0:T(1024)S(1)} reduce(f32[1,65536]{1,0:T(1,128)} %param.13, f32[]{:T(128)} %broadcast.102), dimensions={0}, to_apply=%param.13.reduce_sub_computation.3 | reduce | bytes 524292 | tf_op args[1]
  3.6 1.4 %convert_reduce_fusion = bf16[131072]{0:T(1024)(128)(2,1)S(1)} fusion(f32[1,131072]{1,0:T(1,128)S(1)} %copy-done), kind=kLoop, calls=%fused_computation.2 | loop fusion | flops 131072 | bytes 786432 | tf_op jit(solution)/shard_map/convert_element_type | solution.py:339
  5.1 0.2 convert_element_type.12.refs_10_
  5.2 0.6 collective-permute-start
  6.5 0.6 copy-done.9
  7.5 0.7 %pad_maximum_fusion.refs_8_ = bf16[2,256,256]{2,1,0:T(8,128)(2,1)} fusion(bf16[1,256,256]{2,1,0:T(8,128)(2,1)S(1)} %get-tuple-element.16, bf16[1,256,256]{2,1,0:T(8,128)(2,1)S(1)} %get-tuple-element.17), kind=kLoop, calls=%fused_computation.3 | loop fusion | flops 131072 | bytes 524288 | tf_op jit(solution)/shard_map/stack | solution.py:288
  8.2 0.7 %pad_maximum_fusion.1.refs_9_ = bf16[2,256,256]{2,1,0:T(8,128)(2,1)} fusion(bf16[1,256,256]{2,1,0:T(8,128)(2,1)S(1)} %get-tuple-element.11, bf16[1,256,256]{2,1,0:T(8,128)(2,1)S(1)} %get-tuple-element.10), kind=kLoop, calls=%fused_computation.4 | loop fusion | flops 131072 | bytes 524288 | tf_op jit(solution)/shard_map/stack | solution.py:291
  9.0 0.7 copy-done.10
  9.8 0.6 pad_add_fusion.scalar_ref
  10.4 0.9 %concatenate.16.x_ref = bf16[6,128,512]{2,1,0:T(8,128)(2,1)} pad(bf16[6,8,512]{2,1,0:T(8,128)(2,1)S(1)} %bitcast.35, bf16[]{:T(256)} %constant.80.clone.1), padding=0_0x0_120x0_0 | pad | bytes 835586 | tf_op jit(solution)/shard_map/concatenate | solution.py:280
  11.4 0.7 %copy-done.7 = f32[256,256]{1,0:T(8,128)} copy-done((f32[256,256]{1,0:T(8,128)}, f32[256,256]{1,0:T(8,128)S(1)}, u32[]{:S(2)}) %copy-start.7) | copy-done | bytes 262168
  12.1 0.7 %copy-done.8 = bf16[256,512]{1,0:T(8,128)(2,1)} copy-done((bf16[256,512]{1,0:T(8,128)(2,1)}, bf16[256,512]{1,0:T(8,128)(2,1)S(1)}, u32[]{:S(2)}) %copy-start.8) | copy-done | bytes 262168
  12.8 22.2 %shard_map.131 = f32[6,256,4]{2,1,0:T(8,128)} custom-call(s32[2]{0:T(128)} %pad_add_fusion.scalar_ref, bf16[6,128,512]{2,1,0:T(8,128)(2,1)} %concatenate.16.x_ref, bf16[256,128]{1,0:T(8,128)(2,1)} %constant.110.refs_0_, bf16[256,128]{1,0:T(8,128)(2,1)} %constant.111.refs_1_, f32[256,512]{1,0:T(8,128)} %constant.96.clone.refs_2_, ...), custom_call_target="tpu_custom_call" | custom-call | flops 8455716864 | bytes 8388608 | tf_op jit(solution)/shard_map/pallas_call | solution.py:318
  35.0 1.6 %reshape.92 = f32[6,1024]{1,0:T(8,128)S(1)} reshape(f32[6,256,4]{2,1,0:T(8,128)} %shard_map.131) | data formatting | bytes 49152 | tf_op jit(solution)/shard_map/reshape | solution.py:327
  36.7 1.1 %collective-permute-done.2 = f32[6,512]{1,0:T(8,128)S(1)} collective-permute-done((f32[6,512]{1,0:T(8,128)S(1)}, f32[6,512]{1,0:T(8,128)S(1)}, u32[]{:S(2)}, u32[]{:S(2)}) %collective-permute-start.2) | collective-permute-done | bytes 12320 | tf_op jit(solution)/shard_map/ppermute | solution.py:356
  37.8 0.6 fusion.6
  38.4 0.6 gather_fusion
  39.1 0.7 %broadcast_in_dim.81.send_ref = f32[32,1,640]{2,1,0:T(1,128)} reshape(f32[32,640]{1,0:T(8,128)S(1)} %select_select_fusion) | data formatting | bytes 163840 | tf_op jit(solution)/shard_map/broadcast_in_dim | solution.py:368
  39.8 23.2 %shard_map.132 = (f32[32,1,640]{2,1,0:T(1,128)}, f32[1,512]{1,0:T(1,128)}) custom-call(f32[32,1,640]{2,1,0:T(1,128)} %broadcast_in_dim.81.send_ref, f32[1,512]{1,0:T(1,128)} %bitcast.36), custom_call_target="tpu_custom_call" | custom-call | tf_op jit(solution)/shard_map/pallas_call | solution.py:157
  63.1 0.9 %copy.18 = f32[32,1,640]{2,0,1:T(8,128)S(1)} copy(f32[32,1,640]{2,1,0:T(1,128)} %get-tuple-element.4) | data formatting | bytes 163840
  64.4 0.6 gather_fusion.1
  65.0 0.7 %broadcast_select_fusion = f32[12,512]{1,0:T(8,128)} fusion(f32[12,512]{1,0:T(8,128)S(1)} %gather_fusion.1, pred[12]{0:T(512)(128)(4,1)S(1)} %compare_and_fusion), kind=kLoop, calls=%fused_computation.16 | loop fusion | flops 6144 | bytes 49164 | tf_op jit(solution)/shard_map/jit(_take)/select_n | solution.py:374
  65.7 0.6 copy.22
  (43 shorter events, 1.4 us)
Async XLA Ops:
  1.1 2.5 %copy-start = (f32[1,131072]{1,0:T(1,128)S(1)}, f32[1,131072]{1,0:T(1,128)}, u32[]{:S(2)}) copy-start(f32[1,131072]{1,0:T(1,128)} %param.12) | copy-start | bytes 1572868
  3.5 1.5 %copy-start.3 = (f32[256,256]{1,0:T(8,128)}, f32[256,256]{1,0:T(8,128)S(1)}, u32[]{:S(2)}) copy-start(f32[256,256]{1,0:T(8,128)S(1)} %reshape_squeeze.3.refs_12_) | copy-start | bytes 786436
  3.5 7.8 %collective-permute-start.1 = (f32[256,256]{1,0:T(8,128)S(1)}, f32[256,256]{1,0:T(8,128)S(1)}, u32[]{:S(2)}, u32[]{:S(2)}) collective-permute-start(f32[256,256]{1,0:T(8,128)S(1)} %reshape_squeeze.3.refs_12_), channel_id=1, source_target_pairs={{0,128},{128,0},{1,129},{129,1},{2,130},{130,2},{3,131},{131,3},{4... | collective-permute-start | bytes 786440 | tf_op jit(solution)/shard_map/ppermute | solution.py:342
  5.0 2.3 %copy-start.1 = (bf16[512,256]{1,0:T(8,128)(2,1)S(1)}, bf16[512,256]{1,0:T(8,128)(2,1)}, u32[]{:S(2)}) copy-start(bf16[512,256]{1,0:T(8,128)(2,1)} %constant.112) | copy-start | bytes 786436
  5.0 2.3 %copy-start.2 = (bf16[512,256]{1,0:T(8,128)(2,1)S(1)}, bf16[512,256]{1,0:T(8,128)(2,1)}, u32[]{:S(2)}) copy-start(bf16[512,256]{1,0:T(8,128)(2,1)} %constant.113) | copy-start | bytes 786436
  5.2 2.3 %copy-start.4 = (bf16[256,512]{1,0:T(8,128)(2,1)}, bf16[256,512]{1,0:T(8,128)(2,1)S(1)}, u32[]{:S(2)}) copy-start(bf16[256,512]{1,0:T(8,128)(2,1)S(1)} %convert_element_type.12.refs_10_) | copy-start | bytes 786436
  5.2 6.1 %collective-permute-start = (bf16[256,512]{1,0:T(8,128)(2,1)S(1)}, bf16[256,512]{1,0:T(8,128)(2,1)S(1)}, u32[]{:S(2)}, u32[]{:S(2)}) collective-permute-start(bf16[256,512]{1,0:T(8,128)(2,1)S(1)} %convert_element_type.12.refs_10_), channel_id=1, source_target_pairs={{0,128},{128,0},{1,129},{129,1},{2,130},{130,2},{3,131},{131,3},{4... | collective-permute-start | bytes 786440 | tf_op jit(solution)/shard_map/ppermute | solution.py:341
  6.5 0.7 copy-start.9
  8.2 1.5 %copy-start.5 = (bf16[12,4096]{1,0:T(8,128)(2,1)S(1)}, bf16[12,4096]{1,0:T(8,128)(2,1)}, u32[]{:S(2)}) copy-start(bf16[12,4096]{1,0:T(8,128)(2,1)} %param.14) | copy-start | bytes 294916
  9.0 0.7 copy-start.10
  11.3 0.7 %copy-start.7 = (f32[256,256]{1,0:T(8,128)}, f32[256,256]{1,0:T(8,128)S(1)}, u32[]{:S(2)}) copy-start(f32[256,256]{1,0:T(8,128)S(1)} %collective-permute-done.1.refs_13_) | copy-start | bytes 786436
  12.1 0.7 %copy-start.8 = (bf16[256,512]{1,0:T(8,128)(2,1)}, bf16[256,512]{1,0:T(8,128)(2,1)S(1)}, u32[]{:S(2)}) copy-start(bf16[256,512]{1,0:T(8,128)(2,1)S(1)} %collective-permute-done.refs_11_) | copy-start | bytes 786436
  36.6 1.3 %collective-permute-start.2 = (f32[6,512]{1,0:T(8,128)S(1)}, f32[6,512]{1,0:T(8,128)S(1)}, u32[]{:S(2)}, u32[]{:S(2)}) collective-permute-start(f32[6,512]{1,0:T(8,128)S(1)} %get-tuple-element.14), channel_id=1, source_target_pairs={{0,128},{128,0},{1,129},{129,1},{2,130},{130,2},{3,131},{131,3},{4... | collective-permute-start | bytes 36872 | tf_op jit(solution)/shard_map/ppermute | solution.py:356
  65.0 0.7 %copy-start.6 = (f32[1,512]{1,0:T(1,128)S(1)}, f32[1,512]{1,0:T(1,128)}, u32[]{:S(2)}) copy-start(f32[1,512]{1,0:T(1,128)} %get-tuple-element.5) | copy-start | bytes 6148

commit v12 on v10

--- a/solution.py
+++ b/solution.py
@@ -45,8 +45,8 @@
 
 
 def route_kernel(
-    stages, send_ref, local_ref, recv_out, out_ref, recv_buf, slot_send, slot_recv, acc_ref,
-    *scratch,
+    split, send_ref, recv_out, out_ref, recv_buf, slot_send, slot_recv, acc_ref,
+    held, grp_send, grp_recv,
 ):
     det = lax.axis_index("det")
     grp = lax.axis_index("grp")
@@ -54,18 +54,6 @@
     n_grp = lax.axis_size("grp")
     n_filt = send_ref.shape[0]
     mesh_ids = pl.DeviceIdType.MESH
-
-    def position(size, stride):
-        if stride == 0:
-            return grp
-        return lax.rem(filt // stride, size)
-
-    def peer(size, stride, target):
-        if stride == 0:
-            return (det, target, filt)
-        here = position(size, stride)
-        return (det, grp, filt + (target - here) * stride)
-
     barrier = pltpu.get_barrier_semaphore()
     for i in range(n_filt - 1):
         target = lax.rem(filt + 1 + i, n_filt)
@@ -87,34 +75,6 @@
         )
         copy.start()
         slots.append(copy)
-    live = [(size, stride) for size, stride in stages if size > 1]
-    value = local_ref[...]
-    source = local_ref
-    for k, (size, stride) in enumerate(live):
-        held, send_sems, recv_sems = scratch[3 * k:3 * k + 3]
-        here = position(size, stride)
-        copies = []
-        for i in range(size - 1):
-            target = lax.rem(here + 1 + i, size)
-            row = size - 2 - i
-            copy = pltpu.make_async_remote_copy(
-                src_ref=source,
-                dst_ref=held.at[row],
-                send_sem=send_sems.at[i],
-                recv_sem=recv_sems.at[row],
-                device_id=peer(size, stride, target),
-                device_id_type=mesh_ids,
-            )
-            copy.start()
-            copies.append(copy)
-        for copy in copies:
-            copy.wait_send()
-            copy.wait_recv()
-        value = jnp.maximum(value, jnp.max(held[...], axis=0))
-        if k + 1 < len(live):
-            acc_ref[k] = value
-            source = acc_ref.at[k]
-    out_ref[...] = value
     for copy in slots:
         copy.wait_send()
     for i in range(n_filt - 1):
@@ -128,43 +88,56 @@
             device_id_type=mesh_ids,
         ).wait_recv()
     recv_buf[filt] = send_ref[filt]
-    recv_out[...] = recv_buf[...]
-
-
-def stage_layout(n_grp, n_filt):
-    inner = 8 if n_filt % 8 == 0 else n_filt
-    return ((inner, 1), (n_filt // inner, inner), (n_grp, 0))
-
-
-def route_and_max(send_rows, local_max):
-    stages = stage_layout(lax.axis_size("grp"), lax.axis_size("filt"))
-    live = [size for size, _ in stages if size > 1]
-    width = local_max.shape[-1]
+    rows = recv_buf[...]
+    recv_out[...] = rows
+    value = jnp.max(rows[:, :, split:], axis=0)
+    if n_grp > 1:
+        acc_ref[...] = value
+        copies = []
+        for i in range(n_grp - 1):
+            target = lax.rem(grp + 1 + i, n_grp)
+            row = n_grp - 2 - i
+            copy = pltpu.make_async_remote_copy(
+                src_ref=acc_ref,
+                dst_ref=held.at[row],
+                send_sem=grp_send.at[i],
+                recv_sem=grp_recv.at[row],
+                device_id=(det, target, filt),
+                device_id_type=mesh_ids,
+            )
+            copy.start()
+            copies.append(copy)
+        for copy in copies:
+            copy.wait_send()
+            copy.wait_recv()
+        value = jnp.maximum(value, jnp.max(held[...], axis=0))
+    out_ref[...] = value
+
+
+def route_and_max(send_rows, split):
+    n_grp = lax.axis_size("grp")
     n_filt = send_rows.shape[0]
-    scratch = [
-        pltpu.VMEM(send_rows.shape, send_rows.dtype),
-        pltpu.SemaphoreType.DMA((n_filt,)),
-        pltpu.SemaphoreType.DMA((n_filt,)),
-        pltpu.VMEM((max(len(live), 1), 1, width), jnp.float32),
-    ]
-    for size in live:
-        scratch += [
-            pltpu.VMEM((size - 1, 1, width), jnp.float32),
-            pltpu.SemaphoreType.DMA((size - 1,)),
-            pltpu.SemaphoreType.DMA((size - 1,)),
-        ]
+    width = send_rows.shape[-1] - split
     vmem = pl.BlockSpec(memory_space=pltpu.VMEM)
     recv, out = pl.pallas_call(
-        functools.partial(route_kernel, stages),
+        functools.partial(route_kernel, split),
         out_shape=(
             jax.ShapeDtypeStruct(send_rows.shape, send_rows.dtype),
             jax.ShapeDtypeStruct((1, width), jnp.float32),
         ),
-        in_specs=[vmem, vmem],
+        in_specs=[vmem],
         out_specs=(vmem, vmem),
-        scratch_shapes=scratch,
+        scratch_shapes=[
+            pltpu.VMEM(send_rows.shape, send_rows.dtype),
+            pltpu.SemaphoreType.DMA((n_filt,)),
+            pltpu.SemaphoreType.DMA((n_filt,)),
+            pltpu.VMEM((1, width), jnp.float32),
+            pltpu.VMEM((max(n_grp - 1, 1), 1, width), jnp.float32),
+            pltpu.SemaphoreType.DMA((max(n_grp - 1, 1),)),
+            pltpu.SemaphoreType.DMA((max(n_grp - 1, 1),)),
+        ],
         compiler_params=pltpu.CompilerParams(collective_id=0, has_side_effects=True),
-    )(send_rows, local_max.reshape(1, width))
+    )(send_rows)
     return recv, out.reshape(width)
 
 
@@ -326,8 +299,8 @@
     half_blk = n_blk // 2
     filt_count = lax.axis_size("filt")
     swap = [(0, 1), (1, 0)]
-    own_signal = strain[0].astype(jnp.bfloat16).reshape(N1, N2)
-    own_weight = inv_asd[0].reshape(N2 // 2, N1)
+    own_signal = strain.reshape(N1, N2).astype(jnp.bfloat16)
+    own_weight = inv_asd.reshape(N2 // 2, N1)
     other_signal = lax.ppermute(own_signal, "det", swap)
     other_weight = lax.ppermute(own_weight, "det", swap)
     samples = jnp.arange(TL, dtype=jnp.int32)
@@ -355,8 +328,12 @@
     used = jnp.any(placing, axis=1)
     flagged = jnp.concatenate([local, jnp.ones((per_dev, 128), jnp.float32)], axis=1)
     send_rows = jnp.where(used[:, None], jnp.take(flagged, source, axis=0), 0.0)
-    recv_rows, loudest = route_and_max(send_rows[:, None, :], local_max)
-    recv_rows = recv_rows.reshape(filt_count, half_blk + 128)
+    split = half_blk + 128
+    send_rows = jnp.concatenate(
+        [send_rows, jnp.broadcast_to(local_max[None, :], (filt_count, half_blk))], axis=1
+    )
+    recv_rows, loudest = route_and_max(send_rows[:, None, :], split)
+    recv_rows = recv_rows.reshape(filt_count, split + half_blk)
     valid = recv_rows[:, half_blk] > 0.5
     rank = jnp.cumsum(valid.astype(jnp.int32)) - 1
     hits = jnp.logical_and(valid[None, :], rank[None, :] == positions[:, None])

time: 65.6 us -> 63.3 us (0.965)
  Pallas kernels: 42.6 us -> 40.5 us
    pallas_call x1, Pallas kernels: 23.2 us -> 21.2 us  [route_and_max(): pl.pallas_call(functools.partial(route_kernel, split), out_shape=(jax.Sha...]
  transfers between devices with their start and end apart: 3 -> 3, of which waited for: 1 -> 1; matrix products, arithmetic and copies ran while one was open for 3% -> 4% of each run, Pallas kernels for 0% -> 0%
where the time goes in v12:
time: 63.3 us; the launch traced here: 62.2 us
  Pallas kernels  40.5 us (64%)
  local copies, waits for them, and re-layouts  12.8 us (20%)
  other arithmetic  5.38 us (8%)
  between operations  1.62 us (3%)
  waiting for transfers between devices  1.16 us (2%)
  starting transfers between devices  0.77 us (1%)
    pallas_call x1, Pallas kernels, route_and_max(): pl.pallas_call(functools.partial(route_kernel, split), out_shape=(jax.Sha...  21.2 us
    pallas_call x1, Pallas kernels, filter_bank(): pl.pallas_call(filter_kernel, out_shape=jax.ShapeDtypeStruct((count, N1,...  19.3 us
    unnamed x34, local copies, waits for them, and re-layouts  9.96 us
    unnamed x1, other arithmetic  2.28 us
    convert_element_type x1, other arithmetic, shards(): own_signal = strain.reshape(N1, N2).astype(jnp.bfloat16)  1.38 us
  transfers between devices with their start and end apart: 3, of which 1 were waited for; matrix products, arithmetic and copies ran while one was open for 4% of the time, Pallas kernels for 0%

profile of v12, /device:TPU:32, one launch (start us, length us, event | category | flops | bytes accessed | tf_op | source)
XLA Modules:
  0.0 62.2 jit_solution(9639105888802691164)
XLA Ops:
  0.6 0.5 broadcast.105
  1.1 2.3 %reduce.8 = f32[65536]{0:T(1024)S(1)} reduce(f32[1,65536]{1,0:T(1,128)} %param.13, f32[]{:T(128)} %broadcast.105), dimensions={0}, to_apply=%param.13.reduce_sub_computation.3 | reduce | bytes 524292 | tf_op args[1]
  3.6 1.4 %convert_reduce_fusion = bf16[131072]{0:T(1024)(128)(2,1)S(1)} fusion(f32[1,131072]{1,0:T(1,128)S(1)} %copy-done.8), kind=kLoop, calls=%fused_computation.2 | loop fusion | flops 131072 | bytes 786432 | tf_op jit(solution)/shard_map/convert_element_type | solution.py:302
  5.0 0.2 convert_element_type.10.sown_ref
  5.2 0.6 collective-permute-start
  6.5 0.6 %copy-done.13 = s32[12]{0:T(128)S(1)} copy-done((s32[12]{0:T(128)S(1)}, s32[12]{0:T(128)}, u32[]{:S(2)}) %copy-start.13) | copy-done | bytes 72
  7.6 0.7 %copy-done.14 = s32[12]{0:T(128)S(1)} copy-done((s32[12]{0:T(128)S(1)}, s32[12]{0:T(128)}, u32[]{:S(2)}) %copy-start.14) | copy-done | bytes 72
  8.7 0.8 %copy-done.2 = bf16[512,256]{1,0:T(8,128)(2,1)S(1)} copy-done((bf16[512,256]{1,0:T(8,128)(2,1)S(1)}, bf16[512,256]{1,0:T(8,128)(2,1)}, u32[]{:S(2)}) %copy-start.2) | copy-done | bytes 262168
  9.6 1.0 %copy-done = f32[256,512]{1,0:T(8,128)S(1)} copy-done((f32[256,512]{1,0:T(8,128)S(1)}, f32[256,512]{1,0:T(8,128)}, u32[]{:S(2)}) %copy-start) | copy-done | bytes 524312
  10.6 1.0 %copy-done.1 = f32[256,512]{1,0:T(8,128)S(1)} copy-done((f32[256,512]{1,0:T(8,128)S(1)}, f32[256,512]{1,0:T(8,128)}, u32[]{:S(2)}) %copy-start.1) | copy-done | bytes 524312
  11.7 0.9 %copy-done.3 = bf16[512,256]{1,0:T(8,128)(2,1)S(1)} copy-done((bf16[512,256]{1,0:T(8,128)(2,1)S(1)}, bf16[512,256]{1,0:T(8,128)(2,1)}, u32[]{:S(2)}) %copy-start.3) | copy-done | bytes 262168
  12.6 0.9 %copy-done.5 = bf16[256,256]{1,0:T(8,128)(2,1)S(1)} copy-done((bf16[256,256]{1,0:T(8,128)(2,1)S(1)}, bf16[256,256]{1,0:T(8,128)(2,1)}, u32[]{:S(2)}) %copy-start.5) | copy-done | bytes 131096
  13.5 0.8 %copy-done.6 = bf16[256,128]{1,0:T(8,128)(2,1)S(1)} copy-done((bf16[256,128]{1,0:T(8,128)(2,1)S(1)}, bf16[256,128]{1,0:T(8,128)(2,1)}, u32[]{:S(2)}) %copy-start.6) | copy-done | bytes 65560
  14.4 0.8 %copy-done.7 = bf16[256,128]{1,0:T(8,128)(2,1)S(1)} copy-done((bf16[256,128]{1,0:T(8,128)(2,1)S(1)}, bf16[256,128]{1,0:T(8,128)(2,1)}, u32[]{:S(2)}) %copy-start.7) | copy-done | bytes 65560
  15.2 19.3 %shard_map.131 = f32[6,256,4]{2,1,0:T(8,128)S(1)} custom-call(s32[2]{0:T(128)S(1)} %pad_add_fusion.scalar_ref, bf16[6,128,512]{2,1,0:T(8,128)(2,1)S(1)} %concatenate.19.x_ref, bf16[256,128]{1,0:T(8,128)(2,1)S(1)} %copy-done.6, bf16[256,128]{1,0:T(8,128)(2,1)S(1)} %copy-done.7, f32[256,512]{1,0:T(8,128)S(1)} %copy-done, f32[256,512]{1,0:T(8,128)S(1)} %copy-done.1, ...), custom_call_target="tpu_custom_call" | custom-call | flops 8455716864 | bytes 8388608 | tf_op jit(solution)/shard_map/pallas_call | solution.py:281
  34.6 0.4 reshape.93
  35.1 1.2 %collective-permute-done.2 = f32[6,512]{1,0:T(8,128)S(1)} collective-permute-done((f32[6,512]{1,0:T(8,128)S(1)}, f32[6,512]{1,0:T(8,128)S(1)}, u32[]{:S(2)}, u32[]{:S(2)}) %collective-permute-start.2) | collective-permute-done | bytes 12320 | tf_op jit(solution)/shard_map/ppermute | solution.py:319
  36.3 0.6 gather_fusion
  37.0 0.8 %broadcast_in_dim.88.send_ref = f32[32,1,1152]{2,1,0:T(1,128)} reshape(f32[32,1152]{1,0:T(8,128)S(1)} %pad_maximum_fusion.2) | data formatting | bytes 294912 | tf_op jit(solution)/shard_map/broadcast_in_dim | solution.py:335
  37.8 21.2 %shard_map.132 = (f32[32,1,1152]{2,1,0:T(1,128)}, f32[1,512]{1,0:T(1,128)}) custom-call(f32[32,1,1152]{2,1,0:T(1,128)} %broadcast_in_dim.88.send_ref), custom_call_target="tpu_custom_call" | custom-call | tf_op jit(solution)/shard_map/pallas_call | solution.py:122
  59.0 0.9 %copy.18 = f32[32,1,1152]{2,0,1:T(8,128)S(1)} copy(f32[32,1,1152]{2,1,0:T(1,128)} %get-tuple-element.4) | data formatting | bytes 294912
  60.3 0.6 gather_fusion.1
  60.9 0.7 %broadcast_select_fusion = f32[12,512]{1,0:T(8,128)} fusion(f32[12,512]{1,0:T(8,128)S(1)} %gather_fusion.1, pred[12]{0:T(512)(128)(4,1)S(1)} %compare_and_fusion), kind=kLoop, calls=%fused_computation.17 | loop fusion | flops 6144 | bytes 49164 | tf_op jit(solution)/shard_map/jit(_take)/select_n | solution.py:341
  61.6 0.6 copy.22
  (53 shorter events, 1.7 us)
Async XLA Ops:
  1.1 2.5 %copy-start.8 = (f32[1,131072]{1,0:T(1,128)S(1)}, f32[1,131072]{1,0:T(1,128)}, u32[]{:S(2)}) copy-start(f32[1,131072]{1,0:T(1,128)} %param.12) | copy-start | bytes 1572868
  3.5 5.2 %collective-permute-start.1 = (f32[256,256]{1,0:T(8,128)S(1)}, f32[256,256]{1,0:T(8,128)S(1)}, u32[]{:S(2)}, u32[]{:S(2)}) collective-permute-start(f32[256,256]{1,0:T(8,128)S(1)} %reshape.92.wown_ref), channel_id=1, source_target_pairs={{0,128},{128,0},{1,129},{129,1},{2,130},{130,2},{3,131},{131,3},{4... | collective-permute-start | bytes 786440 | tf_op jit(solution)/shard_map/ppermute | solution.py:305
  5.0 2.3 %copy-start.9 = (bf16[512,256]{1,0:T(8,128)(2,1)S(1)}, bf16[512,256]{1,0:T(8,128)(2,1)}, u32[]{:S(2)}) copy-start(bf16[512,256]{1,0:T(8,128)(2,1)} %constant.112) | copy-start | bytes 786436
  5.0 2.3 %copy-start.10 = (bf16[512,256]{1,0:T(8,128)(2,1)S(1)}, bf16[512,256]{1,0:T(8,128)(2,1)}, u32[]{:S(2)}) copy-start(bf16[512,256]{1,0:T(8,128)(2,1)} %constant.113) | copy-start | bytes 786436
  5.2 3.5 %collective-permute-start = (bf16[256,512]{1,0:T(8,128)(2,1)S(1)}, bf16[256,512]{1,0:T(8,128)(2,1)S(1)}, u32[]{:S(2)}, u32[]{:S(2)}) collective-permute-start(bf16[256,512]{1,0:T(8,128)(2,1)S(1)} %convert_element_type.10.sown_ref), channel_id=1, source_target_pairs={{0,128},{128,0},{1,129},{129,1},{2,130},{130,2},{3,131},{131,3},{4... | collective-permute-start | bytes 786440 | tf_op jit(solution)/shard_map/ppermute | solution.py:304
  6.5 0.7 %copy-start.13 = (s32[12]{0:T(128)S(1)}, s32[12]{0:T(128)}, u32[]{:S(2)}) copy-start(s32[12]{0:T(128)} %param.16) | copy-start | bytes 148
  7.5 0.9 %copy-start.11 = (bf16[12,4096]{1,0:T(8,128)(2,1)S(1)}, bf16[12,4096]{1,0:T(8,128)(2,1)}, u32[]{:S(2)}) copy-start(bf16[12,4096]{1,0:T(8,128)(2,1)} %param.14) | copy-start | bytes 294916
  7.6 0.7 %copy-start.14 = (s32[12]{0:T(128)S(1)}, s32[12]{0:T(128)}, u32[]{:S(2)}) copy-start(s32[12]{0:T(128)} %param.15) | copy-start | bytes 148
  8.6 1.0 %copy-start.2 = (bf16[512,256]{1,0:T(8,128)(2,1)S(1)}, bf16[512,256]{1,0:T(8,128)(2,1)}, u32[]{:S(2)}) copy-start(bf16[512,256]{1,0:T(8,128)(2,1)} %constant.98.clone.cs_ref) | copy-start | bytes 786436
  8.6 1.0 %copy-start.4 = (bf16[256,256]{1,0:T(8,128)(2,1)S(1)}, bf16[256,256]{1,0:T(8,128)(2,1)}, u32[]{:S(2)}) copy-start(bf16[256,256]{1,0:T(8,128)(2,1)} %constant.94.clone.cf_ref) | copy-start | bytes 393220
  9.6 1.0 %copy-start = (f32[256,512]{1,0:T(8,128)S(1)}, f32[256,512]{1,0:T(8,128)}, u32[]{:S(2)}) copy-start(f32[256,512]{1,0:T(8,128)} %constant.96.clone.ct_ref) | copy-start | bytes 1572868
  10.6 1.0 %copy-start.1 = (f32[256,512]{1,0:T(8,128)S(1)}, f32[256,512]{1,0:T(8,128)}, u32[]{:S(2)}) copy-start(f32[256,512]{1,0:T(8,128)} %constant.97.clone.st_ref) | copy-start | bytes 1572868
  11.7 0.9 %copy-start.3 = (bf16[512,256]{1,0:T(8,128)(2,1)S(1)}, bf16[512,256]{1,0:T(8,128)(2,1)}, u32[]{:S(2)}) copy-start(bf16[512,256]{1,0:T(8,128)(2,1)} %constant.99.clone.ss_ref) | copy-start | bytes 786436
  12.6 0.9 %copy-start.5 = (bf16[256,256]{1,0:T(8,128)(2,1)S(1)}, bf16[256,256]{1,0:T(8,128)(2,1)}, u32[]{:S(2)}) copy-start(bf16[256,256]{1,0:T(8,128)(2,1)} %constant.95.clone.sf_ref) | copy-start | bytes 393220
  13.5 0.8 %copy-start.6 = (bf16[256,128]{1,0:T(8,128)(2,1)S(1)}, bf16[256,128]{1,0:T(8,128)(2,1)}, u32[]{:S(2)}) copy-start(bf16[256,128]{1,0:T(8,128)(2,1)} %constant.110.cfn_ref) | copy-start | bytes 196612
  14.4 0.8 %copy-start.7 = (bf16[256,128]{1,0:T(8,128)(2,1)S(1)}, bf16[256,128]{1,0:T(8,128)(2,1)}, u32[]{:S(2)}) copy-start(bf16[256,128]{1,0:T(8,128)(2,1)} %constant.111.sfn_ref) | copy-start | bytes 196612
  35.0 1.3 %collective-permute-start.2 = (f32[6,512]{1,0:T(8,128)S(1)}, f32[6,512]{1,0:T(8,128)S(1)}, u32[]{:S(2)}, u32[]{:S(2)}) collective-permute-start(f32[6,512]{1,0:T(8,128)S(1)} %get-tuple-element.14), channel_id=1, source_target_pairs={{0,128},{128,0},{1,129},{129,1},{2,130},{130,2},{3,131},{131,3},{4... | collective-permute-start | bytes 36872 | tf_op jit(solution)/shard_map/ppermute | solution.py:319
  60.9 0.7 %copy-start.12 = (f32[1,512]{1,0:T(1,128)S(1)}, f32[1,512]{1,0:T(1,128)}, u32[]{:S(2)}) copy-start(f32[1,512]{1,0:T(1,128)} %get-tuple-element.5) | copy-start | bytes 6148

commit v13 on v12

--- a/solution.py
+++ b/solution.py
@@ -147,11 +147,13 @@
     )
 
 
-def filter_kernel(
-    scalar_ref, x_ref, cfn_ref, sfn_ref, ct_ref, st_ref, cs_ref, ss_ref, cf_ref, sf_ref,
-    cfr_ref, sfr_ref, sown_ref, soth_ref, wown_ref, woth_ref, out_ref,
-    er_ref, ei_ref, pr_ref, pi_ref, w2_ref,
-):
+def filter_kernel(scalar_ref, x_ref, *refs):
+    sources = refs[:8]
+    cfr_ref, sfr_ref, sown_ref, soth_ref, wown_ref, woth_ref = refs[8:14]
+    out_ref, er_ref, ei_ref, pr_ref, pi_ref, w2_ref = refs[14:20]
+    held = refs[20:28]
+    fetch_sems = refs[28]
+    cfn_ref, sfn_ref, ct_ref, st_ref, cs_ref, ss_ref, cf_ref, sf_ref = held
     f32 = jnp.float32
     bf16 = jnp.bfloat16
 
@@ -174,6 +176,14 @@
 
     @pl.when(pl.program_id(0) == 0)
     def _():
+        fetches = [
+            pltpu.make_async_copy(src, dst, fetch_sems.at[k])
+            for k, (src, dst) in enumerate(zip(sources, held))
+        ]
+        for fetch in fetches:
+            fetch.start()
+        for fetch in fetches:
+            fetch.wait()
         det = scalar_ref[1]
         for slot, sig_ref, w_ref in ((det, sown_ref, wown_ref), (1 - det, soth_ref, woth_ref)):
             real_s, imag_s = first_stage(cf_ref[...], sf_ref[...], sig_ref[...])
@@ -267,7 +277,8 @@
         num_scalar_prefetch=1,
         grid=(count,),
         in_specs=[pl.BlockSpec((1, pad_rows, width), lambda i, r: (i, 0, 0))]
-        + [whole(a) for a in operands],
+        + [pl.BlockSpec(memory_space=pl.ANY)] * 8
+        + [whole(a) for a in operands[8:]],
         out_specs=pl.BlockSpec((1, N1, tiles), lambda i, r: (i, 0, 0)),
         scratch_shapes=[
             pltpu.VMEM((N1, N2), jnp.bfloat16),
@@ -275,14 +286,16 @@
             pltpu.VMEM((2, N1, N2 // 2), jnp.float32),
             pltpu.VMEM((2, N1, N2 // 2), jnp.float32),
             pltpu.VMEM((2, N1, N2 // 2), jnp.float32),
-        ],
+        ]
+        + [pltpu.VMEM(a.shape, a.dtype) for a in operands[:8]]
+        + [pltpu.SemaphoreType.DMA((8,))],
     )
     matmuls = 2 * N1 * pad_rows * N2 + 4 * N1 * N2 * (N2 // 2) + 16 * N1 * (N2 // 2) * N2
     out = pl.pallas_call(
         filter_kernel,
         out_shape=jax.ShapeDtypeStruct((count, N1, tiles), jnp.float32),
         grid_spec=grid_spec,
-        compiler_params=pltpu.CompilerParams(vmem_limit_bytes=48 * 1024 * 1024),
+        compiler_params=pltpu.CompilerParams(vmem_limit_bytes=56 * 1024 * 1024),
         cost_estimate=pl.CostEstimate(
             flops=2 * matmuls * count, transcendentals=0, bytes_accessed=8 * 1024 * 1024
         ),

time: 63.3 us -> 64.7 us (1.022)
  local copies, waits for them, and re-layouts: 12.8 us -> 9.59 us
  Pallas kernels: 40.5 us -> 43.4 us
  other arithmetic: 5.38 us -> 7.26 us
    unnamed x34 -> x26, local copies, waits for them, and re-layouts: 9.96 us -> 4.77 us
    pallas_call x1, Pallas kernels: 19.3 us -> 22.2 us  [filter_bank(): pl.pallas_call(filter_kernel, out_shape=jax.ShapeDtypeStruct((count, N1,...]
    reshape x1, local copies, waits for them, and re-layouts: 0.43 us -> 1.56 us  [filter_bank(): return out.reshape(count, N1 * tiles)]
    concatenate x1, local copies, waits for them, and re-layouts: 0.06 us -> 0.95 us  [filter_bank(): jnp.concatenate([windowed, jnp.zeros((count, pad_rows - rows_used, width)...]
    another operation x1, other arithmetic: 0.03 us -> 0.73 us  [filter_bank(): jnp.stack([lax.dynamic_slice_in_dim(doubled_sin, quot + v, N1) for v in r...]
    another operation x1, other arithmetic: 0.03 us -> 0.73 us  [filter_bank(): jnp.stack([lax.dynamic_slice_in_dim(doubled_cos, quot + v, N1) for v in r...]
  transfers between devices with their start and end apart: 3 -> 3, of which waited for: 1 -> 1; matrix products, arithmetic and copies ran while one was open for 4% -> 8% of each run, Pallas kernels for 0% -> 0%
where the time goes in v13:
time: 64.7 us; the launch traced here: 63.8 us
  Pallas kernels  43.4 us (67%)
  local copies, waits for them, and re-layouts  9.59 us (15%)
  other arithmetic  7.26 us (11%)
  between operations  1.58 us (2%)
  waiting for transfers between devices  1.14 us (2%)
  starting transfers between devices  0.8 us (1%)
    pallas_call x1, Pallas kernels, filter_bank(): pl.pallas_call(filter_kernel, out_shape=jax.ShapeDtypeStruct((count, N1,...  22.2 us
    pallas_call x1, Pallas kernels, route_and_max(): pl.pallas_call(functools.partial(route_kernel, split), out_shape=(jax.Sha...  21.2 us
    unnamed x26, local copies, waits for them, and re-layouts  4.77 us
    unnamed x1, other arithmetic  2.28 us
    reshape x1, local copies, waits for them, and re-layouts, filter_bank(): return out.reshape(count, N1 * tiles)  1.56 us
    convert_element_type x1, other arithmetic, shards(): own_signal = strain.reshape(N1, N2).astype(jnp.bfloat16)  1.38 us
  transfers between devices with their start and end apart: 3, of which 1 were waited for; matrix products, arithmetic and copies ran while one was open for 8% of the time, Pallas kernels for 0%

profile of v13, /device:TPU:32, one launch (start us, length us, event | category | flops | bytes accessed | tf_op | source)
XLA Modules:
  0.0 63.8 jit_solution(7942757597099472451)
XLA Ops:
  0.6 0.5 broadcast.105
  1.1 2.3 %reduce.8 = f32[65536]{0:T(1024)S(1)} reduce(f32[1,65536]{1,0:T(1,128)} %param.13, f32[]{:T(128)} %broadcast.105), dimensions={0}, to_apply=%param.13.reduce_sub_computation.3 | reduce | bytes 524292 | tf_op args[1]
  3.6 1.4 %convert_reduce_fusion = bf16[131072]{0:T(1024)(128)(2,1)S(1)} fusion(f32[1,131072]{1,0:T(1,128)S(1)} %copy-done), kind=kLoop, calls=%fused_computation.2 | loop fusion | flops 131072 | bytes 786432 | tf_op jit(solution)/shard_map/convert_element_type | solution.py:315
  5.1 0.2 convert_element_type.10.refs_10_
  5.2 0.6 collective-permute-start
  6.5 0.6 %copy-done.9 = s32[12]{0:T(128)S(1)} copy-done((s32[12]{0:T(128)S(1)}, s32[12]{0:T(128)}, u32[]{:S(2)}) %copy-start.9) | copy-done | bytes 72
  7.5 0.7 %pad_maximum_fusion.refs_8_ = bf16[2,256,256]{2,1,0:T(8,128)(2,1)} fusion(bf16[1,256,256]{2,1,0:T(8,128)(2,1)S(1)} %get-tuple-element.16, bf16[1,256,256]{2,1,0:T(8,128)(2,1)S(1)} %get-tuple-element.17), kind=kLoop, calls=%fused_computation.3 | loop fusion | flops 131072 | bytes 524288 | tf_op jit(solution)/shard_map/stack | solution.py:260
  8.2 0.7 %pad_maximum_fusion.1.refs_9_ = bf16[2,256,256]{2,1,0:T(8,128)(2,1)} fusion(bf16[1,256,256]{2,1,0:T(8,128)(2,1)S(1)} %get-tuple-element.11, bf16[1,256,256]{2,1,0:T(8,128)(2,1)S(1)} %get-tuple-element.10), kind=kLoop, calls=%fused_computation.4 | loop fusion | flops 131072 | bytes 524288 | tf_op jit(solution)/shard_map/stack | solution.py:263
  9.0 0.7 %copy-done.10 = s32[12]{0:T(128)S(1)} copy-done((s32[12]{0:T(128)S(1)}, s32[12]{0:T(128)}, u32[]{:S(2)}) %copy-start.10) | copy-done | bytes 72
  9.8 0.6 pad_add_fusion.scalar_ref
  10.4 0.9 %concatenate.19.x_ref = bf16[6,128,512]{2,1,0:T(8,128)(2,1)} pad(bf16[6,8,512]{2,1,0:T(8,128)(2,1)S(1)} %bitcast.34, bf16[]{:T(256)} %constant.80.clone.1), padding=0_0x0_120x0_0 | pad | bytes 835586 | tf_op jit(solution)/shard_map/concatenate | solution.py:252
  11.4 0.7 %copy-done.7 = f32[256,256]{1,0:T(8,128)} copy-done((f32[256,256]{1,0:T(8,128)}, f32[256,256]{1,0:T(8,128)S(1)}, u32[]{:S(2)}) %copy-start.7) | copy-done | bytes 262168
  12.1 0.7 %copy-done.8 = bf16[256,512]{1,0:T(8,128)(2,1)} copy-done((bf16[256,512]{1,0:T(8,128)(2,1)}, bf16[256,512]{1,0:T(8,128)(2,1)S(1)}, u32[]{:S(2)}) %copy-start.8) | copy-done | bytes 262168
  12.8 22.2 %shard_map.131 = f32[6,256,4]{2,1,0:T(8,128)} custom-call(s32[2]{0:T(128)} %pad_add_fusion.scalar_ref, bf16[6,128,512]{2,1,0:T(8,128)(2,1)} %concatenate.19.x_ref, bf16[256,128]{1,0:T(8,128)(2,1)} %constant.110.refs_0_, bf16[256,128]{1,0:T(8,128)(2,1)} %constant.111.refs_1_, f32[256,512]{1,0:T(8,128)} %constant.96.clone.refs_2_, ...), custom_call_target="tpu_custom_call" | custom-call | flops 8455716864 | bytes 8388608 | tf_op jit(solution)/shard_map/pallas_call | solution.py:294
  35.0 1.6 %reshape.93 = f32[6,1024]{1,0:T(8,128)S(1)} reshape(f32[6,256,4]{2,1,0:T(8,128)} %shard_map.131) | data formatting | bytes 49152 | tf_op jit(solution)/shard_map/reshape | solution.py:303
  36.6 0.1 collective-permute-start.2
  36.7 1.1 %collective-permute-done.2 = f32[6,512]{1,0:T(8,128)S(1)} collective-permute-done((f32[6,512]{1,0:T(8,128)S(1)}, f32[6,512]{1,0:T(8,128)S(1)}, u32[]{:S(2)}, u32[]{:S(2)}) %collective-permute-start.2) | collective-permute-done | bytes 12320 | tf_op jit(solution)/shard_map/ppermute | solution.py:332
  37.9 0.6 gather_fusion
  38.6 0.8 %broadcast_in_dim.88.send_ref = f32[32,1,1152]{2,1,0:T(1,128)} reshape(f32[32,1152]{1,0:T(8,128)S(1)} %pad_maximum_fusion.2) | data formatting | bytes 294912 | tf_op jit(solution)/shard_map/broadcast_in_dim | solution.py:348
  39.4 21.2 %shard_map.132 = (f32[32,1,1152]{2,1,0:T(1,128)}, f32[1,512]{1,0:T(1,128)}) custom-call(f32[32,1,1152]{2,1,0:T(1,128)} %broadcast_in_dim.88.send_ref), custom_call_target="tpu_custom_call" | custom-call | tf_op jit(solution)/shard_map/pallas_call | solution.py:122
  60.5 0.9 %copy.18 = f32[32,1,1152]{2,0,1:T(8,128)S(1)} copy(f32[32,1,1152]{2,1,0:T(1,128)} %get-tuple-element.4) | data formatting | bytes 294912
  61.9 0.6 gather_fusion.1
  62.5 0.7 %broadcast_select_fusion = f32[12,512]{1,0:T(8,128)} fusion(f32[12,512]{1,0:T(8,128)S(1)} %gather_fusion.1, pred[12]{0:T(512)(128)(4,1)S(1)} %compare_and_fusion), kind=kLoop, calls=%fused_computation.17 | loop fusion | flops 6144 | bytes 49164 | tf_op jit(solution)/shard_map/jit(_take)/select_n | solution.py:354
  63.2 0.6 copy.22
  (45 shorter events, 1.3 us)
Async XLA Ops:
  1.1 2.5 %copy-start = (f32[1,131072]{1,0:T(1,128)S(1)}, f32[1,131072]{1,0:T(1,128)}, u32[]{:S(2)}) copy-start(f32[1,131072]{1,0:T(1,128)} %param.12) | copy-start | bytes 1572868
  3.5 1.5 %copy-start.3 = (f32[256,256]{1,0:T(8,128)}, f32[256,256]{1,0:T(8,128)S(1)}, u32[]{:S(2)}) copy-start(f32[256,256]{1,0:T(8,128)S(1)} %reshape.92.refs_12_) | copy-start | bytes 786436
  3.5 7.8 %collective-permute-start.1 = (f32[256,256]{1,0:T(8,128)S(1)}, f32[256,256]{1,0:T(8,128)S(1)}, u32[]{:S(2)}, u32[]{:S(2)}) collective-permute-start(f32[256,256]{1,0:T(8,128)S(1)} %reshape.92.refs_12_), channel_id=1, source_target_pairs={{0,128},{128,0},{1,129},{129,1},{2,130},{130,2},{3,131},{131,3},{4... | collective-permute-start | bytes 786440 | tf_op jit(solution)/shard_map/ppermute | solution.py:318
  5.0 2.3 %copy-start.1 = (bf16[512,256]{1,0:T(8,128)(2,1)S(1)}, bf16[512,256]{1,0:T(8,128)(2,1)}, u32[]{:S(2)}) copy-start(bf16[512,256]{1,0:T(8,128)(2,1)} %constant.112) | copy-start | bytes 786436
  5.0 2.3 %copy-start.2 = (bf16[512,256]{1,0:T(8,128)(2,1)S(1)}, bf16[512,256]{1,0:T(8,128)(2,1)}, u32[]{:S(2)}) copy-start(bf16[512,256]{1,0:T(8,128)(2,1)} %constant.113) | copy-start | bytes 786436
  5.2 2.3 %copy-start.4 = (bf16[256,512]{1,0:T(8,128)(2,1)}, bf16[256,512]{1,0:T(8,128)(2,1)S(1)}, u32[]{:S(2)}) copy-start(bf16[256,512]{1,0:T(8,128)(2,1)S(1)} %convert_element_type.10.refs_10_) | copy-start | bytes 786436
  5.2 6.1 %collective-permute-start = (bf16[256,512]{1,0:T(8,128)(2,1)S(1)}, bf16[256,512]{1,0:T(8,128)(2,1)S(1)}, u32[]{:S(2)}, u32[]{:S(2)}) collective-permute-start(bf16[256,512]{1,0:T(8,128)(2,1)S(1)} %convert_element_type.10.refs_10_), channel_id=1, source_target_pairs={{0,128},{128,0},{1,129},{129,1},{2,130},{130,2},{3,131},{131,3},{4... | collective-permute-start | bytes 786440 | tf_op jit(solution)/shard_map/ppermute | solution.py:317
  6.5 0.7 %copy-start.9 = (s32[12]{0:T(128)S(1)}, s32[12]{0:T(128)}, u32[]{:S(2)}) copy-start(s32[12]{0:T(128)} %param.16) | copy-start | bytes 148
  8.2 1.5 %copy-start.5 = (bf16[12,4096]{1,0:T(8,128)(2,1)S(1)}, bf16[12,4096]{1,0:T(8,128)(2,1)}, u32[]{:S(2)}) copy-start(bf16[12,4096]{1,0:T(8,128)(2,1)} %param.14) | copy-start | bytes 294916
  9.0 0.7 %copy-start.10 = (s32[12]{0:T(128)S(1)}, s32[12]{0:T(128)}, u32[]{:S(2)}) copy-start(s32[12]{0:T(128)} %param.15) | copy-start | bytes 148
  11.3 0.7 %copy-start.7 = (f32[256,256]{1,0:T(8,128)}, f32[256,256]{1,0:T(8,128)S(1)}, u32[]{:S(2)}) copy-start(f32[256,256]{1,0:T(8,128)S(1)} %collective-permute-done.1.refs_13_) | copy-start | bytes 786436
  12.1 0.7 %copy-start.8 = (bf16[256,512]{1,0:T(8,128)(2,1)}, bf16[256,512]{1,0:T(8,128)(2,1)S(1)}, u32[]{:S(2)}) copy-start(bf16[256,512]{1,0:T(8,128)(2,1)S(1)} %collective-permute-done.refs_11_) | copy-start | bytes 786436
  36.6 1.3 %collective-permute-start.2 = (f32[6,512]{1,0:T(8,128)S(1)}, f32[6,512]{1,0:T(8,128)S(1)}, u32[]{:S(2)}, u32[]{:S(2)}) collective-permute-start(f32[6,512]{1,0:T(8,128)S(1)} %get-tuple-element.14), channel_id=1, source_target_pairs={{0,128},{128,0},{1,129},{129,1},{2,130},{130,2},{3,131},{131,3},{4... | collective-permute-start | bytes 36872 | tf_op jit(solution)/shard_map/ppermute | solution.py:332
  62.5 0.7 %copy-start.6 = (f32[1,512]{1,0:T(1,128)S(1)}, f32[1,512]{1,0:T(1,128)}, u32[]{:S(2)}) copy-start(f32[1,512]{1,0:T(1,128)} %get-tuple-element.5) | copy-start | bytes 6148

commit v14 on v12

--- a/solution.py
+++ b/solution.py
@@ -149,8 +149,7 @@
 
 def filter_kernel(
     scalar_ref, x_ref, cfn_ref, sfn_ref, ct_ref, st_ref, cs_ref, ss_ref, cf_ref, sf_ref,
-    cfr_ref, sfr_ref, sown_ref, soth_ref, wown_ref, woth_ref, out_ref,
-    er_ref, ei_ref, pr_ref, pi_ref, w2_ref,
+    sown_ref, soth_ref, wown_ref, woth_ref, out_ref, rho_ref, pr_ref, pi_ref, w2_ref,
 ):
     f32 = jnp.float32
     bf16 = jnp.bfloat16
@@ -212,25 +211,23 @@
     )
     first = (z_real * z_real + z_imag * z_imag) / (NFFT * sigma0)
     sigma1, e_real, e_imag = back_half(1)
-    er_ref[...] = e_real
-    ei_ref[...] = e_imag
+    z_real = jnp.dot(cos_first, e_real, preferred_element_type=f32) - jnp.dot(
+        sin_first, e_imag, preferred_element_type=f32
+    )
+    z_imag = jnp.dot(sin_first, e_real, preferred_element_type=f32) + jnp.dot(
+        cos_first, e_imag, preferred_element_type=f32
+    )
+    rho_ref[...] = (z_real * z_real + z_imag * z_imag) / (NFFT * sigma1)
     rem = scalar_ref[0]
+    quot = scalar_ref[2]
+    rows = first.shape[0]
     tiles = first.shape[1] // BLK
     for col in range(tiles):
         src = lax.rem(col + rem, tiles)
         carry = (col + rem) // tiles
         cols = pl.ds(pl.multiple_of(src * BLK, BLK), BLK)
-        e_r = er_ref[:, cols]
-        e_i = ei_ref[:, cols]
-        cos_rows = cfr_ref[carry]
-        sin_rows = sfr_ref[carry]
-        z_real = jnp.dot(cos_rows, e_r, preferred_element_type=f32) - jnp.dot(
-            sin_rows, e_i, preferred_element_type=f32
-        )
-        z_imag = jnp.dot(sin_rows, e_r, preferred_element_type=f32) + jnp.dot(
-            cos_rows, e_i, preferred_element_type=f32
-        )
-        second = (z_real * z_real + z_imag * z_imag) / (NFFT * sigma1)
+        shift = lax.rem(rows - lax.rem(quot + carry, rows), rows)
+        second = pltpu.roll(rho_ref[:, cols], shift, 0)
         network = first[:, col * BLK:(col + 1) * BLK] + second
         out_ref[0, :, col:col + 1] = jnp.max(network, axis=1, keepdims=True)
 
@@ -244,18 +241,10 @@
     )
     tiles = N2 // BLK
     quot = shift // tiles
-    scalars = jnp.stack([lax.rem(shift, tiles), det]).astype(jnp.int32)
-    doubled_cos = jnp.concatenate([cos_first, cos_first], axis=0)
-    doubled_sin = jnp.concatenate([sin_first, sin_first], axis=0)
-    cos_rolled = jnp.stack(
-        [lax.dynamic_slice_in_dim(doubled_cos, quot + v, N1) for v in range(2)]
-    )
-    sin_rolled = jnp.stack(
-        [lax.dynamic_slice_in_dim(doubled_sin, quot + v, N1) for v in range(2)]
-    )
+    scalars = jnp.stack([lax.rem(shift, tiles), det, quot]).astype(jnp.int32)
     operands = [
         cos_first[:, :pad_rows], sin_first[:, :pad_rows], cos_twist, sin_twist,
-        cos_second, sin_second, cos_first, sin_first, cos_rolled, sin_rolled,
+        cos_second, sin_second, cos_first, sin_first,
         signals[0], signals[1], weights[0], weights[1],
     ]
 
@@ -270,8 +259,7 @@
         + [whole(a) for a in operands],
         out_specs=pl.BlockSpec((1, N1, tiles), lambda i, r: (i, 0, 0)),
         scratch_shapes=[
-            pltpu.VMEM((N1, N2), jnp.bfloat16),
-            pltpu.VMEM((N1, N2), jnp.bfloat16),
+            pltpu.VMEM((N1, N2), jnp.float32),
             pltpu.VMEM((2, N1, N2 // 2), jnp.float32),
             pltpu.VMEM((2, N1, N2 // 2), jnp.float32),
             pltpu.VMEM((2, N1, N2 // 2), jnp.float32),

time: 63.3 us -> 61.5 us (0.972)
  local copies, waits for them, and re-layouts: 12.8 us -> 10.9 us
    unnamed x34 -> x30, local copies, waits for them, and re-layouts: 9.96 us -> 8.25 us
  transfers between devices with their start and end apart: 3 -> 3, of which waited for: 1 -> 1; matrix products, arithmetic and copies ran while one was open for 4% -> 3% of each run, Pallas kernels for 0% -> 0%
where the time goes in v14:
time: 61.5 us; the launch traced here: 60.2 us
  Pallas kernels  40.4 us (66%)
  local copies, waits for them, and re-layouts  10.9 us (18%)
  other arithmetic  5.33 us (9%)
  between operations  1.56 us (3%)
  starting transfers between devices  1.24 us (2%)
  waiting for transfers between devices  0.84 us (1%)
    pallas_call x1, Pallas kernels, route_and_max(): pl.pallas_call(functools.partial(route_kernel, split), out_shape=(jax.Sha...  21.3 us
    pallas_call x1, Pallas kernels, filter_bank(): pl.pallas_call(filter_kernel, out_shape=jax.ShapeDtypeStruct((count, N1,...  19 us
    unnamed x30, local copies, waits for them, and re-layouts  8.25 us
    unnamed x1, other arithmetic  2.28 us
    convert_element_type x1, other arithmetic, shards(): own_signal = strain.reshape(N1, N2).astype(jnp.bfloat16)  1.38 us
  transfers between devices with their start and end apart: 3, of which 1 were waited for; matrix products, arithmetic and copies ran while one was open for 3% of the time, Pallas kernels for 0%

profile of v14, /device:TPU:32, one launch (start us, length us, event | category | flops | bytes accessed | tf_op | source)
XLA Modules:
  0.0 60.2 jit_solution(17942950157207311968)
XLA Ops:
  0.6 0.5 broadcast.105
  1.1 2.3 %reduce.8 = f32[65536]{0:T(1024)S(1)} reduce(f32[1,65536]{1,0:T(1,128)} %param.13, f32[]{:T(128)} %broadcast.105), dimensions={0}, to_apply=%param.13.reduce_sub_computation.3 | reduce | bytes 524292 | tf_op args[1]
  3.6 1.4 %convert_reduce_fusion = bf16[131072]{0:T(1024)(128)(2,1)S(1)} fusion(f32[1,131072]{1,0:T(1,128)S(1)} %copy-done.8), kind=kLoop, calls=%fused_computation.2 | loop fusion | flops 131072 | bytes 786432 | tf_op jit(solution)/shard_map/convert_element_type | solution.py:290
  5.0 0.2 convert_element_type.10.sown_ref
  5.2 0.6 collective-permute-start
  6.7 0.6 %copy-done.12 = s32[12]{0:T(128)S(1)} copy-done((s32[12]{0:T(128)S(1)}, s32[12]{0:T(128)}, u32[]{:S(2)}) %copy-start.12) | copy-done | bytes 72
  7.8 0.7 %copy-done = f32[256,512]{1,0:T(8,128)S(1)} copy-done((f32[256,512]{1,0:T(8,128)S(1)}, f32[256,512]{1,0:T(8,128)}, u32[]{:S(2)}) %copy-start) | copy-done | bytes 524312
  8.5 0.1 copy-done.2
  8.7 1.0 %copy-done.1 = f32[256,512]{1,0:T(8,128)S(1)} copy-done((f32[256,512]{1,0:T(8,128)S(1)}, f32[256,512]{1,0:T(8,128)}, u32[]{:S(2)}) %copy-start.1) | copy-done | bytes 524312
  9.7 0.9 %copy-done.3 = bf16[512,256]{1,0:T(8,128)(2,1)S(1)} copy-done((bf16[512,256]{1,0:T(8,128)(2,1)S(1)}, bf16[512,256]{1,0:T(8,128)(2,1)}, u32[]{:S(2)}) %copy-start.3) | copy-done | bytes 262168
  10.7 0.9 %copy-done.5 = bf16[256,256]{1,0:T(8,128)(2,1)S(1)} copy-done((bf16[256,256]{1,0:T(8,128)(2,1)S(1)}, bf16[256,256]{1,0:T(8,128)(2,1)}, u32[]{:S(2)}) %copy-start.5) | copy-done | bytes 131096
  11.6 0.8 %copy-done.6 = bf16[256,128]{1,0:T(8,128)(2,1)S(1)} copy-done((bf16[256,128]{1,0:T(8,128)(2,1)S(1)}, bf16[256,128]{1,0:T(8,128)(2,1)}, u32[]{:S(2)}) %copy-start.6) | copy-done | bytes 65560
  12.4 0.8 %copy-done.7 = bf16[256,128]{1,0:T(8,128)(2,1)S(1)} copy-done((bf16[256,128]{1,0:T(8,128)(2,1)S(1)}, bf16[256,128]{1,0:T(8,128)(2,1)}, u32[]{:S(2)}) %copy-start.7) | copy-done | bytes 65560
  13.3 19.0 %shard_map.131 = f32[6,256,4]{2,1,0:T(8,128)S(1)} custom-call(s32[3]{0:T(128)S(1)} %pad_add_fusion.scalar_ref, bf16[6,128,512]{2,1,0:T(8,128)(2,1)S(1)} %concatenate.13.x_ref, bf16[256,128]{1,0:T(8,128)(2,1)S(1)} %copy-done.6, bf16[256,128]{1,0:T(8,128)(2,1)S(1)} %copy-done.7, f32[256,512]{1,0:T(8,128)S(1)} %copy-done, f32[256,512]{1,0:T(8,128)S(1)} %copy-done.1, ...), custom_call_target="tpu_custom_call" | custom-call | flops 8455716864 | bytes 8388608 | tf_op jit(solution)/shard_map/pallas_call | solution.py:269
  32.3 0.4 reshape.93
  32.7 0.6 collective-permute-start.2
  33.3 0.8 %collective-permute-done.2 = f32[6,512]{1,0:T(8,128)S(1)} collective-permute-done((f32[6,512]{1,0:T(8,128)S(1)}, f32[6,512]{1,0:T(8,128)S(1)}, u32[]{:S(2)}, u32[]{:S(2)}) %collective-permute-start.2) | collective-permute-done | bytes 12320 | tf_op jit(solution)/shard_map/ppermute | solution.py:307
  34.2 0.6 gather_fusion
  34.9 0.8 %broadcast_in_dim.88.send_ref = f32[32,1,1152]{2,1,0:T(1,128)} reshape(f32[32,1152]{1,0:T(8,128)S(1)} %pad_maximum_fusion) | data formatting | bytes 294912 | tf_op jit(solution)/shard_map/broadcast_in_dim | solution.py:323
  35.7 21.3 %shard_map.132 = (f32[32,1,1152]{2,1,0:T(1,128)}, f32[1,512]{1,0:T(1,128)}) custom-call(f32[32,1,1152]{2,1,0:T(1,128)} %broadcast_in_dim.88.send_ref), custom_call_target="tpu_custom_call" | custom-call | tf_op jit(solution)/shard_map/pallas_call | solution.py:122
  57.0 0.9 %copy.18 = f32[32,1,1152]{2,0,1:T(8,128)S(1)} copy(f32[32,1,1152]{2,1,0:T(1,128)} %get-tuple-element.4) | data formatting | bytes 294912
  58.4 0.6 gather_fusion.1
  59.0 0.7 %broadcast_select_fusion = f32[12,512]{1,0:T(8,128)} fusion(f32[12,512]{1,0:T(8,128)S(1)} %gather_fusion.1, pred[12]{0:T(512)(128)(4,1)S(1)} %compare_and_fusion), kind=kLoop, calls=%fused_computation.11 | loop fusion | flops 6144 | bytes 49164 | tf_op jit(solution)/shard_map/jit(_take)/select_n | solution.py:329
  59.7 0.6 copy.22
  (46 shorter events, 1.4 us)
Async XLA Ops:
  1.1 2.5 %copy-start.8 = (f32[1,131072]{1,0:T(1,128)S(1)}, f32[1,131072]{1,0:T(1,128)}, u32[]{:S(2)}) copy-start(f32[1,131072]{1,0:T(1,128)} %param.12) | copy-start | bytes 1572868
  3.5 4.3 %collective-permute-start.1 = (f32[256,256]{1,0:T(8,128)S(1)}, f32[256,256]{1,0:T(8,128)S(1)}, u32[]{:S(2)}, u32[]{:S(2)}) collective-permute-start(f32[256,256]{1,0:T(8,128)S(1)} %reshape.92.wown_ref), channel_id=1, source_target_pairs={{0,128},{128,0},{1,129},{129,1},{2,130},{130,2},{3,131},{131,3},{4... | collective-permute-start | bytes 786440 | tf_op jit(solution)/shard_map/ppermute | solution.py:293
  5.0 2.5 %copy-start.9 = (bf16[12,4096]{1,0:T(8,128)(2,1)S(1)}, bf16[12,4096]{1,0:T(8,128)(2,1)}, u32[]{:S(2)}) copy-start(bf16[12,4096]{1,0:T(8,128)(2,1)} %param.14) | copy-start | bytes 294916
  5.2 0.7 %copy-start.11 = (s32[12]{0:T(128)S(1)}, s32[12]{0:T(128)}, u32[]{:S(2)}) copy-start(s32[12]{0:T(128)} %param.16) | copy-start | bytes 148
  5.2 2.6 %collective-permute-start = (bf16[256,512]{1,0:T(8,128)(2,1)S(1)}, bf16[256,512]{1,0:T(8,128)(2,1)S(1)}, u32[]{:S(2)}, u32[]{:S(2)}) collective-permute-start(bf16[256,512]{1,0:T(8,128)(2,1)S(1)} %convert_element_type.10.sown_ref), channel_id=1, source_target_pairs={{0,128},{128,0},{1,129},{129,1},{2,130},{130,2},{3,131},{131,3},{4... | collective-permute-start | bytes 786440 | tf_op jit(solution)/shard_map/ppermute | solution.py:292
  6.7 0.7 %copy-start.12 = (s32[12]{0:T(128)S(1)}, s32[12]{0:T(128)}, u32[]{:S(2)}) copy-start(s32[12]{0:T(128)} %param.15) | copy-start | bytes 148
  7.5 1.0 %copy-start = (f32[256,512]{1,0:T(8,128)S(1)}, f32[256,512]{1,0:T(8,128)}, u32[]{:S(2)}) copy-start(f32[256,512]{1,0:T(8,128)} %constant.94.clone.ct_ref) | copy-start | bytes 1572868
  7.7 1.0 %copy-start.2 = (bf16[512,256]{1,0:T(8,128)(2,1)S(1)}, bf16[512,256]{1,0:T(8,128)(2,1)}, u32[]{:S(2)}) copy-start(bf16[512,256]{1,0:T(8,128)(2,1)} %constant.96.clone.cs_ref) | copy-start | bytes 786436
  7.7 1.0 %copy-start.4 = (bf16[256,256]{1,0:T(8,128)(2,1)S(1)}, bf16[256,256]{1,0:T(8,128)(2,1)}, u32[]{:S(2)}) copy-start(bf16[256,256]{1,0:T(8,128)(2,1)} %constant.92.clone.cf_ref) | copy-start | bytes 393220
  8.7 1.0 %copy-start.1 = (f32[256,512]{1,0:T(8,128)S(1)}, f32[256,512]{1,0:T(8,128)}, u32[]{:S(2)}) copy-start(f32[256,512]{1,0:T(8,128)} %constant.95.clone.st_ref) | copy-start | bytes 1572868
  9.7 0.9 %copy-start.3 = (bf16[512,256]{1,0:T(8,128)(2,1)S(1)}, bf16[512,256]{1,0:T(8,128)(2,1)}, u32[]{:S(2)}) copy-start(bf16[512,256]{1,0:T(8,128)(2,1)} %constant.97.clone.ss_ref) | copy-start | bytes 786436
  10.7 0.9 %copy-start.5 = (bf16[256,256]{1,0:T(8,128)(2,1)S(1)}, bf16[256,256]{1,0:T(8,128)(2,1)}, u32[]{:S(2)}) copy-start(bf16[256,256]{1,0:T(8,128)(2,1)} %constant.93.clone.sf_ref) | copy-start | bytes 393220
  11.6 0.8 %copy-start.6 = (bf16[256,128]{1,0:T(8,128)(2,1)S(1)}, bf16[256,128]{1,0:T(8,128)(2,1)}, u32[]{:S(2)}) copy-start(bf16[256,128]{1,0:T(8,128)(2,1)} %constant.108.cfn_ref) | copy-start | bytes 196612
  12.4 0.8 %copy-start.7 = (bf16[256,128]{1,0:T(8,128)(2,1)S(1)}, bf16[256,128]{1,0:T(8,128)(2,1)}, u32[]{:S(2)}) copy-start(bf16[256,128]{1,0:T(8,128)(2,1)} %constant.109.sfn_ref) | copy-start | bytes 196612
  32.7 1.4 %collective-permute-start.2 = (f32[6,512]{1,0:T(8,128)S(1)}, f32[6,512]{1,0:T(8,128)S(1)}, u32[]{:S(2)}, u32[]{:S(2)}) collective-permute-start(f32[6,512]{1,0:T(8,128)S(1)} %get-tuple-element.10), channel_id=1, source_target_pairs={{0,128},{128,0},{1,129},{129,1},{2,130},{130,2},{3,131},{131,3},{4... | collective-permute-start | bytes 36872 | tf_op jit(solution)/shard_map/ppermute | solution.py:307
  59.0 0.7 %copy-start.10 = (f32[1,512]{1,0:T(1,128)S(1)}, f32[1,512]{1,0:T(1,128)}, u32[]{:S(2)}) copy-start(f32[1,512]{1,0:T(1,128)} %get-tuple-element.5) | copy-start | bytes 6148

commit v15 on v14

--- a/solution.py
+++ b/solution.py
@@ -148,7 +148,7 @@
 
 
 def filter_kernel(
-    scalar_ref, x_ref, cfn_ref, sfn_ref, ct_ref, st_ref, cs_ref, ss_ref, cf_ref, sf_ref,
+    scalar_ref, x_ref, ct_ref, st_ref, cs_ref, ss_ref, cf_ref, sf_ref,
     sown_ref, soth_ref, wown_ref, woth_ref, out_ref, rho_ref, pr_ref, pi_ref, w2_ref,
 ):
     f32 = jnp.float32
@@ -181,7 +181,8 @@
             pi_ref[slot] = weight * imag_s
             w2_ref[slot] = weight * weight
 
-    temp_real, temp_imag = first_stage(cfn_ref[...], sfn_ref[...], x_ref[0])
+    used = x_ref.shape[1]
+    temp_real, temp_imag = first_stage(cf_ref[:, :used], sf_ref[:, :used], x_ref[0])
     power = temp_real * temp_real + temp_imag * temp_imag
     cos_back = cs_ref[...]
     sin_back = ss_ref[...]
@@ -243,7 +244,7 @@
     quot = shift // tiles
     scalars = jnp.stack([lax.rem(shift, tiles), det, quot]).astype(jnp.int32)
     operands = [
-        cos_first[:, :pad_rows], sin_first[:, :pad_rows], cos_twist, sin_twist,
+        cos_twist, sin_twist,
         cos_second, sin_second, cos_first, sin_first,
         signals[0], signals[1], weights[0], weights[1],
     ]

time: 61.5 us -> 59.7 us (0.971)
  local copies, waits for them, and re-layouts: 10.9 us -> 9.24 us
    unnamed x30 -> x26, local copies, waits for them, and re-layouts: 8.25 us -> 6.58 us
  transfers between devices with their start and end apart: 3 -> 3, of which waited for: 1 -> 1; matrix products, arithmetic and copies ran while one was open for 3% -> 4% of each run, Pallas kernels for 0% -> 0%
where the time goes in v15:
time: 59.7 us; the launch traced here: 58.5 us
  Pallas kernels  40.3 us (68%)
  local copies, waits for them, and re-layouts  9.24 us (15%)
  other arithmetic  5.33 us (9%)
  between operations  1.55 us (3%)
  starting transfers between devices  1.24 us (2%)
  waiting for transfers between devices  0.84 us (1%)
    pallas_call x1, Pallas kernels, route_and_max(): pl.pallas_call(functools.partial(route_kernel, split), out_shape=(jax.Sha...  21.4 us
    pallas_call x1, Pallas kernels, filter_bank(): pl.pallas_call(filter_kernel, out_shape=jax.ShapeDtypeStruct((count, N1,...  19 us
    unnamed x26, local copies, waits for them, and re-layouts  6.58 us
    unnamed x1, other arithmetic  2.28 us
    convert_element_type x1, other arithmetic, shards(): own_signal = strain.reshape(N1, N2).astype(jnp.bfloat16)  1.38 us
  transfers between devices with their start and end apart: 3, of which 1 were waited for; matrix products, arithmetic and copies ran while one was open for 4% of the time, Pallas kernels for 0%

profile of v15, /device:TPU:32, one launch (start us, length us, event | category | flops | bytes accessed | tf_op | source)
XLA Modules:
  0.0 58.5 jit_solution(13174151331303166211)
XLA Ops:
  0.6 0.5 broadcast.105
  1.1 2.3 %reduce.8 = f32[65536]{0:T(1024)S(1)} reduce(f32[1,65536]{1,0:T(1,128)} %param.13, f32[]{:T(128)} %broadcast.105), dimensions={0}, to_apply=%param.13.reduce_sub_computation.3 | reduce | bytes 524292 | tf_op args[1]
  3.6 1.4 %convert_reduce_fusion = bf16[131072]{0:T(1024)(128)(2,1)S(1)} fusion(f32[1,131072]{1,0:T(1,128)S(1)} %copy-done.6), kind=kLoop, calls=%fused_computation.2 | loop fusion | flops 131072 | bytes 786432 | tf_op jit(solution)/shard_map/convert_element_type | solution.py:291
  5.0 0.2 convert_element_type.10.sown_ref
  5.2 0.6 collective-permute-start
  6.7 0.6 %copy-done.10 = s32[12]{0:T(128)S(1)} copy-done((s32[12]{0:T(128)S(1)}, s32[12]{0:T(128)}, u32[]{:S(2)}) %copy-start.10) | copy-done | bytes 72
  7.8 0.7 %copy-done = f32[256,512]{1,0:T(8,128)S(1)} copy-done((f32[256,512]{1,0:T(8,128)S(1)}, f32[256,512]{1,0:T(8,128)}, u32[]{:S(2)}) %copy-start) | copy-done | bytes 524312
  8.5 0.1 copy-done.2
  8.7 1.0 %copy-done.1 = f32[256,512]{1,0:T(8,128)S(1)} copy-done((f32[256,512]{1,0:T(8,128)S(1)}, f32[256,512]{1,0:T(8,128)}, u32[]{:S(2)}) %copy-start.1) | copy-done | bytes 524312
  9.7 0.9 %copy-done.3 = bf16[512,256]{1,0:T(8,128)(2,1)S(1)} copy-done((bf16[512,256]{1,0:T(8,128)(2,1)S(1)}, bf16[512,256]{1,0:T(8,128)(2,1)}, u32[]{:S(2)}) %copy-start.3) | copy-done | bytes 262168
  10.7 0.9 %copy-done.5 = bf16[256,256]{1,0:T(8,128)(2,1)S(1)} copy-done((bf16[256,256]{1,0:T(8,128)(2,1)S(1)}, bf16[256,256]{1,0:T(8,128)(2,1)}, u32[]{:S(2)}) %copy-start.5) | copy-done | bytes 131096
  11.6 19.0 %shard_map.131 = f32[6,256,4]{2,1,0:T(8,128)S(1)} custom-call(s32[3]{0:T(128)S(1)} %pad_add_fusion.scalar_ref, bf16[6,128,512]{2,1,0:T(8,128)(2,1)S(1)} %concatenate.13.x_ref, f32[256,512]{1,0:T(8,128)S(1)} %copy-done, f32[256,512]{1,0:T(8,128)S(1)} %copy-done.1, bf16[512,256]{1,0:T(8,128)(2,1)S(1)} %copy-done.2, bf16[512,256]{1,0:T(8,128)(2,1)S(1)} %copy-done.3, ...), custom_call_target="tpu_custom_call" | custom-call | flops 8455716864 | bytes 8388608 | tf_op jit(solution)/shard_map/pallas_call | solution.py:270
  30.6 0.4 reshape.93
  31.0 0.6 collective-permute-start.2
  31.6 0.8 %collective-permute-done.2 = f32[6,512]{1,0:T(8,128)S(1)} collective-permute-done((f32[6,512]{1,0:T(8,128)S(1)}, f32[6,512]{1,0:T(8,128)S(1)}, u32[]{:S(2)}, u32[]{:S(2)}) %collective-permute-start.2) | collective-permute-done | bytes 12320 | tf_op jit(solution)/shard_map/ppermute | solution.py:308
  32.5 0.6 %gather_fusion = f32[32,512]{1,0:T(8,128)S(1)} fusion(f32[12,512]{1,0:T(8,128)S(1)} %get-tuple-element.9, s32[1024]{0:T(1024)S(1)} %pad_clamp_fusion.1), kind=kCustom, calls=%fused_computation | custom fusion | bytes 131200 | tf_op jit(solution)/shard_map/jit(_take)/gather | solution.py:319
  33.2 0.8 %broadcast_in_dim.88.send_ref = f32[32,1,1152]{2,1,0:T(1,128)} reshape(f32[32,1152]{1,0:T(8,128)S(1)} %pad_maximum_fusion) | data formatting | bytes 294912 | tf_op jit(solution)/shard_map/broadcast_in_dim | solution.py:324
  33.9 21.4 %shard_map.132 = (f32[32,1,1152]{2,1,0:T(1,128)}, f32[1,512]{1,0:T(1,128)}) custom-call(f32[32,1,1152]{2,1,0:T(1,128)} %broadcast_in_dim.88.send_ref), custom_call_target="tpu_custom_call" | custom-call | tf_op jit(solution)/shard_map/pallas_call | solution.py:122
  55.3 0.9 %copy.18 = f32[32,1,1152]{2,0,1:T(8,128)S(1)} copy(f32[32,1,1152]{2,1,0:T(1,128)} %get-tuple-element.4) | data formatting | bytes 294912
  56.2 0.1 fusion.5
  56.5 0.1 select_reduce_fusion
  56.7 0.6 gather_fusion.1
  57.3 0.7 %broadcast_select_fusion = f32[12,512]{1,0:T(8,128)} fusion(f32[12,512]{1,0:T(8,128)S(1)} %gather_fusion.1, pred[12]{0:T(512)(128)(4,1)S(1)} %compare_and_fusion), kind=kLoop, calls=%fused_computation.11 | loop fusion | flops 6144 | bytes 49164 | tf_op jit(solution)/shard_map/jit(_take)/select_n | solution.py:330
  58.0 0.6 copy.22
  (42 shorter events, 1.2 us)
Async XLA Ops:
  1.1 2.5 %copy-start.6 = (f32[1,131072]{1,0:T(1,128)S(1)}, f32[1,131072]{1,0:T(1,128)}, u32[]{:S(2)}) copy-start(f32[1,131072]{1,0:T(1,128)} %param.12) | copy-start | bytes 1572868
  3.5 4.3 %collective-permute-start.1 = (f32[256,256]{1,0:T(8,128)S(1)}, f32[256,256]{1,0:T(8,128)S(1)}, u32[]{:S(2)}, u32[]{:S(2)}) collective-permute-start(f32[256,256]{1,0:T(8,128)S(1)} %reshape.92.wown_ref), channel_id=1, source_target_pairs={{0,128},{128,0},{1,129},{129,1},{2,130},{130,2},{3,131},{131,3},{4... | collective-permute-start | bytes 786440 | tf_op jit(solution)/shard_map/ppermute | solution.py:294
  5.0 2.5 %copy-start.7 = (bf16[12,4096]{1,0:T(8,128)(2,1)S(1)}, bf16[12,4096]{1,0:T(8,128)(2,1)}, u32[]{:S(2)}) copy-start(bf16[12,4096]{1,0:T(8,128)(2,1)} %param.14) | copy-start | bytes 294916
  5.2 0.7 %copy-start.9 = (s32[12]{0:T(128)S(1)}, s32[12]{0:T(128)}, u32[]{:S(2)}) copy-start(s32[12]{0:T(128)} %param.16) | copy-start | bytes 148
  5.2 2.6 %collective-permute-start = (bf16[256,512]{1,0:T(8,128)(2,1)S(1)}, bf16[256,512]{1,0:T(8,128)(2,1)S(1)}, u32[]{:S(2)}, u32[]{:S(2)}) collective-permute-start(bf16[256,512]{1,0:T(8,128)(2,1)S(1)} %convert_element_type.10.sown_ref), channel_id=1, source_target_pairs={{0,128},{128,0},{1,129},{129,1},{2,130},{130,2},{3,131},{131,3},{4... | collective-permute-start | bytes 786440 | tf_op jit(solution)/shard_map/ppermute | solution.py:293
  6.7 0.7 %copy-start.10 = (s32[12]{0:T(128)S(1)}, s32[12]{0:T(128)}, u32[]{:S(2)}) copy-start(s32[12]{0:T(128)} %param.15) | copy-start | bytes 148
  7.5 1.0 %copy-start = (f32[256,512]{1,0:T(8,128)S(1)}, f32[256,512]{1,0:T(8,128)}, u32[]{:S(2)}) copy-start(f32[256,512]{1,0:T(8,128)} %constant.94.clone.ct_ref) | copy-start | bytes 1572868
  7.7 1.0 %copy-start.2 = (bf16[512,256]{1,0:T(8,128)(2,1)S(1)}, bf16[512,256]{1,0:T(8,128)(2,1)}, u32[]{:S(2)}) copy-start(bf16[512,256]{1,0:T(8,128)(2,1)} %constant.96.clone.cs_ref) | copy-start | bytes 786436
  7.7 1.0 %copy-start.4 = (bf16[256,256]{1,0:T(8,128)(2,1)S(1)}, bf16[256,256]{1,0:T(8,128)(2,1)}, u32[]{:S(2)}) copy-start(bf16[256,256]{1,0:T(8,128)(2,1)} %constant.92.clone.cf_ref) | copy-start | bytes 393220
  8.7 1.0 %copy-start.1 = (f32[256,512]{1,0:T(8,128)S(1)}, f32[256,512]{1,0:T(8,128)}, u32[]{:S(2)}) copy-start(f32[256,512]{1,0:T(8,128)} %constant.95.clone.st_ref) | copy-start | bytes 1572868
  9.7 0.9 %copy-start.3 = (bf16[512,256]{1,0:T(8,128)(2,1)S(1)}, bf16[512,256]{1,0:T(8,128)(2,1)}, u32[]{:S(2)}) copy-start(bf16[512,256]{1,0:T(8,128)(2,1)} %constant.97.clone.ss_ref) | copy-start | bytes 786436
  10.7 0.9 %copy-start.5 = (bf16[256,256]{1,0:T(8,128)(2,1)S(1)}, bf16[256,256]{1,0:T(8,128)(2,1)}, u32[]{:S(2)}) copy-start(bf16[256,256]{1,0:T(8,128)(2,1)} %constant.93.clone.sf_ref) | copy-start | bytes 393220
  31.0 1.4 %collective-permute-start.2 = (f32[6,512]{1,0:T(8,128)S(1)}, f32[6,512]{1,0:T(8,128)S(1)}, u32[]{:S(2)}, u32[]{:S(2)}) collective-permute-start(f32[6,512]{1,0:T(8,128)S(1)} %get-tuple-element.10), channel_id=1, source_target_pairs={{0,128},{128,0},{1,129},{129,1},{2,130},{130,2},{3,131},{131,3},{4... | collective-permute-start | bytes 36872 | tf_op jit(solution)/shard_map/ppermute | solution.py:308
  57.3 0.7 %copy-start.8 = (f32[1,512]{1,0:T(1,128)S(1)}, f32[1,512]{1,0:T(1,128)}, u32[]{:S(2)}) copy-start(f32[1,512]{1,0:T(1,128)} %get-tuple-element.5) | copy-start | bytes 6148

commit v16 on v15

--- a/solution.py
+++ b/solution.py
@@ -175,8 +175,16 @@
     def _():
         det = scalar_ref[1]
         for slot, sig_ref, w_ref in ((det, sown_ref, wown_ref), (1 - det, soth_ref, woth_ref)):
-            real_s, imag_s = first_stage(cf_ref[...], sf_ref[...], sig_ref[...])
-            weight = jnp.transpose(w_ref[...])
+            rows = sig_ref.shape[0] // (N2 // BLK)
+            signal = jnp.concatenate(
+                [sig_ref[pl.ds(c, rows, stride=N2 // BLK), :] for c in range(N2 // BLK)], axis=1
+            ).astype(bf16)
+            real_s, imag_s = first_stage(cf_ref[...], sf_ref[...], signal)
+            halves = N1 // BLK
+            raw = jnp.concatenate(
+                [w_ref[pl.ds(h, N2 // 2, stride=halves), :] for h in range(halves)], axis=1
+            )
+            weight = jnp.transpose(raw)
             pr_ref[slot] = weight * real_s
             pi_ref[slot] = weight * imag_s
             w2_ref[slot] = weight * weight
@@ -288,8 +296,8 @@
     half_blk = n_blk // 2
     filt_count = lax.axis_size("filt")
     swap = [(0, 1), (1, 0)]
-    own_signal = strain.reshape(N1, N2).astype(jnp.bfloat16)
-    own_weight = inv_asd.reshape(N2 // 2, N1)
+    own_signal = strain.reshape(-1, BLK)
+    own_weight = inv_asd.reshape(-1, BLK)
     other_signal = lax.ppermute(own_signal, "det", swap)
     other_weight = lax.ppermute(own_weight, "det", swap)
     samples = jnp.arange(TL, dtype=jnp.int32)

time: 59.7 us -> 57.4 us (0.961)
  other arithmetic: 5.33 us -> 4.58 us
  Pallas kernels: 40.3 us -> 39.6 us
    unnamed x1 -> x0, other arithmetic: 2.28 us -> none
    convert_element_type x1 -> x0, other arithmetic: 1.38 us -> none  [shards(): own_signal = strain.reshape(N1, N2).astype(jnp.bfloat16)]
    select_n x1, other arithmetic: 0.08 us -> 1.03 us  [shards(): jnp.where(samples[None, :] < BLK * my_blocks[:, None], my_rows, jnp.zeros...]
    mul x1, other arithmetic: 0.07 us -> 0.73 us  [shards(): BLK * my_blocks[:, None]]
    reduce_sum x1, other arithmetic: 0.09 us -> 0.74 us  [shards(): source = jnp.sum(jnp.where(placing, positions[None, :], 0), axis=1)]
    reduce_or x1, other arithmetic: 0.09 us -> 0.74 us  [shards(): used = jnp.any(placing, axis=1)]
    unnamed x26 -> x21, local copies, waits for them, and re-layouts: 6.58 us -> 6.35 us
  transfers between devices with their start and end apart: 3 -> 3, of which waited for: 1 -> 1; matrix products, arithmetic and copies ran while one was open for 4% -> 6% of each run, Pallas kernels for 0% -> 0%
where the time goes in v16:
time: 57.4 us; the launch traced here: 56.4 us
  Pallas kernels  39.6 us (69%)
  local copies, waits for them, and re-layouts  8.78 us (15%)
  other arithmetic  4.58 us (8%)
  between operations  1.51 us (3%)
  waiting for transfers between devices  1.09 us (2%)
  starting transfers between devices  0.77 us (1%)
    pallas_call x1, Pallas kernels, route_and_max(): pl.pallas_call(functools.partial(route_kernel, split), out_shape=(jax.Sha...  21.2 us
    pallas_call x1, Pallas kernels, filter_bank(): pl.pallas_call(filter_kernel, out_shape=jax.ShapeDtypeStruct((count, N1,...  18.5 us
    unnamed x21, local copies, waits for them, and re-layouts  6.35 us
  transfers between devices with their start and end apart: 3, of which 1 were waited for; matrix products, arithmetic and copies ran while one was open for 6% of the time, Pallas kernels for 0%

profile of v16, /device:TPU:32, one launch (start us, length us, event | category | flops | bytes accessed | tf_op | source)
XLA Modules:
  0.0 56.4 jit_solution(13116206131380773186)
XLA Ops:
  0.7 0.5 collective-permute-start.1
  1.2 0.7 %select_reduce_fusion.1 = s32[32]{0:T(128)S(1)} fusion(s32[12]{0:T(128)} %param.16), kind=kLoop, calls=%fused_computation.14 | loop fusion | flops 1120 | bytes 176 | tf_op jit(solution)/shard_map/reduce_sum | solution.py:324
  2.0 0.7 %fusion.1 = pred[32]{0:T(512)(128)(4,1)S(1)} fusion(s32[12]{0:T(128)} %param.16), kind=kLoop, calls=%fused_computation.16 | loop fusion | flops 736 | bytes 80 | tf_op jit(solution)/shard_map/reduce_or | solution.py:325
  3.4 0.7 %dynamic-slice_multiply_fusion = s32[6]{0:T(128)S(1)} fusion(s32[12]{0:T(128)} %param.15, s32[]{:T(128)S(6)} %select_n.83), kind=kLoop, calls=%fused_computation.31 | loop fusion | flops 6 | bytes 52 | tf_op jit(solution)/shard_map/mul | solution.py:307
  4.1 1.0 %fusion = bf16[6,4096]{1,0:T(8,128)(2,1)S(1)} fusion(bf16[12,4096]{1,0:T(8,128)(2,1)} %param.14, s32[]{:T(128)S(6)} %select_n.83, s32[6]{0:T(128)S(1)} %dynamic-slice_multiply_fusion), kind=kLoop, calls=%fused_computation.5 | loop fusion | flops 49152 | bytes 98332 | tf_op jit(solution)/shard_map/jit(_where)/select_n | solution.py:306
  5.4 0.8 %copy-done = f32[1,131072]{1,0:T(1,128)S(1)} copy-done((f32[1,131072]{1,0:T(1,128)S(1)}, f32[1,131072]{1,0:T(1,128)}, u32[]{:S(2)}) %copy-start) | copy-done | bytes 524312
  6.3 1.0 %copy-done.2 = f32[256,512]{1,0:T(8,128)S(1)} copy-done((f32[256,512]{1,0:T(8,128)S(1)}, f32[256,512]{1,0:T(8,128)}, u32[]{:S(2)}) %copy-start.2) | copy-done | bytes 524312
  7.4 1.0 %copy-done.3 = f32[256,512]{1,0:T(8,128)S(1)} copy-done((f32[256,512]{1,0:T(8,128)S(1)}, f32[256,512]{1,0:T(8,128)}, u32[]{:S(2)}) %copy-start.3) | copy-done | bytes 524312
  8.4 0.9 %copy-done.5 = bf16[512,256]{1,0:T(8,128)(2,1)S(1)} copy-done((bf16[512,256]{1,0:T(8,128)(2,1)S(1)}, bf16[512,256]{1,0:T(8,128)(2,1)}, u32[]{:S(2)}) %copy-start.5) | copy-done | bytes 262168
  9.3 0.9 %copy-done.7 = bf16[256,256]{1,0:T(8,128)(2,1)S(1)} copy-done((bf16[256,256]{1,0:T(8,128)(2,1)S(1)}, bf16[256,256]{1,0:T(8,128)(2,1)}, u32[]{:S(2)}) %copy-start.7) | copy-done | bytes 131096
  10.3 18.5 %shard_map.131 = f32[6,256,4]{2,1,0:T(8,128)S(1)} custom-call(s32[3]{0:T(128)S(1)} %pad_add_fusion.scalar_ref, bf16[6,128,512]{2,1,0:T(8,128)(2,1)S(1)} %concatenate.13.x_ref, f32[256,512]{1,0:T(8,128)S(1)} %copy-done.2, f32[256,512]{1,0:T(8,128)S(1)} %copy-done.3, bf16[512,256]{1,0:T(8,128)(2,1)S(1)} %copy-done.4, bf16[512,256]{1,0:T(8,128)(2,1)S(1)} %copy-done.5, ...), custom_call_target="tpu_custom_call" | custom-call | flops 8455716864 | bytes 8388608 | tf_op jit(solution)/shard_map/pallas_call | solution.py:278
  28.7 0.4 reshape.95
  29.2 0.2 collective-permute-start.2
  29.4 1.1 %collective-permute-done.2 = f32[6,512]{1,0:T(8,128)S(1)} collective-permute-done((f32[6,512]{1,0:T(8,128)S(1)}, f32[6,512]{1,0:T(8,128)S(1)}, u32[]{:S(2)}, u32[]{:S(2)}) %collective-permute-start.2) | collective-permute-done | bytes 12320 | tf_op jit(solution)/shard_map/ppermute | solution.py:316
  30.5 0.6 %gather_fusion = f32[32,512]{1,0:T(8,128)S(1)} fusion(f32[12,512]{1,0:T(8,128)S(1)} %get-tuple-element.9, s32[1024]{0:T(1024)S(1)} %pad_clamp_fusion.1), kind=kCustom, calls=%fused_computation | custom fusion | bytes 131200 | tf_op jit(solution)/shard_map/jit(_take)/gather | solution.py:327
  31.2 0.8 %broadcast_in_dim.88.send_ref = f32[32,1,1152]{2,1,0:T(1,128)} reshape(f32[32,1152]{1,0:T(8,128)S(1)} %pad_maximum_fusion) | data formatting | bytes 294912 | tf_op jit(solution)/shard_map/broadcast_in_dim | solution.py:332
  31.9 21.2 %shard_map.132 = (f32[32,1,1152]{2,1,0:T(1,128)}, f32[1,512]{1,0:T(1,128)}) custom-call(f32[32,1,1152]{2,1,0:T(1,128)} %broadcast_in_dim.88.send_ref), custom_call_target="tpu_custom_call" | custom-call | tf_op jit(solution)/shard_map/pallas_call | solution.py:122
  53.1 0.9 %copy.18 = f32[32,1,1152]{2,0,1:T(8,128)S(1)} copy(f32[32,1,1152]{2,1,0:T(1,128)} %get-tuple-element.4) | data formatting | bytes 294912
  54.1 0.1 fusion.5
  54.2 0.1 add_reduce_fusion
  54.4 0.1 select_reduce_fusion
  54.5 0.6 %gather_fusion.1 = f32[12,512]{1,0:T(8,128)S(1)} fusion(f32[32,512]{1,0:T(8,128)S(1)} %slice.13, s32[1024]{0:T(1024)S(1)} %pad_clamp_fusion), kind=kCustom, calls=%fused_computation.1 | custom fusion | bytes 49200 | tf_op jit(solution)/shard_map/jit(_take)/gather | solution.py:338
  55.1 0.7 %broadcast_select_fusion = f32[12,512]{1,0:T(8,128)} fusion(f32[12,512]{1,0:T(8,128)S(1)} %gather_fusion.1, pred[12]{0:T(512)(128)(4,1)S(1)} %compare_and_fusion), kind=kLoop, calls=%fused_computation.10 | loop fusion | flops 6144 | bytes 49164 | tf_op jit(solution)/shard_map/jit(_take)/select_n | solution.py:338
  55.8 0.6 %copy.22 = f32[512]{0:T(512)} copy(f32[512]{0:T(512)S(1)} %bitcast.34) | data formatting | bytes 4096
  (33 shorter events, 0.6 us)
Async XLA Ops:
  0.6 4.8 %copy-start.6 = (bf16[256,256]{1,0:T(8,128)(2,1)S(1)}, bf16[256,256]{1,0:T(8,128)(2,1)}, u32[]{:S(2)}) copy-start(bf16[256,256]{1,0:T(8,128)(2,1)} %constant.92.clone.cf_ref) | copy-start | bytes 393220
  0.6 4.8 %collective-permute-start = (f32[1024,128]{1,0:T(8,128)}, f32[1024,128]{1,0:T(8,128)S(1)}, u32[]{:S(2)}, u32[]{:S(2)}) collective-permute-start(f32[1024,128]{1,0:T(8,128)} %bitcast.26), channel_id=1, source_target_pairs={{0,128},{128,0},{1,129},{129,1},{2,130},{130,2},{3,131},{131,3},{4... | collective-permute-start | bytes 1572872 | tf_op jit(solution)/shard_map/ppermute | solution.py:301
  0.7 4.7 %collective-permute-start.1 = (f32[512,128]{1,0:T(8,128)}, f32[512,128]{1,0:T(8,128)S(1)}, u32[]{:S(2)}, u32[]{:S(2)}) collective-permute-start(f32[512,128]{1,0:T(8,128)} %bitcast.28), channel_id=1, source_target_pairs={{0,128},{128,0},{1,129},{129,1},{2,130},{130,2},{3,131},{131,3},{4... | collective-permute-start | bytes 786440 | tf_op jit(solution)/shard_map/ppermute | solution.py:302
  4.1 1.3 %copy-start.4 = (bf16[512,256]{1,0:T(8,128)(2,1)S(1)}, bf16[512,256]{1,0:T(8,128)(2,1)}, u32[]{:S(2)}) copy-start(bf16[512,256]{1,0:T(8,128)(2,1)} %constant.96.clone.cs_ref) | copy-start | bytes 786436
  5.2 1.0 %copy-start = (f32[1,131072]{1,0:T(1,128)S(1)}, f32[1,131072]{1,0:T(1,128)}, u32[]{:S(2)}) copy-start(f32[1,131072]{1,0:T(1,128)} %param.12) | copy-start | bytes 1572868
  5.3 1.0 %copy-start.1 = (f32[1,65536]{1,0:T(1,128)S(1)}, f32[1,65536]{1,0:T(1,128)}, u32[]{:S(2)}) copy-start(f32[1,65536]{1,0:T(1,128)} %param.13) | copy-start | bytes 786436
  6.3 1.0 %copy-start.2 = (f32[256,512]{1,0:T(8,128)S(1)}, f32[256,512]{1,0:T(8,128)}, u32[]{:S(2)}) copy-start(f32[256,512]{1,0:T(8,128)} %constant.94.clone.ct_ref) | copy-start | bytes 1572868
  7.4 1.0 %copy-start.3 = (f32[256,512]{1,0:T(8,128)S(1)}, f32[256,512]{1,0:T(8,128)}, u32[]{:S(2)}) copy-start(f32[256,512]{1,0:T(8,128)} %constant.95.clone.st_ref) | copy-start | bytes 1572868
  8.4 0.9 %copy-start.5 = (bf16[512,256]{1,0:T(8,128)(2,1)S(1)}, bf16[512,256]{1,0:T(8,128)(2,1)}, u32[]{:S(2)}) copy-start(bf16[512,256]{1,0:T(8,128)(2,1)} %constant.97.clone.ss_ref) | copy-start | bytes 786436
  9.3 0.9 %copy-start.7 = (bf16[256,256]{1,0:T(8,128)(2,1)S(1)}, bf16[256,256]{1,0:T(8,128)(2,1)}, u32[]{:S(2)}) copy-start(bf16[256,256]{1,0:T(8,128)(2,1)} %constant.93.clone.sf_ref) | copy-start | bytes 393220
  29.2 1.3 %collective-permute-start.2 = (f32[6,512]{1,0:T(8,128)S(1)}, f32[6,512]{1,0:T(8,128)S(1)}, u32[]{:S(2)}, u32[]{:S(2)}) collective-permute-start(f32[6,512]{1,0:T(8,128)S(1)} %get-tuple-element.10), channel_id=1, source_target_pairs={{0,128},{128,0},{1,129},{129,1},{2,130},{130,2},{3,131},{131,3},{4... | collective-permute-start | bytes 36872 | tf_op jit(solution)/shard_map/ppermute | solution.py:316
  55.1 0.7 %copy-start.8 = (f32[1,512]{1,0:T(1,128)S(1)}, f32[1,512]{1,0:T(1,128)}, u32[]{:S(2)}) copy-start(f32[1,512]{1,0:T(1,128)} %get-tuple-element.5) | copy-start | bytes 6148

commit v17 on v16

--- a/solution.py
+++ b/solution.py
@@ -89,7 +89,7 @@
         ).wait_recv()
     recv_buf[filt] = send_ref[filt]
     rows = recv_buf[...]
-    recv_out[...] = rows
+    recv_out[...] = rows[:, :, :split]
     value = jnp.max(rows[:, :, split:], axis=0)
     if n_grp > 1:
         acc_ref[...] = value
@@ -122,7 +122,7 @@
     recv, out = pl.pallas_call(
         functools.partial(route_kernel, split),
         out_shape=(
-            jax.ShapeDtypeStruct(send_rows.shape, send_rows.dtype),
+            jax.ShapeDtypeStruct((n_filt, 1, split), send_rows.dtype),
             jax.ShapeDtypeStruct((1, width), jnp.float32),
         ),
         in_specs=[vmem],
@@ -330,7 +330,7 @@
         [send_rows, jnp.broadcast_to(local_max[None, :], (filt_count, half_blk))], axis=1
     )
     recv_rows, loudest = route_and_max(send_rows[:, None, :], split)
-    recv_rows = recv_rows.reshape(filt_count, split + half_blk)
+    recv_rows = recv_rows.reshape(filt_count, split)
     valid = recv_rows[:, half_blk] > 0.5
     rank = jnp.cumsum(valid.astype(jnp.int32)) - 1
     hits = jnp.logical_and(valid[None, :], rank[None, :] == positions[:, None])

time: 57.4 us -> 57.3 us (level)
  no operation moved by 1% of the time
where the time goes in v17:
time: 57.3 us; the launch traced here: 56.3 us
  Pallas kernels  39.6 us (69%)
  local copies, waits for them, and re-layouts  8.76 us (15%)
  other arithmetic  4.58 us (8%)
  between operations  1.5 us (3%)
  waiting for transfers between devices  1.09 us (2%)
  starting transfers between devices  0.77 us (1%)
    pallas_call x1, Pallas kernels, route_and_max(): pl.pallas_call(functools.partial(route_kernel, split), out_shape=(jax.Sha...  21.2 us
    pallas_call x1, Pallas kernels, filter_bank(): pl.pallas_call(filter_kernel, out_shape=jax.ShapeDtypeStruct((count, N1,...  18.5 us
    unnamed x21, local copies, waits for them, and re-layouts  6.33 us
  transfers between devices with their start and end apart: 3, of which 1 were waited for; matrix products, arithmetic and copies ran while one was open for 6% of the time, Pallas kernels for 0%

profile of v17, /device:TPU:32, one launch (start us, length us, event | category | flops | bytes accessed | tf_op | source)
XLA Modules:
  0.0 56.3 jit_solution(17041242910321359496)
XLA Ops:
  0.7 0.5 collective-permute-start.1
  1.2 0.7 %select_reduce_fusion.1 = s32[32]{0:T(128)S(1)} fusion(s32[12]{0:T(128)} %param.16), kind=kLoop, calls=%fused_computation.14 | loop fusion | flops 1120 | bytes 176 | tf_op jit(solution)/shard_map/reduce_sum | solution.py:324
  2.0 0.7 %fusion.1 = pred[32]{0:T(512)(128)(4,1)S(1)} fusion(s32[12]{0:T(128)} %param.16), kind=kLoop, calls=%fused_computation.16 | loop fusion | flops 736 | bytes 80 | tf_op jit(solution)/shard_map/reduce_or | solution.py:325
  3.4 0.7 %dynamic-slice_multiply_fusion = s32[6]{0:T(128)S(1)} fusion(s32[12]{0:T(128)} %param.15, s32[]{:T(128)S(6)} %select_n.83), kind=kLoop, calls=%fused_computation.31 | loop fusion | flops 6 | bytes 52 | tf_op jit(solution)/shard_map/mul | solution.py:307
  4.1 1.0 %fusion = bf16[6,4096]{1,0:T(8,128)(2,1)S(1)} fusion(bf16[12,4096]{1,0:T(8,128)(2,1)} %param.14, s32[]{:T(128)S(6)} %select_n.83, s32[6]{0:T(128)S(1)} %dynamic-slice_multiply_fusion), kind=kLoop, calls=%fused_computation.4 | loop fusion | flops 49152 | bytes 98332 | tf_op jit(solution)/shard_map/jit(_where)/select_n | solution.py:306
  5.4 0.8 %copy-done = f32[1,131072]{1,0:T(1,128)S(1)} copy-done((f32[1,131072]{1,0:T(1,128)S(1)}, f32[1,131072]{1,0:T(1,128)}, u32[]{:S(2)}) %copy-start) | copy-done | bytes 524312
  6.3 1.0 %copy-done.2 = f32[256,512]{1,0:T(8,128)S(1)} copy-done((f32[256,512]{1,0:T(8,128)S(1)}, f32[256,512]{1,0:T(8,128)}, u32[]{:S(2)}) %copy-start.2) | copy-done | bytes 524312
  7.4 1.0 %copy-done.3 = f32[256,512]{1,0:T(8,128)S(1)} copy-done((f32[256,512]{1,0:T(8,128)S(1)}, f32[256,512]{1,0:T(8,128)}, u32[]{:S(2)}) %copy-start.3) | copy-done | bytes 524312
  8.4 0.9 %copy-done.5 = bf16[512,256]{1,0:T(8,128)(2,1)S(1)} copy-done((bf16[512,256]{1,0:T(8,128)(2,1)S(1)}, bf16[512,256]{1,0:T(8,128)(2,1)}, u32[]{:S(2)}) %copy-start.5) | copy-done | bytes 262168
  9.3 0.9 %copy-done.7 = bf16[256,256]{1,0:T(8,128)(2,1)S(1)} copy-done((bf16[256,256]{1,0:T(8,128)(2,1)S(1)}, bf16[256,256]{1,0:T(8,128)(2,1)}, u32[]{:S(2)}) %copy-start.7) | copy-done | bytes 131096
  10.3 18.5 %shard_map.131 = f32[6,256,4]{2,1,0:T(8,128)S(1)} custom-call(s32[3]{0:T(128)S(1)} %pad_add_fusion.scalar_ref, bf16[6,128,512]{2,1,0:T(8,128)(2,1)S(1)} %concatenate.13.x_ref, f32[256,512]{1,0:T(8,128)S(1)} %copy-done.2, f32[256,512]{1,0:T(8,128)S(1)} %copy-done.3, bf16[512,256]{1,0:T(8,128)(2,1)S(1)} %copy-done.4, bf16[512,256]{1,0:T(8,128)(2,1)S(1)} %copy-done.5, ...), custom_call_target="tpu_custom_call" | custom-call | flops 8455716864 | bytes 8388608 | tf_op jit(solution)/shard_map/pallas_call | solution.py:278
  28.7 0.4 reshape.95
  29.2 0.2 collective-permute-start.2
  29.4 1.1 %collective-permute-done.2 = f32[6,512]{1,0:T(8,128)S(1)} collective-permute-done((f32[6,512]{1,0:T(8,128)S(1)}, f32[6,512]{1,0:T(8,128)S(1)}, u32[]{:S(2)}, u32[]{:S(2)}) %collective-permute-start.2) | collective-permute-done | bytes 12320 | tf_op jit(solution)/shard_map/ppermute | solution.py:316
  30.5 0.6 %gather_fusion = f32[32,512]{1,0:T(8,128)S(1)} fusion(f32[12,512]{1,0:T(8,128)S(1)} %get-tuple-element.9, s32[1024]{0:T(1024)S(1)} %pad_clamp_fusion.1), kind=kCustom, calls=%fused_computation | custom fusion | bytes 131200 | tf_op jit(solution)/shard_map/jit(_take)/gather | solution.py:327
  31.2 0.8 %broadcast_in_dim.88.send_ref = f32[32,1,1152]{2,1,0:T(1,128)} reshape(f32[32,1152]{1,0:T(8,128)S(1)} %pad_maximum_fusion) | data formatting | bytes 294912 | tf_op jit(solution)/shard_map/broadcast_in_dim | solution.py:332
  31.9 21.2 %shard_map.132 = (f32[32,1,640]{2,1,0:T(1,128)}, f32[1,512]{1,0:T(1,128)}) custom-call(f32[32,1,1152]{2,1,0:T(1,128)} %broadcast_in_dim.88.send_ref), custom_call_target="tpu_custom_call" | custom-call | tf_op jit(solution)/shard_map/pallas_call | solution.py:122
  53.1 0.9 %copy.18 = f32[32,1,640]{2,0,1:T(8,128)S(1)} copy(f32[32,1,640]{2,1,0:T(1,128)} %get-tuple-element.4) | data formatting | bytes 163840
  54.0 0.1 fusion.5
  54.2 0.1 add_reduce_fusion
  54.3 0.1 select_reduce_fusion
  54.5 0.6 %gather_fusion.1 = f32[12,512]{1,0:T(8,128)S(1)} fusion(f32[32,512]{1,0:T(8,128)S(1)} %slice.13, s32[1024]{0:T(1024)S(1)} %pad_clamp_fusion), kind=kCustom, calls=%fused_computation.1 | custom fusion | bytes 49200 | tf_op jit(solution)/shard_map/jit(_take)/gather | solution.py:338
  55.0 0.7 %broadcast_select_fusion = f32[12,512]{1,0:T(8,128)} fusion(f32[12,512]{1,0:T(8,128)S(1)} %gather_fusion.1, pred[12]{0:T(512)(128)(4,1)S(1)} %compare_and_fusion), kind=kLoop, calls=%fused_computation.10 | loop fusion | flops 6144 | bytes 49164 | tf_op jit(solution)/shard_map/jit(_take)/select_n | solution.py:338
  55.7 0.6 %copy.22 = f32[512]{0:T(512)} copy(f32[512]{0:T(512)S(1)} %bitcast.34) | data formatting | bytes 4096
  (33 shorter events, 0.6 us)
Async XLA Ops:
  0.6 4.8 %copy-start.6 = (bf16[256,256]{1,0:T(8,128)(2,1)S(1)}, bf16[256,256]{1,0:T(8,128)(2,1)}, u32[]{:S(2)}) copy-start(bf16[256,256]{1,0:T(8,128)(2,1)} %constant.92.clone.cf_ref) | copy-start | bytes 393220
  0.6 4.8 %collective-permute-start = (f32[1024,128]{1,0:T(8,128)}, f32[1024,128]{1,0:T(8,128)S(1)}, u32[]{:S(2)}, u32[]{:S(2)}) collective-permute-start(f32[1024,128]{1,0:T(8,128)} %bitcast.26), channel_id=1, source_target_pairs={{0,128},{128,0},{1,129},{129,1},{2,130},{130,2},{3,131},{131,3},{4... | collective-permute-start | bytes 1572872 | tf_op jit(solution)/shard_map/ppermute | solution.py:301
  0.7 4.7 %collective-permute-start.1 = (f32[512,128]{1,0:T(8,128)}, f32[512,128]{1,0:T(8,128)S(1)}, u32[]{:S(2)}, u32[]{:S(2)}) collective-permute-start(f32[512,128]{1,0:T(8,128)} %bitcast.28), channel_id=1, source_target_pairs={{0,128},{128,0},{1,129},{129,1},{2,130},{130,2},{3,131},{131,3},{4... | collective-permute-start | bytes 786440 | tf_op jit(solution)/shard_map/ppermute | solution.py:302
  4.1 1.3 %copy-start.4 = (bf16[512,256]{1,0:T(8,128)(2,1)S(1)}, bf16[512,256]{1,0:T(8,128)(2,1)}, u32[]{:S(2)}) copy-start(bf16[512,256]{1,0:T(8,128)(2,1)} %constant.96.clone.cs_ref) | copy-start | bytes 786436
  5.2 1.0 %copy-start = (f32[1,131072]{1,0:T(1,128)S(1)}, f32[1,131072]{1,0:T(1,128)}, u32[]{:S(2)}) copy-start(f32[1,131072]{1,0:T(1,128)} %param.12) | copy-start | bytes 1572868
  5.3 1.0 %copy-start.1 = (f32[1,65536]{1,0:T(1,128)S(1)}, f32[1,65536]{1,0:T(1,128)}, u32[]{:S(2)}) copy-start(f32[1,65536]{1,0:T(1,128)} %param.13) | copy-start | bytes 786436
  6.3 1.0 %copy-start.2 = (f32[256,512]{1,0:T(8,128)S(1)}, f32[256,512]{1,0:T(8,128)}, u32[]{:S(2)}) copy-start(f32[256,512]{1,0:T(8,128)} %constant.94.clone.ct_ref) | copy-start | bytes 1572868
  7.4 1.0 %copy-start.3 = (f32[256,512]{1,0:T(8,128)S(1)}, f32[256,512]{1,0:T(8,128)}, u32[]{:S(2)}) copy-start(f32[256,512]{1,0:T(8,128)} %constant.95.clone.st_ref) | copy-start | bytes 1572868
  8.4 0.9 %copy-start.5 = (bf16[512,256]{1,0:T(8,128)(2,1)S(1)}, bf16[512,256]{1,0:T(8,128)(2,1)}, u32[]{:S(2)}) copy-start(bf16[512,256]{1,0:T(8,128)(2,1)} %constant.97.clone.ss_ref) | copy-start | bytes 786436
  9.3 0.9 %copy-start.7 = (bf16[256,256]{1,0:T(8,128)(2,1)S(1)}, bf16[256,256]{1,0:T(8,128)(2,1)}, u32[]{:S(2)}) copy-start(bf16[256,256]{1,0:T(8,128)(2,1)} %constant.93.clone.sf_ref) | copy-start | bytes 393220
  29.2 1.3 %collective-permute-start.2 = (f32[6,512]{1,0:T(8,128)S(1)}, f32[6,512]{1,0:T(8,128)S(1)}, u32[]{:S(2)}, u32[]{:S(2)}) collective-permute-start(f32[6,512]{1,0:T(8,128)S(1)} %get-tuple-element.10), channel_id=1, source_target_pairs={{0,128},{128,0},{1,129},{129,1},{2,130},{130,2},{3,131},{131,3},{4... | collective-permute-start | bytes 36872 | tf_op jit(solution)/shard_map/ppermute | solution.py:316
  55.0 0.7 %copy-start.8 = (f32[1,512]{1,0:T(1,128)S(1)}, f32[1,512]{1,0:T(1,128)}, u32[]{:S(2)}) copy-start(f32[1,512]{1,0:T(1,128)} %get-tuple-element.5) | copy-start | bytes 6148

commit v18 on v17

--- a/solution.py
+++ b/solution.py
@@ -189,56 +189,60 @@
             pi_ref[slot] = weight * imag_s
             w2_ref[slot] = weight * weight
 
-    used = x_ref.shape[1]
-    temp_real, temp_imag = first_stage(cf_ref[:, :used], sf_ref[:, :used], x_ref[0])
-    power = temp_real * temp_real + temp_imag * temp_imag
-    cos_back = cs_ref[...]
-    sin_back = ss_ref[...]
-
-    def back_half(d):
-        cos_twist = ct_ref[...]
-        sin_twist = st_ref[...]
-        sigma = jnp.sum(w2_ref[d] * power, axis=(0, 1), keepdims=True)
-        data_real = pr_ref[d]
-        data_imag = pi_ref[d]
-        q_real = (temp_real * data_real + temp_imag * data_imag).astype(bf16)
-        q_imag = (temp_real * data_imag - temp_imag * data_real).astype(bf16)
-        d_real = dot_nt(q_real, cos_back) - dot_nt(q_imag, sin_back)
-        d_imag = dot_nt(q_real, sin_back) + dot_nt(q_imag, cos_back)
-        e_real = (d_real * cos_twist - d_imag * sin_twist).astype(bf16)
-        e_imag = (d_real * sin_twist + d_imag * cos_twist).astype(bf16)
-        return sigma, e_real, e_imag
-
-    sigma0, e_real, e_imag = back_half(0)
-    cos_first = cf_ref[...]
-    sin_first = sf_ref[...]
-    z_real = jnp.dot(cos_first, e_real, preferred_element_type=f32) - jnp.dot(
-        sin_first, e_imag, preferred_element_type=f32
-    )
-    z_imag = jnp.dot(sin_first, e_real, preferred_element_type=f32) + jnp.dot(
-        cos_first, e_imag, preferred_element_type=f32
-    )
-    first = (z_real * z_real + z_imag * z_imag) / (NFFT * sigma0)
-    sigma1, e_real, e_imag = back_half(1)
-    z_real = jnp.dot(cos_first, e_real, preferred_element_type=f32) - jnp.dot(
-        sin_first, e_imag, preferred_element_type=f32
-    )
-    z_imag = jnp.dot(sin_first, e_real, preferred_element_type=f32) + jnp.dot(
-        cos_first, e_imag, preferred_element_type=f32
-    )
-    rho_ref[...] = (z_real * z_real + z_imag * z_imag) / (NFFT * sigma1)
-    rem = scalar_ref[0]
-    quot = scalar_ref[2]
-    rows = first.shape[0]
-    tiles = first.shape[1] // BLK
-    for col in range(tiles):
-        src = lax.rem(col + rem, tiles)
-        carry = (col + rem) // tiles
-        cols = pl.ds(pl.multiple_of(src * BLK, BLK), BLK)
-        shift = lax.rem(rows - lax.rem(quot + carry, rows), rows)
-        second = pltpu.roll(rho_ref[:, cols], shift, 0)
-        network = first[:, col * BLK:(col + 1) * BLK] + second
-        out_ref[0, :, col:col + 1] = jnp.max(network, axis=1, keepdims=True)
+    def one(j):
+        used = x_ref.shape[1]
+        temp_real, temp_imag = first_stage(cf_ref[:, :used], sf_ref[:, :used], x_ref[j])
+        power = temp_real * temp_real + temp_imag * temp_imag
+        cos_back = cs_ref[...]
+        sin_back = ss_ref[...]
+
+        def back_half(d):
+            cos_twist = ct_ref[...]
+            sin_twist = st_ref[...]
+            sigma = jnp.sum(w2_ref[d] * power, axis=(0, 1), keepdims=True)
+            data_real = pr_ref[d]
+            data_imag = pi_ref[d]
+            q_real = (temp_real * data_real + temp_imag * data_imag).astype(bf16)
+            q_imag = (temp_real * data_imag - temp_imag * data_real).astype(bf16)
+            d_real = dot_nt(q_real, cos_back) - dot_nt(q_imag, sin_back)
+            d_imag = dot_nt(q_real, sin_back) + dot_nt(q_imag, cos_back)
+            e_real = (d_real * cos_twist - d_imag * sin_twist).astype(bf16)
+            e_imag = (d_real * sin_twist + d_imag * cos_twist).astype(bf16)
+            return sigma, e_real, e_imag
+
+        sigma0, e_real, e_imag = back_half(0)
+        cos_first = cf_ref[...]
+        sin_first = sf_ref[...]
+        z_real = jnp.dot(cos_first, e_real, preferred_element_type=f32) - jnp.dot(
+            sin_first, e_imag, preferred_element_type=f32
+        )
+        z_imag = jnp.dot(sin_first, e_real, preferred_element_type=f32) + jnp.dot(
+            cos_first, e_imag, preferred_element_type=f32
+        )
+        first = (z_real * z_real + z_imag * z_imag) / (NFFT * sigma0)
+        sigma1, e_real, e_imag = back_half(1)
+        z_real = jnp.dot(cos_first, e_real, preferred_element_type=f32) - jnp.dot(
+            sin_first, e_imag, preferred_element_type=f32
+        )
+        z_imag = jnp.dot(sin_first, e_real, preferred_element_type=f32) + jnp.dot(
+            cos_first, e_imag, preferred_element_type=f32
+        )
+        rho_ref[...] = (z_real * z_real + z_imag * z_imag) / (NFFT * sigma1)
+        rem = scalar_ref[0]
+        quot = scalar_ref[2]
+        rows = first.shape[0]
+        tiles = first.shape[1] // BLK
+        for col in range(tiles):
+            src = lax.rem(col + rem, tiles)
+            carry = (col + rem) // tiles
+            cols = pl.ds(pl.multiple_of(src * BLK, BLK), BLK)
+            shift = lax.rem(rows - lax.rem(quot + carry, rows), rows)
+            second = pltpu.roll(rho_ref[:, cols], shift, 0)
+            network = first[:, col * BLK:(col + 1) * BLK] + second
+            out_ref[j, :, col:col + 1] = jnp.max(network, axis=1, keepdims=True)
+
+    for j in range(x_ref.shape[0]):
+        one(j)
 
 
 def filter_bank(windowed, tables, signals, weights, shift, det):
@@ -263,10 +267,10 @@
 
     grid_spec = pltpu.PrefetchScalarGridSpec(
         num_scalar_prefetch=1,
-        grid=(count,),
-        in_specs=[pl.BlockSpec((1, pad_rows, width), lambda i, r: (i, 0, 0))]
+        grid=(count // 2,),
+        in_specs=[pl.BlockSpec((2, pad_rows, width), lambda i, r: (i, 0, 0))]
         + [whole(a) for a in operands],
-        out_specs=pl.BlockSpec((1, N1, tiles), lambda i, r: (i, 0, 0)),
+        out_specs=pl.BlockSpec((2, N1, tiles), lambda i, r: (i, 0, 0)),
         scratch_shapes=[
             pltpu.VMEM((N1, N2), jnp.float32),
             pltpu.VMEM((2, N1, N2 // 2), jnp.float32),

time: 57.3 us -> 56.9 us (level)
  no operation moved by 1% of the time
where the time goes in v18:
time: 56.9 us; the launch traced here: 55.9 us
  Pallas kernels  39.2 us (69%)
  local copies, waits for them, and re-layouts  8.76 us (15%)
  other arithmetic  4.58 us (8%)
  between operations  1.5 us (3%)
  waiting for transfers between devices  1.09 us (2%)
  starting transfers between devices  0.77 us (1%)
    pallas_call x1, Pallas kernels, route_and_max(): pl.pallas_call(functools.partial(route_kernel, split), out_shape=(jax.Sha...  21.2 us
    pallas_call x1, Pallas kernels, filter_bank(): pl.pallas_call(filter_kernel, out_shape=jax.ShapeDtypeStruct((count, N1,...  18 us
    unnamed x21, local copies, waits for them, and re-layouts  6.33 us
  transfers between devices with their start and end apart: 3, of which 1 were waited for; matrix products, arithmetic and copies ran while one was open for 6% of the time, Pallas kernels for 0%

profile of v18, /device:TPU:32, one launch (start us, length us, event | category | flops | bytes accessed | tf_op | source)
XLA Modules:
  0.0 55.9 jit_solution(6559047606326767077)
XLA Ops:
  0.7 0.5 collective-permute-start.1
  1.2 0.7 %select_reduce_fusion.1 = s32[32]{0:T(128)S(1)} fusion(s32[12]{0:T(128)} %param.16), kind=kLoop, calls=%fused_computation.14 | loop fusion | flops 1120 | bytes 176 | tf_op jit(solution)/shard_map/reduce_sum | solution.py:328
  2.0 0.7 %fusion.1 = pred[32]{0:T(512)(128)(4,1)S(1)} fusion(s32[12]{0:T(128)} %param.16), kind=kLoop, calls=%fused_computation.16 | loop fusion | flops 736 | bytes 80 | tf_op jit(solution)/shard_map/reduce_or | solution.py:329
  3.4 0.7 %dynamic-slice_multiply_fusion = s32[6]{0:T(128)S(1)} fusion(s32[12]{0:T(128)} %param.15, s32[]{:T(128)S(6)} %select_n.83), kind=kLoop, calls=%fused_computation.31 | loop fusion | flops 6 | bytes 52 | tf_op jit(solution)/shard_map/mul | solution.py:311
  4.1 1.0 %fusion = bf16[6,4096]{1,0:T(8,128)(2,1)S(1)} fusion(bf16[12,4096]{1,0:T(8,128)(2,1)} %param.14, s32[]{:T(128)S(6)} %select_n.83, s32[6]{0:T(128)S(1)} %dynamic-slice_multiply_fusion), kind=kLoop, calls=%fused_computation.4 | loop fusion | flops 49152 | bytes 98332 | tf_op jit(solution)/shard_map/jit(_where)/select_n | solution.py:310
  5.4 0.8 %copy-done = f32[1,131072]{1,0:T(1,128)S(1)} copy-done((f32[1,131072]{1,0:T(1,128)S(1)}, f32[1,131072]{1,0:T(1,128)}, u32[]{:S(2)}) %copy-start) | copy-done | bytes 524312
  6.3 1.0 %copy-done.2 = f32[256,512]{1,0:T(8,128)S(1)} copy-done((f32[256,512]{1,0:T(8,128)S(1)}, f32[256,512]{1,0:T(8,128)}, u32[]{:S(2)}) %copy-start.2) | copy-done | bytes 524312
  7.4 1.0 %copy-done.3 = f32[256,512]{1,0:T(8,128)S(1)} copy-done((f32[256,512]{1,0:T(8,128)S(1)}, f32[256,512]{1,0:T(8,128)}, u32[]{:S(2)}) %copy-start.3) | copy-done | bytes 524312
  8.4 0.9 %copy-done.5 = bf16[512,256]{1,0:T(8,128)(2,1)S(1)} copy-done((bf16[512,256]{1,0:T(8,128)(2,1)S(1)}, bf16[512,256]{1,0:T(8,128)(2,1)}, u32[]{:S(2)}) %copy-start.5) | copy-done | bytes 262168
  9.3 0.9 %copy-done.7 = bf16[256,256]{1,0:T(8,128)(2,1)S(1)} copy-done((bf16[256,256]{1,0:T(8,128)(2,1)S(1)}, bf16[256,256]{1,0:T(8,128)(2,1)}, u32[]{:S(2)}) %copy-start.7) | copy-done | bytes 131096
  10.3 18.0 %shard_map.131 = f32[6,256,4]{2,1,0:T(8,128)S(1)} custom-call(s32[3]{0:T(128)S(1)} %pad_add_fusion.scalar_ref, bf16[6,128,512]{2,1,0:T(8,128)(2,1)S(1)} %concatenate.13.x_ref, f32[256,512]{1,0:T(8,128)S(1)} %copy-done.2, f32[256,512]{1,0:T(8,128)S(1)} %copy-done.3, bf16[512,256]{1,0:T(8,128)(2,1)S(1)} %copy-done.4, bf16[512,256]{1,0:T(8,128)(2,1)S(1)} %copy-done.5, ...), custom_call_target="tpu_custom_call" | custom-call | flops 8455716864 | bytes 8388608 | tf_op jit(solution)/shard_map/pallas_call | solution.py:282
  28.2 0.4 reshape.95
  28.7 0.2 collective-permute-start.2
  28.9 1.1 %collective-permute-done.2 = f32[6,512]{1,0:T(8,128)S(1)} collective-permute-done((f32[6,512]{1,0:T(8,128)S(1)}, f32[6,512]{1,0:T(8,128)S(1)}, u32[]{:S(2)}, u32[]{:S(2)}) %collective-permute-start.2) | collective-permute-done | bytes 12320 | tf_op jit(solution)/shard_map/ppermute | solution.py:320
  30.0 0.6 %gather_fusion = f32[32,512]{1,0:T(8,128)S(1)} fusion(f32[12,512]{1,0:T(8,128)S(1)} %get-tuple-element.9, s32[1024]{0:T(1024)S(1)} %pad_clamp_fusion.1), kind=kCustom, calls=%fused_computation | custom fusion | bytes 131200 | tf_op jit(solution)/shard_map/jit(_take)/gather | solution.py:331
  30.7 0.8 %broadcast_in_dim.88.send_ref = f32[32,1,1152]{2,1,0:T(1,128)} reshape(f32[32,1152]{1,0:T(8,128)S(1)} %pad_maximum_fusion) | data formatting | bytes 294912 | tf_op jit(solution)/shard_map/broadcast_in_dim | solution.py:336
  31.5 21.2 %shard_map.132 = (f32[32,1,640]{2,1,0:T(1,128)}, f32[1,512]{1,0:T(1,128)}) custom-call(f32[32,1,1152]{2,1,0:T(1,128)} %broadcast_in_dim.88.send_ref), custom_call_target="tpu_custom_call" | custom-call | tf_op jit(solution)/shard_map/pallas_call | solution.py:122
  52.7 0.9 %copy.18 = f32[32,1,640]{2,0,1:T(8,128)S(1)} copy(f32[32,1,640]{2,1,0:T(1,128)} %get-tuple-element.4) | data formatting | bytes 163840
  53.5 0.1 fusion.5
  53.7 0.1 add_reduce_fusion
  53.9 0.1 select_reduce_fusion
  54.0 0.6 %gather_fusion.1 = f32[12,512]{1,0:T(8,128)S(1)} fusion(f32[32,512]{1,0:T(8,128)S(1)} %slice.13, s32[1024]{0:T(1024)S(1)} %pad_clamp_fusion), kind=kCustom, calls=%fused_computation.1 | custom fusion | bytes 49200 | tf_op jit(solution)/shard_map/jit(_take)/gather | solution.py:342
  54.6 0.7 %broadcast_select_fusion = f32[12,512]{1,0:T(8,128)} fusion(f32[12,512]{1,0:T(8,128)S(1)} %gather_fusion.1, pred[12]{0:T(512)(128)(4,1)S(1)} %compare_and_fusion), kind=kLoop, calls=%fused_computation.10 | loop fusion | flops 6144 | bytes 49164 | tf_op jit(solution)/shard_map/jit(_take)/select_n | solution.py:342
  55.3 0.6 %copy.22 = f32[512]{0:T(512)} copy(f32[512]{0:T(512)S(1)} %bitcast.34) | data formatting | bytes 4096
  (33 shorter events, 0.6 us)
Async XLA Ops:
  0.6 4.8 %copy-start.6 = (bf16[256,256]{1,0:T(8,128)(2,1)S(1)}, bf16[256,256]{1,0:T(8,128)(2,1)}, u32[]{:S(2)}) copy-start(bf16[256,256]{1,0:T(8,128)(2,1)} %constant.92.clone.cf_ref) | copy-start | bytes 393220
  0.6 4.8 %collective-permute-start = (f32[1024,128]{1,0:T(8,128)}, f32[1024,128]{1,0:T(8,128)S(1)}, u32[]{:S(2)}, u32[]{:S(2)}) collective-permute-start(f32[1024,128]{1,0:T(8,128)} %bitcast.26), channel_id=1, source_target_pairs={{0,128},{128,0},{1,129},{129,1},{2,130},{130,2},{3,131},{131,3},{4... | collective-permute-start | bytes 1572872 | tf_op jit(solution)/shard_map/ppermute | solution.py:305
  0.7 4.7 %collective-permute-start.1 = (f32[512,128]{1,0:T(8,128)}, f32[512,128]{1,0:T(8,128)S(1)}, u32[]{:S(2)}, u32[]{:S(2)}) collective-permute-start(f32[512,128]{1,0:T(8,128)} %bitcast.28), channel_id=1, source_target_pairs={{0,128},{128,0},{1,129},{129,1},{2,130},{130,2},{3,131},{131,3},{4... | collective-permute-start | bytes 786440 | tf_op jit(solution)/shard_map/ppermute | solution.py:306
  4.1 1.3 %copy-start.4 = (bf16[512,256]{1,0:T(8,128)(2,1)S(1)}, bf16[512,256]{1,0:T(8,128)(2,1)}, u32[]{:S(2)}) copy-start(bf16[512,256]{1,0:T(8,128)(2,1)} %constant.96.clone.cs_ref) | copy-start | bytes 786436
  5.2 1.0 %copy-start = (f32[1,131072]{1,0:T(1,128)S(1)}, f32[1,131072]{1,0:T(1,128)}, u32[]{:S(2)}) copy-start(f32[1,131072]{1,0:T(1,128)} %param.12) | copy-start | bytes 1572868
  5.3 1.0 %copy-start.1 = (f32[1,65536]{1,0:T(1,128)S(1)}, f32[1,65536]{1,0:T(1,128)}, u32[]{:S(2)}) copy-start(f32[1,65536]{1,0:T(1,128)} %param.13) | copy-start | bytes 786436
  6.3 1.0 %copy-start.2 = (f32[256,512]{1,0:T(8,128)S(1)}, f32[256,512]{1,0:T(8,128)}, u32[]{:S(2)}) copy-start(f32[256,512]{1,0:T(8,128)} %constant.94.clone.ct_ref) | copy-start | bytes 1572868
  7.4 1.0 %copy-start.3 = (f32[256,512]{1,0:T(8,128)S(1)}, f32[256,512]{1,0:T(8,128)}, u32[]{:S(2)}) copy-start(f32[256,512]{1,0:T(8,128)} %constant.95.clone.st_ref) | copy-start | bytes 1572868
  8.4 0.9 %copy-start.5 = (bf16[512,256]{1,0:T(8,128)(2,1)S(1)}, bf16[512,256]{1,0:T(8,128)(2,1)}, u32[]{:S(2)}) copy-start(bf16[512,256]{1,0:T(8,128)(2,1)} %constant.97.clone.ss_ref) | copy-start | bytes 786436
  9.3 0.9 %copy-start.7 = (bf16[256,256]{1,0:T(8,128)(2,1)S(1)}, bf16[256,256]{1,0:T(8,128)(2,1)}, u32[]{:S(2)}) copy-start(bf16[256,256]{1,0:T(8,128)(2,1)} %constant.93.clone.sf_ref) | copy-start | bytes 393220
  28.7 1.3 %collective-permute-start.2 = (f32[6,512]{1,0:T(8,128)S(1)}, f32[6,512]{1,0:T(8,128)S(1)}, u32[]{:S(2)}, u32[]{:S(2)}) collective-permute-start(f32[6,512]{1,0:T(8,128)S(1)} %get-tuple-element.10), channel_id=1, source_target_pairs={{0,128},{128,0},{1,129},{129,1},{2,130},{130,2},{3,131},{131,3},{4... | collective-permute-start | bytes 36872 | tf_op jit(solution)/shard_map/ppermute | solution.py:320
  54.6 0.7 %copy-start.8 = (f32[1,512]{1,0:T(1,128)S(1)}, f32[1,512]{1,0:T(1,128)}, u32[]{:S(2)}) copy-start(f32[1,512]{1,0:T(1,128)} %get-tuple-element.5) | copy-start | bytes 6148

commit v19 on v17

--- a/solution.py
+++ b/solution.py
@@ -323,12 +323,18 @@
     placing = owner[None, :] == slots[:, None]
     source = jnp.sum(jnp.where(placing, positions[None, :], 0), axis=1)
     used = jnp.any(placing, axis=1)
-    flagged = jnp.concatenate([local, jnp.ones((per_dev, 128), jnp.float32)], axis=1)
-    send_rows = jnp.where(used[:, None], jnp.take(flagged, source, axis=0), 0.0)
     split = half_blk + 128
-    send_rows = jnp.concatenate(
-        [send_rows, jnp.broadcast_to(local_max[None, :], (filt_count, half_blk))], axis=1
-    )
+    flagged = jnp.concatenate(
+        [
+            local,
+            jnp.ones((per_dev, 128), jnp.float32),
+            jnp.broadcast_to(local_max[None, :], (per_dev, half_blk)),
+        ],
+        axis=1,
+    )
+    columns = jnp.arange(split + half_blk, dtype=jnp.int32)
+    keep_cols = jnp.logical_or(used[:, None], columns[None, :] >= split)
+    send_rows = jnp.where(keep_cols, jnp.take(flagged, source, axis=0), 0.0)
     recv_rows, loudest = route_and_max(send_rows[:, None, :], split)
     recv_rows = recv_rows.reshape(filt_count, split)
     valid = recv_rows[:, half_blk] > 0.5

time: 57.3 us -> 56.8 us (level)
  local copies, waits for them, and re-layouts: 8.76 us -> 8.03 us
    select_n x2, other arithmetic: 0.08 us -> 0.91 us  [shards(): send_rows = jnp.where(keep_cols, jnp.take(flagged, source, axis=0), 0.0)]
    broadcast_in_dim x1, local copies, waits for them, and re-layouts: 0.75 us -> 0.01 us  [shards(): jnp.ones((per_dev, 128), jnp.float32)]
    reduce_or x1, other arithmetic: 0.74 us -> 0.09 us  [shards(): used = jnp.any(placing, axis=1)]
    unnamed x21 -> x23, local copies, waits for them, and re-layouts: 6.33 us -> 6.31 us
  transfers between devices with their start and end apart: 3 -> 3, of which waited for: 1 -> 1; matrix products, arithmetic and copies ran while one was open for 6% -> 5% of each run, Pallas kernels for 0% -> 0%
where the time goes in v19:
time: 56.8 us; the launch traced here: 55.8 us
  Pallas kernels  39.6 us (70%)
  local copies, waits for them, and re-layouts  8.03 us (14%)
  other arithmetic  4.76 us (8%)
  between operations  1.52 us (3%)
  waiting for transfers between devices  1.06 us (2%)
  starting transfers between devices  0.79 us (1%)
    pallas_call x1, Pallas kernels, route_and_max(): pl.pallas_call(functools.partial(route_kernel, split), out_shape=(jax.Sha...  21.2 us
    pallas_call x1, Pallas kernels, filter_bank(): pl.pallas_call(filter_kernel, out_shape=jax.ShapeDtypeStruct((count, N1,...  18.5 us
    unnamed x23, local copies, waits for them, and re-layouts  6.31 us
  transfers between devices with their start and end apart: 3, of which 1 were waited for; matrix products, arithmetic and copies ran while one was open for 5% of the time, Pallas kernels for 0%

profile of v19, /device:TPU:32, one launch (start us, length us, event | category | flops | bytes accessed | tf_op | source)
XLA Modules:
  0.0 55.8 jit_solution(15726814796799617389)
XLA Ops:
  0.7 0.5 collective-permute-start.1
  1.9 0.7 %select_reduce_fusion.1 = s32[32]{0:T(128)S(1)} fusion(s32[12]{0:T(128)} %param.16), kind=kLoop, calls=%fused_computation.15 | loop fusion | flops 1120 | bytes 176 | tf_op jit(solution)/shard_map/reduce_sum | solution.py:324
  2.7 0.7 %dynamic-slice_multiply_fusion = s32[6]{0:T(128)S(1)} fusion(s32[12]{0:T(128)} %param.15, s32[]{:T(128)S(6)} %select_n.97), kind=kLoop, calls=%fused_computation.33 | loop fusion | flops 6 | bytes 52 | tf_op jit(solution)/shard_map/mul | solution.py:307
  3.4 1.0 %fusion = bf16[6,4096]{1,0:T(8,128)(2,1)S(1)} fusion(bf16[12,4096]{1,0:T(8,128)(2,1)} %param.14, s32[]{:T(128)S(6)} %select_n.97, s32[6]{0:T(128)S(1)} %dynamic-slice_multiply_fusion), kind=kLoop, calls=%fused_computation.5 | loop fusion | flops 49152 | bytes 98332 | tf_op jit(solution)/shard_map/jit(_where)/select_n | solution.py:306
  4.8 0.7 %copy-done = f32[1,131072]{1,0:T(1,128)S(1)} copy-done((f32[1,131072]{1,0:T(1,128)S(1)}, f32[1,131072]{1,0:T(1,128)}, u32[]{:S(2)}) %copy-start) | copy-done | bytes 524312
  5.5 0.2 copy-done.1
  5.7 1.0 %copy-done.2 = f32[256,512]{1,0:T(8,128)S(1)} copy-done((f32[256,512]{1,0:T(8,128)S(1)}, f32[256,512]{1,0:T(8,128)}, u32[]{:S(2)}) %copy-start.2) | copy-done | bytes 524312
  6.7 1.0 %copy-done.3 = f32[256,512]{1,0:T(8,128)S(1)} copy-done((f32[256,512]{1,0:T(8,128)S(1)}, f32[256,512]{1,0:T(8,128)}, u32[]{:S(2)}) %copy-start.3) | copy-done | bytes 524312
  7.8 0.9 %copy-done.5 = bf16[512,256]{1,0:T(8,128)(2,1)S(1)} copy-done((bf16[512,256]{1,0:T(8,128)(2,1)S(1)}, bf16[512,256]{1,0:T(8,128)(2,1)}, u32[]{:S(2)}) %copy-start.5) | copy-done | bytes 262168
  8.7 0.9 %copy-done.7 = bf16[256,256]{1,0:T(8,128)(2,1)S(1)} copy-done((bf16[256,256]{1,0:T(8,128)(2,1)S(1)}, bf16[256,256]{1,0:T(8,128)(2,1)}, u32[]{:S(2)}) %copy-start.7) | copy-done | bytes 131096
  9.6 18.5 %shard_map.131 = f32[6,256,4]{2,1,0:T(8,128)S(1)} custom-call(s32[3]{0:T(128)S(1)} %pad_add_fusion.scalar_ref, bf16[6,128,512]{2,1,0:T(8,128)(2,1)S(1)} %concatenate.12.x_ref, f32[256,512]{1,0:T(8,128)S(1)} %copy-done.2, f32[256,512]{1,0:T(8,128)S(1)} %copy-done.3, bf16[512,256]{1,0:T(8,128)(2,1)S(1)} %copy-done.4, bf16[512,256]{1,0:T(8,128)(2,1)S(1)} %copy-done.5, ...), custom_call_target="tpu_custom_call" | custom-call | flops 8455716864 | bytes 8388608 | tf_op jit(solution)/shard_map/pallas_call | solution.py:278
  28.1 0.4 reshape.164
  28.5 0.2 collective-permute-start.2
  28.7 1.1 %collective-permute-done.2 = f32[6,512]{1,0:T(8,128)S(1)} collective-permute-done((f32[6,512]{1,0:T(8,128)S(1)}, f32[6,512]{1,0:T(8,128)S(1)}, u32[]{:S(2)}, u32[]{:S(2)}) %collective-permute-start.2) | collective-permute-done | bytes 12320 | tf_op jit(solution)/shard_map/ppermute | solution.py:316
  29.9 0.6 %gather_fusion = f32[32,1152]{1,0:T(8,128)S(1)} fusion(f32[12,1152]{1,0:T(8,128)S(1)} %maximum_maximum_fusion, s32[1024]{0:T(1024)S(1)} %pad_clamp_fusion.1), kind=kCustom, calls=%fused_computation | custom fusion | bytes 295040 | tf_op jit(solution)/shard_map/jit(_take)/gather | solution.py:337
  30.5 0.9 %or_select_fusion.send_ref = f32[32,1,1152]{2,1,0:T(1,128)} fusion(pred[1152]{0:T(1024)(128)(4,1)S(1)} %iota_compare_fusion.2, pred[32]{0:T(512)(128)(4,1)S(1)} %fusion.1, f32[32,1152]{1,0:T(8,128)S(1)} %gather_fusion, pred[32]{0:T(512)(128)(4,1)S(1)} %compare_and_fusion.1), kind=kLoop, calls=%fused_computation.2 | loop fusion | flops 110592 | bytes 296128 | tf_op jit(solution)/shard_map/jit(_where)/select_n | solution.py:337
  31.4 21.2 %shard_map.132 = (f32[32,1,640]{2,1,0:T(1,128)}, f32[1,512]{1,0:T(1,128)}) custom-call(f32[32,1,1152]{2,1,0:T(1,128)} %or_select_fusion.send_ref), custom_call_target="tpu_custom_call" | custom-call | tf_op jit(solution)/shard_map/pallas_call | solution.py:122
  52.6 0.9 %copy.18 = f32[32,1,640]{2,0,1:T(8,128)S(1)} copy(f32[32,1,640]{2,1,0:T(1,128)} %get-tuple-element.4) | data formatting | bytes 163840
  53.5 0.1 fusion.5
  53.6 0.1 add_reduce_fusion
  53.8 0.1 select_reduce_fusion
  53.9 0.6 %gather_fusion.1 = f32[12,512]{1,0:T(8,128)S(1)} fusion(f32[32,512]{1,0:T(8,128)S(1)} %slice.13, s32[1024]{0:T(1024)S(1)} %pad_clamp_fusion), kind=kCustom, calls=%fused_computation.1 | custom fusion | bytes 49200 | tf_op jit(solution)/shard_map/jit(_take)/gather | solution.py:344
  54.5 0.7 %broadcast_select_fusion.1 = f32[12,512]{1,0:T(8,128)} fusion(f32[12,512]{1,0:T(8,128)S(1)} %gather_fusion.1, pred[12]{0:T(512)(128)(4,1)S(1)} %compare_and_fusion), kind=kLoop, calls=%fused_computation.11 | loop fusion | flops 6144 | bytes 49164 | tf_op jit(solution)/shard_map/jit(_take)/select_n | solution.py:344
  55.2 0.6 %copy.22 = f32[512]{0:T(512)} copy(f32[512]{0:T(512)S(1)} %bitcast.34) | data formatting | bytes 4096
  (37 shorter events, 0.6 us)
Async XLA Ops:
  0.6 4.2 %copy-start.6 = (bf16[256,256]{1,0:T(8,128)(2,1)S(1)}, bf16[256,256]{1,0:T(8,128)(2,1)}, u32[]{:S(2)}) copy-start(bf16[256,256]{1,0:T(8,128)(2,1)} %constant.94.clone.cf_ref) | copy-start | bytes 393220
  0.6 4.2 %collective-permute-start = (f32[1024,128]{1,0:T(8,128)}, f32[1024,128]{1,0:T(8,128)S(1)}, u32[]{:S(2)}, u32[]{:S(2)}) collective-permute-start(f32[1024,128]{1,0:T(8,128)} %bitcast.26), channel_id=1, source_target_pairs={{0,128},{128,0},{1,129},{129,1},{2,130},{130,2},{3,131},{131,3},{4... | collective-permute-start | bytes 1572872 | tf_op jit(solution)/shard_map/ppermute | solution.py:301
  0.7 4.0 %collective-permute-start.1 = (f32[512,128]{1,0:T(8,128)}, f32[512,128]{1,0:T(8,128)S(1)}, u32[]{:S(2)}, u32[]{:S(2)}) collective-permute-start(f32[512,128]{1,0:T(8,128)} %bitcast.28), channel_id=1, source_target_pairs={{0,128},{128,0},{1,129},{129,1},{2,130},{130,2},{3,131},{131,3},{4... | collective-permute-start | bytes 786440 | tf_op jit(solution)/shard_map/ppermute | solution.py:302
  2.7 1.8 %copy-start.9 = (s32[12]{0:T(128)S(1)}, s32[12]{0:T(128)}, u32[]{:S(2)}) copy-start(s32[12]{0:T(128)} %param.16) | copy-start | bytes 148
  3.4 1.4 %copy-start.4 = (bf16[512,256]{1,0:T(8,128)(2,1)S(1)}, bf16[512,256]{1,0:T(8,128)(2,1)}, u32[]{:S(2)}) copy-start(bf16[512,256]{1,0:T(8,128)(2,1)} %constant.98.clone.cs_ref) | copy-start | bytes 786436
  4.5 1.0 %copy-start = (f32[1,131072]{1,0:T(1,128)S(1)}, f32[1,131072]{1,0:T(1,128)}, u32[]{:S(2)}) copy-start(f32[1,131072]{1,0:T(1,128)} %param.12) | copy-start | bytes 1572868
  4.7 1.0 %copy-start.1 = (f32[1,65536]{1,0:T(1,128)S(1)}, f32[1,65536]{1,0:T(1,128)}, u32[]{:S(2)}) copy-start(f32[1,65536]{1,0:T(1,128)} %param.13) | copy-start | bytes 786436
  5.7 1.0 %copy-start.2 = (f32[256,512]{1,0:T(8,128)S(1)}, f32[256,512]{1,0:T(8,128)}, u32[]{:S(2)}) copy-start(f32[256,512]{1,0:T(8,128)} %constant.96.clone.ct_ref) | copy-start | bytes 1572868
  6.7 1.0 %copy-start.3 = (f32[256,512]{1,0:T(8,128)S(1)}, f32[256,512]{1,0:T(8,128)}, u32[]{:S(2)}) copy-start(f32[256,512]{1,0:T(8,128)} %constant.97.clone.st_ref) | copy-start | bytes 1572868
  7.8 0.9 %copy-start.5 = (bf16[512,256]{1,0:T(8,128)(2,1)S(1)}, bf16[512,256]{1,0:T(8,128)(2,1)}, u32[]{:S(2)}) copy-start(bf16[512,256]{1,0:T(8,128)(2,1)} %constant.99.clone.ss_ref) | copy-start | bytes 786436
  8.7 0.9 %copy-start.7 = (bf16[256,256]{1,0:T(8,128)(2,1)S(1)}, bf16[256,256]{1,0:T(8,128)(2,1)}, u32[]{:S(2)}) copy-start(bf16[256,256]{1,0:T(8,128)(2,1)} %constant.95.clone.sf_ref) | copy-start | bytes 393220
  28.5 1.3 %collective-permute-start.2 = (f32[6,512]{1,0:T(8,128)S(1)}, f32[6,512]{1,0:T(8,128)S(1)}, u32[]{:S(2)}, u32[]{:S(2)}) collective-permute-start(f32[6,512]{1,0:T(8,128)S(1)} %get-tuple-element.10), channel_id=1, source_target_pairs={{0,128},{128,0},{1,129},{129,1},{2,130},{130,2},{3,131},{131,3},{4... | collective-permute-start | bytes 36872 | tf_op jit(solution)/shard_map/ppermute | solution.py:316
  54.5 0.7 %copy-start.8 = (f32[1,512]{1,0:T(1,128)S(1)}, f32[1,512]{1,0:T(1,128)}, u32[]{:S(2)}) copy-start(f32[1,512]{1,0:T(1,128)} %get-tuple-element.5) | copy-start | bytes 6148
